TPU v7x, 32 devices: a whole 2x2x4 slice. The times are simulated.
32 devices in a mesh: dp: 16 (over z, y, core), tensor: 2 (over x).
Axes of the slice: x: 2, y: 2, z: 4, core: 2. Of those that a mesh axis runs over, the one named last changes fastest.
Arguments:
- tokens: bfloat16 [32768, 1024], P(('dp', 'tensor')), may hold values from -40 to 40
- gain_mix: float32 [1024], replicated, may hold values from 0.1 to 1.9
- in_weight: bfloat16 [3, 1024, 1024], P(None, 'dp', 'tensor'), may hold values from -0.1875 to 0.1875
- conv_weight: float32 [3, 1024], replicated, may hold values from -3 to 3
- out_weight: bfloat16 [1024, 1024], P('dp', 'tensor'), may hold values from -0.1875 to 0.1875
- gain_ff: float32 [1024], replicated, may hold values from 0.1 to 1.9
- gate_up_weight: bfloat16 [2, 1024, 4608], P(None, 'dp', 'tensor'), may hold values from -0.1875 to 0.1875
- down_weight: bfloat16 [1024, 4608], P('dp', 'tensor'), may hold values from -0.09375 to 0.09375
- grad_out: bfloat16 [32768, 1024], P(('dp', 'tensor')), may hold values from -9 to 9
Outputs:
- block_out: bfloat16 [32768, 1024], P(('dp', 'tensor'))
- input_grad: float32 [32768, 1024], P(('dp', 'tensor'))
- gain_mix_grad: float32 [1024], replicated
- in_weight_grad: float32 [3, 1024, 1024], P(None, 'dp', 'tensor')
- conv_weight_grad: float32 [3, 1024], replicated
- out_weight_grad: float32 [1024, 1024], P('dp', 'tensor')
- gain_ff_grad: float32 [1024], replicated
- gate_up_weight_grad: float32 [2, 1024, 4608], P(None, 'dp', 'tensor')
- down_weight_grad: float32 [1024, 4608], P('dp', 'tensor')
All inputs are finite; a program needn't handle non-finite values.
Results may differ from a plain program's by a relative error of at most 0.0095.
Values may be sent and summed in bfloat16 or wider, within the bound.
A program may use at most 256 MiB of HBM per device.

v0:
```python
import jax
import jax.numpy as jnp
from jax import lax
from jax.sharding import PartitionSpec as P

KERNEL = 3
LEN = 1024


EPS = 1e-05


def norm_scale(values):
    return lax.rsqrt(jnp.mean(values * values, axis=-1, keepdims=True) + EPS)


def delayed(values, shift_by):
    return jnp.pad(values[:, : values.shape[1] - shift_by], ((0, 0), (shift_by, 0), (0, 0)))


def advanced(values, shift_by):
    return jnp.pad(values[:, shift_by:], ((0, 0), (0, shift_by), (0, 0)))


def norm_back(values, row_scale, gain_vec, grad_normed):
    weighted = grad_normed * gain_vec
    inner_mean = jnp.mean(weighted * values, axis=-1, keepdims=True)
    grad_values = row_scale * weighted - values * row_scale**3 * inner_mean
    gain_grad = jnp.sum(grad_normed * values * row_scale, axis=0)
    return (grad_values, gain_grad)


def per_device(
    tokens,
    gain_mix,
    in_weight,
    conv_weight,
    out_weight,
    gain_ff,
    gate_up_weight,
    down_weight,
    grad_out,
):
    model_width = tokens.shape[1]
    channels = in_weight.shape[2]
    inputs = tokens.astype(jnp.float32)
    scale_mix = norm_scale(inputs)
    normed_mix = (inputs * scale_mix * gain_mix).astype(jnp.bfloat16)
    in_full, out_full, gate_up_full, down_full = (
        lax.all_gather(in_weight, "dp", axis=1, tiled=True),
        lax.all_gather(out_weight, "dp", axis=0, tiled=True),
        lax.all_gather(gate_up_weight, "dp", axis=1, tiled=True),
        lax.all_gather(down_weight, "dp", axis=0, tiled=True),
    )
    mix_rows = lax.all_gather(normed_mix, "tensor", axis=0, tiled=True)
    group_rows = mix_rows.shape[0]
    seq_count = group_rows // LEN
    projected = jnp.einsum("gd,jdc->jgc", mix_rows, in_full, preferred_element_type=jnp.float32)
    input_gate = projected[0].reshape(seq_count, LEN, channels)
    output_gate = projected[1].reshape(seq_count, LEN, channels)
    value_part = projected[2].reshape(seq_count, LEN, channels)
    offset = lax.axis_index("tensor") * channels
    conv_taps = lax.dynamic_slice_in_dim(conv_weight, offset, channels, 1)
    mixed_in = input_gate * value_part
    conv_out = (
        conv_taps[0] * delayed(mixed_in, 2)
        + conv_taps[1] * delayed(mixed_in, 1)
        + conv_taps[2] * mixed_in
    )
    gated_rows = (output_gate * conv_out).astype(jnp.bfloat16).reshape(group_rows, channels)
    rows_part = gated_rows
    mixer_own = lax.psum_scatter(
        lax.dot_general(
            rows_part, out_full, (((1,), (1,)), ((), ())), preferred_element_type=jnp.float32
        ),
        "tensor",
        scatter_dimension=0,
        tiled=True,
    )
    residual = inputs + mixer_own
    scale_ff = norm_scale(residual)
    normed_ff = (residual * scale_ff * gain_ff).astype(jnp.bfloat16)
    ff_rows = lax.all_gather(normed_ff, "tensor", axis=0, tiled=True)
    gate_up = jnp.einsum("gd,jdf->jgf", ff_rows, gate_up_full, preferred_element_type=jnp.float32)
    gate_pre = gate_up[0]
    up_value = gate_up[1]
    sigmoid_gate = jax.nn.sigmoid(gate_pre)
    silu_gate = gate_pre * sigmoid_gate
    hidden = (silu_gate * up_value).astype(jnp.bfloat16)
    rows_part = hidden
    ffn_own = lax.psum_scatter(
        lax.dot_general(
            rows_part, down_full, (((1,), (1,)), ((), ())), preferred_element_type=jnp.float32
        ).astype(jnp.bfloat16),
        "tensor",
        scatter_dimension=0,
        tiled=True,
    ).astype(jnp.float32)
    block_out = (residual + ffn_own).astype(jnp.bfloat16)
    in_back, out_back, gate_up_back, down_back = (
        lax.all_gather(in_weight, "dp", axis=1, tiled=True),
        lax.all_gather(out_weight, "dp", axis=0, tiled=True),
        lax.all_gather(gate_up_weight, "dp", axis=1, tiled=True),
        lax.all_gather(down_weight, "dp", axis=0, tiled=True),
    )
    out_grads = lax.all_gather(grad_out, "tensor", axis=0, tiled=True)
    hidden_grad = jnp.dot(out_grads, down_back, preferred_element_type=jnp.float32)
    down_grad = lax.dot_general(
        out_grads, hidden, (((0,), (0,)), ((), ())), preferred_element_type=jnp.float32
    )
    silu_slope = sigmoid_gate * (1.0 + gate_pre * (1.0 - sigmoid_gate))
    gate_grad = (hidden_grad * up_value * silu_slope).astype(jnp.bfloat16)
    up_grad = (hidden_grad * silu_gate).astype(jnp.bfloat16)
    gate_up_grad = jnp.stack([gate_grad, up_grad])
    grad_part = gate_up_grad
    ffn_in_grad = lax.psum_scatter(
        jnp.einsum("jgf,jdf->gd", grad_part, gate_up_back, preferred_element_type=jnp.float32),
        "tensor",
        scatter_dimension=0,
        tiled=True,
    )
    gate_up_weight_grad = jnp.einsum(
        "gd,jgf->jdf", ff_rows, gate_up_grad, preferred_element_type=jnp.float32
    )
    ffn_weight_parts = (
        lax.psum_scatter(gate_up_weight_grad, "dp", scatter_dimension=1, tiled=True),
        lax.psum_scatter(down_grad, "dp", scatter_dimension=0, tiled=True),
    )
    residual_back, gain_ff_grad = norm_back(residual, scale_ff, gain_ff, ffn_in_grad)
    residual_grad = grad_out.astype(jnp.float32) + residual_back
    mixer_grads = lax.all_gather(residual_grad.astype(jnp.bfloat16), "tensor", axis=0, tiled=True)
    gated_grad = jnp.dot(mixer_grads, out_back, preferred_element_type=jnp.float32).reshape(
        seq_count, LEN, channels
    )
    out_weight_grad = lax.dot_general(
        mixer_grads, gated_rows, (((0,), (0,)), ((), ())), preferred_element_type=jnp.float32
    )
    output_gate_grad = gated_grad * conv_out
    conv_grad_in = gated_grad * output_gate
    mixed_grad = (
        conv_taps[2] * conv_grad_in
        + conv_taps[1] * advanced(conv_grad_in, 1)
        + conv_taps[0] * advanced(conv_grad_in, 2)
    )
    tap_grads = jnp.stack(
        [
            jnp.sum(conv_grad_in * delayed(mixed_in, 2), axis=(0, 1)),
            jnp.sum(conv_grad_in * delayed(mixed_in, 1), axis=(0, 1)),
            jnp.sum(conv_grad_in * mixed_in, axis=(0, 1)),
        ]
    )
    proj_grad = (
        jnp.stack([mixed_grad * value_part, output_gate_grad, mixed_grad * input_gate])
        .astype(jnp.bfloat16)
        .reshape(3, group_rows, channels)
    )
    grad_part = proj_grad
    mixer_in_grad = lax.psum_scatter(
        jnp.einsum("jgc,jdc->gd", grad_part, in_back, preferred_element_type=jnp.float32).astype(
            jnp.bfloat16
        ),
        "tensor",
        scatter_dimension=0,
        tiled=True,
    ).astype(jnp.float32)
    in_weight_grad = jnp.einsum(
        "gd,jgc->jdc", mix_rows, proj_grad, preferred_element_type=jnp.float32
    )
    mixer_weight_parts = (
        lax.psum_scatter(in_weight_grad, "dp", scatter_dimension=1, tiled=True),
        lax.psum_scatter(out_weight_grad, "dp", scatter_dimension=0, tiled=True),
    )
    input_back, gain_mix_grad = norm_back(inputs, scale_mix, gain_mix, mixer_in_grad)
    input_grad = residual_grad + input_back
    conv_full = lax.dynamic_update_slice_in_dim(
        jnp.zeros((KERNEL, model_width), jnp.float32), tap_grads, offset, 1
    )
    gain_mix_sum, gain_ff_sum, conv_sum = lax.psum(
        (gain_mix_grad, gain_ff_grad, conv_full), ("dp", "tensor")
    )
    return (
        block_out,
        input_grad,
        gain_mix_sum,
        mixer_weight_parts[0],
        conv_sum,
        mixer_weight_parts[1],
        gain_ff_sum,
        ffn_weight_parts[0],
        ffn_weight_parts[1],
    )


def solution(mesh):
    in_specs = (
        P(("dp", "tensor"), None),
        P(),
        P(None, "dp", "tensor"),
        P(),
        P("dp", "tensor"),
        P(),
        P(None, "dp", "tensor"),
        P("dp", "tensor"),
        P(("dp", "tensor"), None),
    )
    out_specs = (
        P(("dp", "tensor"), None),
        P(("dp", "tensor"), None),
        P(),
        P(None, "dp", "tensor"),
        P(),
        P("dp", "tensor"),
        P(),
        P(None, "dp", "tensor"),
        P("dp", "tensor"),
    )
    return jax.shard_map(
        per_device, mesh=mesh, in_specs=in_specs, out_specs=out_specs, check_vma=False
    )
```

profile of v0, /device:TPU:0, one launch (start us, length us, event | category | flops | bytes accessed | tf_op | source)
XLA Modules:
  0.0 1576.7 jit_solution(4600095062100172093)
XLA Ops:
  7.2 2.1 fusion.10
  9.3 0.6 multiply_multiply_fusion
  9.9 0.6 copy-done.14
  10.5 3.5 fusion.12
  14.0 0.7 all-gather.11.cloned.1.call-update
  14.8 0.7 all-gather.13.cloned.1.call-update
  15.5 0.9 constant_dynamic-slice_fusion.2
  16.4 57.2 %all-gather.9.cloned.1.call-done = bf16[2048,1024]{1,0:T(8,128)(2,1)} async-done(((bf16[1024,1024]{1,0:T(8,128)(2,1)}), bf16[2048,1024]{1,0:T(8,128)(2,1)}) %all-gather.9.cloned.1.call-update) | async-done | bytes 4194320 | tf_op jit(solution)/shard_map/all_gather | solution.py:55
  73.6 47.7 %all-gather.11.cloned.1.call-done = bf16[3,1024,512]{2,1,0:T(8,128)(2,1)} async-done(((bf16[3,64,512]{2,1,0:T(8,128)(2,1)}), bf16[3,1024,512]{2,1,0:T(8,128)(2,1)}) %all-gather.11.cloned.1.call-update) | async-done | bytes 3145744 | tf_op jit(solution)/shard_map/all_gather | solution.py:50
  121.3 12.2 convolution_bitcast_fusion.2
  133.5 9.5 fusion.31
  143.1 4.7 mul.235
  147.8 2.0 copy-done
  149.8 6.4 multiply_convert_fusion.7
  156.2 3.5 all-gather.13.cloned.1.call-done
  159.7 6.9 fusion.32
  167.2 97.8 %reduce-scatter.9.cloned.1.call-done = f32[1024,1024]{1,0:T(8,128)} async-done(((f32[2048,1024]{1,0:T(8,128)}), f32[1024,1024]{1,0:T(8,128)}) %reduce-scatter.9.cloned.1.call-update) | async-done | bytes 4194320 | tf_op jit(solution)/shard_map/reduce_scatter | solution.py:72
  265.1 2.8 multiply_reduce_fusion.4
  267.9 0.7 multiply_multiply_fusion.1
  268.5 1.4 copy-done.2
  269.9 1.7 multiply_convert_fusion.6
  271.7 0.7 all-gather.21.cloned.1.call-update
  272.4 0.7 all-gather.19.cloned.1.call-update
  273.2 74.9 %all-gather.17.cloned.1.call-done = bf16[2,1024,2304]{2,1,0:T(8,128)(2,1)} async-done(((bf16[2,64,2304]{2,1,0:T(8,128)(2,1)}), bf16[2,1024,2304]{2,1,0:T(8,128)(2,1)}) %all-gather.17.cloned.1.call-update) | async-done | bytes 9437200 | tf_op jit(solution)/shard_map/all_gather | solution.py:52
  348.1 57.1 %all-gather.15.cloned.1.call-done = bf16[2048,1024]{1,0:T(8,128)(2,1)} async-done(((bf16[1024,1024]{1,0:T(8,128)(2,1)}), bf16[2048,1024]{1,0:T(8,128)(2,1)}) %all-gather.15.cloned.1.call-update) | async-done | bytes 4194320 | tf_op jit(solution)/shard_map/all_gather | solution.py:83
  405.3 28.0 %convolution_bitcast_fusion = f32[2,2048,2304]{2,1,0:T(8,128)} fusion(bf16[2,1024,2304]{2,1,0:T(8,128)(2,1)} %all-gather.17.cloned.1.call-done, bf16[2048,1024]{1,0:T(8,128)(2,1)} %all-gather.15.cloned.1.call-done), kind=kOutput, calls=%fused_computation | convolution fusion | flops 19327352832 | bytes 51380224 | tf_op jit(solution)/shard_map/gd,jdf->jgf/dot_general | solution.py:84
  433.2 30.3 %all-gather.21.cloned.1.call-done = bf16[2048,1024]{1,0:T(8,128)(2,1)} async-done(((bf16[1024,1024]{1,0:T(8,128)(2,1)}), bf16[2048,1024]{1,0:T(8,128)(2,1)}) %all-gather.21.cloned.1.call-update) | async-done | bytes 4194320 | tf_op jit(solution)/shard_map/all_gather | solution.py:106
  463.6 55.4 %all-gather.19.cloned.1.call-done = bf16[1024,2304]{1,0:T(8,128)(2,1)} async-done(((bf16[64,2304]{1,0:T(8,128)(2,1)}), bf16[1024,2304]{1,0:T(8,128)(2,1)}) %all-gather.19.cloned.1.call-update) | async-done | bytes 4718608 | tf_op jit(solution)/shard_map/all_gather | solution.py:53
  519.0 34.8 %fusion.5 = (bf16[1,2048,2304]{2,1,0:T(8,128)(2,1)}, bf16[1,2048,2304]{2,1,0:T(8,128)(2,1)}, bf16[2048,2304]{1,0:T(8,128)(2,1)}) fusion(f32[2,2048,2304]{2,1,0:T(8,128)} %convolution_bitcast_fusion, bf16[2048,1024]{1,0:T(8,128)(2,1)} %all-gather.21.cloned.1.call-done, bf16[1024,2304]{1,0:T(8,128)(2,1)} %all-gather.19.cloned.1.call-done), kind=kOutput, calls=%fused_computation.19 | convolution fusion | flops 9734455296 | bytes 74973184 | tf_op jit(solution)/shard_map/dot_general | solution.py:107
  553.8 27.2 %fusion.7 = f32[2048,1024]{1,0:T(8,128)} fusion(bf16[2,1024,2304]{2,1,0:T(8,128)(2,1)} %all-gather.17.cloned.1.call-done, bf16[1,2048,2304]{2,1,0:T(8,128)(2,1)} %get-tuple-element.48, bf16[1,2048,2304]{2,1,0:T(8,128)(2,1)} %get-tuple-element.47), kind=kOutput, calls=%fused_computation.26 | convolution fusion | flops 19336790016 | bytes 36700160 | tf_op jit(solution)/shard_map/jgf,jdf->gd/dot_general | solution.py:117
  581.0 15.2 convolution_convert_fusion
  596.4 82.7 %reduce-scatter.13.cloned.1.call-done = f32[1024,1024]{1,0:T(8,128)} async-done(((f32[2048,1024]{1,0:T(8,128)}), f32[1024,1024]{1,0:T(8,128)}) %reduce-scatter.13.cloned.1.call-update) | async-done | bytes 4194320 | tf_op jit(solution)/shard_map/reduce_scatter | solution.py:116
  679.0 5.1 multiply_reduce_fusion
  684.1 51.5 %reduce-scatter.11.cloned.1.call-done = bf16[1024,1024]{1,0:T(8,128)(2,1)} async-done(((bf16[2048,1024]{1,0:T(8,128)(2,1)}), bf16[1024,1024]{1,0:T(8,128)(2,1)}) %reduce-scatter.11.cloned.1.call-update) | async-done | bytes 2097168 | tf_op jit(solution)/shard_map/reduce_scatter | solution.py:91
  735.6 6.8 fusion.30
  742.5 56.8 %all-gather.23.cloned.1.call-done = bf16[2048,1024]{1,0:T(8,128)(2,1)} async-done(((bf16[1024,1024]{1,0:T(8,128)(2,1)}), bf16[2048,1024]{1,0:T(8,128)(2,1)}) %all-gather.23.cloned.1.call-update) | async-done | bytes 4194320 | tf_op jit(solution)/shard_map/all_gather | solution.py:131
  799.3 9.0 fusion.17
  808.4 0.4 copy-done.8
  808.8 4.0 multiply_reduce_fusion.2
  812.8 2.5 slice.60
  815.3 2.7 slice.61
  818.0 1.0 copy-done.6
  819.0 8.4 multiply_convert_fusion.5
  827.5 4.4 multiply_convert_fusion.3
  831.9 1.4 copy-done.13
  833.6 8.2 bitcast_convert_fusion
  841.9 27.3 %fusion.3 = f32[2,1024,2304]{1,2,0:T(8,128)} fusion(bf16[1,2048,2304]{2,1,0:T(8,128)(2,1)} %get-tuple-element.48, bf16[1,2048,2304]{2,1,0:T(8,128)(2,1)} %get-tuple-element.47, bf16[2048,1024]{1,0:T(8,128)(2,1)} %all-gather.15.cloned.1.call-done), kind=kOutput, calls=%fused_computation.11 | convolution fusion | flops 19336790016 | bytes 41943040 | tf_op jit(solution)/shard_map/gd,jgf->jdf/dot_general | solution.py:122
  869.2 28.4 %copy.26 = f32[2,1024,2304]{2,0,1:T(2,128)} copy(f32[2,1024,2304]{1,2,0:T(8,128)} %fusion.3) | data formatting | bytes 37748736 | tf_op jit(solution)/shard_map/gd,jgf->jdf/transpose | solution.py:122
  897.6 11.5 fusion.23
  909.1 9.4 copy.24
  918.6 16.3 %convolution_bitcast_fusion.1 = f32[1024,2304]{0,1:T(8,128)} fusion(bf16[2048,2304]{1,0:T(8,128)(2,1)} %get-tuple-element.49, bf16[2048,1024]{1,0:T(8,128)(2,1)} %all-gather.21.cloned.1.call-done), kind=kOutput, calls=%fused_computation.21 | convolution fusion | flops 9663676416 | bytes 23068672 | tf_op jit(solution)/shard_map/dot_general | solution.py:108
  934.8 9.6 copy.32
  944.6 6.8 fusion.33
  951.4 0.6 dynamic-slice
  952.8 3.2 fusion.16
  956.0 41.3 %all-reduce.6 = (f32[1024]{0:T(1024)}, f32[3,1024]{1,0:T(4,128)}, f32[1024]{0:T(1024)}) all-reduce(f32[1024]{0:T(1024)S(1)} %get-tuple-element.31, f32[3,1024]{1,0:T(4,128)S(1)} %maximum_dynamic-update-slice_fusion, f32[1024]{0:T(1024)S(1)} %copy-done.26), channel_id=1, replica_groups=mesh['dp'=16,'tensor'=2] {'dp','tensor'}, use_global_device_ids=true, to_apply=%region_9.10 | all-reduce | flops 5120 | bytes 40960 | tf_op jit(solution)/shard_map/psum | solution.py:178
  997.4 4.8 fusion.9
  1002.2 386.5 %all-reduce.10.cloned.1.call-done = (f32[3,1024,512]{2,0,1:T(4,128)}, f32[2,1024,2304]{2,0,1:T(2,128)}) async-done(((f32[3,1024,512]{2,0,1:T(4,128)}, f32[2,1024,2304]{2,0,1:T(2,128)}), (f32[3,1024,512]{2,0,1:T(4,128)}, f32[2,1024,2304]{2,0,1:T(2,128)})) %all-reduce.10.cloned.1.call-update) | async-done | bytes 25165840
  1388.7 1.4 constant_dynamic-slice_fusion
  1390.1 1.1 copy.28
  1391.1 1.1 constant_dynamic-slice_fusion.1
  1392.3 0.9 copy.27
  1393.2 110.9 %reduce-scatter.19.cloned.1.call-done = f32[64,2304]{1,0:T(8,128)} async-done(((f32[1024,2304]{1,0:T(8,128)}), f32[64,2304]{1,0:T(8,128)}) %reduce-scatter.19.cloned.1.call-update) | async-done | bytes 589840
  1504.1 65.6 %reduce-scatter.17.cloned.1.call-done = f32[64,512]{1,0:T(8,128)} async-done(((f32[1024,512]{1,0:T(8,128)}), f32[64,512]{1,0:T(8,128)}) %reduce-scatter.17.cloned.1.call-update) | async-done | bytes 131088 | tf_op jit(solution)/shard_map/reduce_scatter | solution.py:171
  (85 shorter events, 1.8 us)
Async XLA Ops:
  7.2 66.4 %all-gather.9.cloned.1.call-start = ((), (), s32[]{:S(2)}) async-start(), calls=%async_computation.6 | async-start | bytes 6291456 | tf_op jit(solution)/shard_map/all_gather | solution.py:55
  9.9 0.6 copy-start.14
  14.0 107.3 %all-gather.11.cloned.1.call-start = ((), (), s32[]{:S(2)}) async-start(), calls=%async_computation.7 | async-start | bytes 3342336 | tf_op jit(solution)/shard_map/all_gather | solution.py:50
  14.7 145.0 %all-gather.13.cloned.1.call-start = ((), (), s32[]{:S(2)}) async-start(), calls=%async_computation.8 | async-start | bytes 1114112 | tf_op jit(solution)/shard_map/all_gather | solution.py:51
  15.5 249.6 %reduce-scatter.9.cloned.1.call-start = ((), (), s32[]{:S(2)}) async-start(), calls=%async_computation.9 | async-start | bytes 12582912 | tf_op jit(solution)/shard_map/reduce_scatter | solution.py:72
  16.4 131.4 %copy-start.18 = (f32[1,512]{1,0:T(1,128)}, f32[1,512]{1,0:T(1,128)S(1)}, u32[]{:S(2)}) copy-start(f32[1,512]{1,0:T(1,128)S(1)} %get-tuple-element.55) | copy-start | bytes 6148
  16.4 131.4 %copy-start.20 = (f32[1,512]{1,0:T(1,128)}, f32[1,512]{1,0:T(1,128)S(1)}, u32[]{:S(2)}) copy-start(f32[1,512]{1,0:T(1,128)S(1)} %get-tuple-element.56) | copy-start | bytes 6148
  16.4 131.4 %copy-start.22 = (f32[1,512]{1,0:T(1,128)}, f32[1,512]{1,0:T(1,128)S(1)}, u32[]{:S(2)}) copy-start(f32[1,512]{1,0:T(1,128)S(1)} %get-tuple-element.57) | copy-start | bytes 6148
  143.0 4.7 copy-start.5
  147.8 2.0 copy-start
  156.2 10.3 copy-start.10
  166.6 98.5 %copy-start.3 = (bf16[1024,1024]{1,0:T(8,128)(2,1)S(1)}, bf16[1024,1024]{1,0:T(8,128)(2,1)}, u32[]{:S(2)}) copy-start(bf16[1024,1024]{1,0:T(8,128)(2,1)} %param.9) | copy-start | bytes 6291460
  166.6 181.5 %all-gather.17.cloned.1.call-start = ((), (), s32[]{:S(2)}) async-start(), calls=%async_computation.11 | async-start | bytes 10027008 | tf_op jit(solution)/shard_map/all_gather | solution.py:52
  167.2 102.7 %copy-start.16 = (f32[1024]{0:T(1024)S(1)}, f32[1024]{0:T(1024)}, u32[]{:S(2)}) copy-start(f32[1024]{0:T(1024)} %param.14) | copy-start | bytes 12292
  167.2 238.1 %all-gather.15.cloned.1.call-start = ((), (), s32[]{:S(2)}) async-start(), calls=%async_computation.10 | async-start | bytes 6291456 | tf_op jit(solution)/shard_map/all_gather | solution.py:83
  267.9 2.0 copy-start.2
  271.6 191.9 %all-gather.21.cloned.1.call-start = ((), (), s32[]{:S(2)}) async-start(), calls=%async_computation.14 | async-start | bytes 6291456 | tf_op jit(solution)/shard_map/all_gather | solution.py:106
  272.4 246.6 %all-gather.19.cloned.1.call-start = ((), (), s32[]{:S(2)}) async-start(), calls=%async_computation.12 | async-start | bytes 5013504 | tf_op jit(solution)/shard_map/all_gather | solution.py:53
  273.1 405.9 %reduce-scatter.13.cloned.1.call-start = ((), (), s32[]{:S(2)}) async-start(), calls=%async_computation.15 | async-start | bytes 12582912 | tf_op jit(solution)/shard_map/reduce_scatter | solution.py:116
  581.0 154.6 %reduce-scatter.11.cloned.1.call-start = ((), (), s32[]{:S(2)}) async-start(), calls=%async_computation.13 | async-start | bytes 6291456 | tf_op jit(solution)/shard_map/reduce_scatter | solution.py:91
  596.3 139.3 %copy-start.9 = (bf16[1024,1024]{1,0:T(8,128)(2,1)S(1)}, bf16[1024,1024]{1,0:T(8,128)(2,1)}, u32[]{:S(2)}) copy-start(bf16[1024,1024]{1,0:T(8,128)(2,1)} %param.17) | copy-start | bytes 6291460
  596.3 139.3 %copy-start.25 = (f32[1024]{0:T(1024)S(1)}, f32[1024]{0:T(1024)}, u32[]{:S(2)}) copy-start(f32[1024]{0:T(1024)} %get-tuple-element.60) | copy-start | bytes 12292
  596.3 203.0 %all-gather.23.cloned.1.call-start = ((), (), s32[]{:S(2)}) async-start(), calls=%async_computation.16 | async-start | bytes 6291456 | tf_op jit(solution)/shard_map/all_gather | solution.py:131
  735.6 63.7 %copy-start.28 = (bf16[1024,512]{1,0:T(8,128)(2,1)S(1)}, bf16[1024,512]{1,0:T(8,128)(2,1)}, u32[]{:S(2)}) copy-start(bf16[1024,512]{1,0:T(8,128)(2,1)} %all-gather.13.cloned.1.call-done) | copy-start | bytes 3145732
  742.4 210.3 %reduce-scatter.15.cloned.1.call-start = ((), (), s32[]{:S(2)}) async-start(), calls=%async_computation.17 | async-start | bytes 6291456 | tf_op jit(solution)/shard_map/reduce_scatter | solution.py:158
  799.3 9.1 copy-start.1
  799.3 9.1 copy-start.7
  799.3 9.5 copy-start.8
  815.3 3.7 copy-start.6
  815.3 3.7 copy-start.19
  815.3 3.7 copy-start.21
  815.3 3.7 copy-start.23
  827.5 5.8 copy-start.11
  827.5 5.8 copy-start.12
  827.5 6.2 copy-start.27
  831.8 1.4 copy-start.13
  841.9 546.8 %all-reduce.10.cloned.1.call-start = ((), (), s32[]{:S(2)}) async-start(), calls=%async_computation.20 | async-start | bytes 54525952
  918.5 585.6 %reduce-scatter.19.cloned.1.call-start = ((), (), s32[]{:S(2)}) async-start(), calls=%async_computation.19 | async-start | bytes 10027008
  944.5 6.9 copy-start.29
  944.5 8.2 copy-start.4
  944.5 8.2 copy-start.15
  944.5 8.2 copy-start.17
  944.5 625.1 %reduce-scatter.17.cloned.1.call-start = ((), (), s32[]{:S(2)}) async-start(), calls=%async_computation.18 | async-start | bytes 2228224 | tf_op jit(solution)/shard_map/reduce_scatter | solution.py:171
  951.4 4.6 copy-start.26
  951.4 46.0 %copy-start.24 = (f32[1024]{0:T(1024)S(1)}, f32[1024]{0:T(1024)}, u32[]{:S(2)}) copy-start(f32[1024]{0:T(1024)} %get-tuple-element.58) | copy-start | bytes 12292
Sparse Core Ops, SparseCore 0:
  14.1 59.4 all-gather.8
  75.8 45.4 all-gather.10
  123.5 36.2 all-gather.12
  166.7 98.2 reduce-scatter.8
  267.2 80.9 all-gather.16
  350.1 55.1 all-gather.14
  406.8 56.7 all-gather.20
  465.8 53.1 all-gather.18
  581.1 97.8 reduce-scatter.12
  681.2 54.3 reduce-scatter.10
  742.5 56.7 all-gather.22
  842.0 54.3 reduce-scatter.14
  918.6 470.0 all-reduce.9
  1393.2 110.8 reduce-scatter.18
  1508.2 61.4 reduce-scatter.16
where the time goes:
time: 1590 us; the launch traced here: 1580 us
  waiting for transfers between devices  1180 us (74%)
  matrix products  203 us (13%)
  local copies, waits for them, and re-layouts  75.3 us (5%)
  other arithmetic  59.3 us (4%)
  blocking collectives  41.3 us (3%)
    unnamed x17, waiting for transfers between devices  501 us
    reduce_scatter x1, waiting for transfers between devices, per_device(): lax.psum_scatter(lax.dot_general(rows_part, out_full, (((1,), (1,)), ((),...  97.8 us
    reduce_scatter x1, waiting for transfers between devices, per_device(): lax.psum_scatter(jnp.einsum('jgf,jdf->gd', grad_part, gate_up_back, prefe...  82.7 us
    all_gather x1, waiting for transfers between devices, per_device(): lax.all_gather(gate_up_weight, 'dp', axis=1, tiled=True)  74.9 us
    reduce_scatter x1, waiting for transfers between devices, per_device(): lax.psum_scatter(out_weight_grad, 'dp', scatter_dimension=0, tiled=True)  65.6 us
    all_gather x1, waiting for transfers between devices, per_device(): mix_rows = lax.all_gather(normed_mix, 'tensor', axis=0, tiled=True)  57.2 us
    all_gather x1, waiting for transfers between devices, per_device(): ff_rows = lax.all_gather(normed_ff, 'tensor', axis=0, tiled=True)  57.1 us
    all_gather x1, waiting for transfers between devices, per_device(): lax.all_gather(residual_grad.astype(jnp.bfloat16), 'tensor', axis=0, tile...  56.8 us
  transfers between devices with their start and end apart: 15, of which 14 were waited for; matrix products, arithmetic and copies ran while one was open for 13% of the time, Pallas kernels for 0%

commit v1 on v0

v1 whole, which is shorter than its diff:
```python
import jax
import jax.numpy as jnp
from jax import lax
from jax.sharding import PartitionSpec as P

LEN = 1024


EPS = 1e-05


def norm_scale(values):
    return lax.rsqrt(jnp.mean(values * values, axis=-1, keepdims=True) + EPS)


def delayed(values, shift_by):
    return jnp.pad(values[:, : values.shape[1] - shift_by], ((0, 0), (shift_by, 0), (0, 0)))


def advanced(values, shift_by):
    return jnp.pad(values[:, shift_by:], ((0, 0), (0, shift_by), (0, 0)))


def norm_back(values, row_scale, gain_vec, grad_normed):
    weighted = grad_normed * gain_vec
    inner_mean = jnp.mean(weighted * values, axis=-1, keepdims=True)
    grad_values = row_scale * weighted - values * row_scale**3 * inner_mean
    gain_grad = jnp.sum(grad_normed * values * row_scale, axis=0)
    return (grad_values, gain_grad)


def gather_cols(shard, col_axis):
    part = lax.all_gather(shard, "tensor", axis=col_axis, tiled=True)
    return lax.all_gather(part, "dp", axis=col_axis - 1, tiled=True)


def scatter_sum(partial, col_axis):
    if col_axis == 2:
        return jnp.stack([scatter_sum(one, 1) for one in partial])
    part = lax.psum_scatter(
        partial.astype(jnp.bfloat16), "dp", scatter_dimension=col_axis - 1, tiled=True
    )
    return lax.psum_scatter(part, "tensor", scatter_dimension=col_axis, tiled=True).astype(
        jnp.float32
    )


def per_device(
    tokens,
    gain_mix,
    in_weight,
    conv_weight,
    out_weight,
    gain_ff,
    gate_up_weight,
    down_weight,
    grad_out,
):
    inputs = tokens.astype(jnp.float32)
    in_full = gather_cols(in_weight, 2)
    out_full = gather_cols(out_weight, 1)
    gate_up_full = gather_cols(gate_up_weight, 2)
    down_full = gather_cols(down_weight, 1)
    rows, width = tokens.shape
    seq_count = rows // LEN
    scale_mix = norm_scale(inputs)
    normed_mix = (inputs * scale_mix * gain_mix).astype(jnp.bfloat16)
    projected = jnp.einsum("gd,jdc->jgc", normed_mix, in_full, preferred_element_type=jnp.float32)
    shaped = (seq_count, LEN, width)
    input_gate = projected[0].reshape(shaped)
    output_gate = projected[1].reshape(shaped)
    value_part = projected[2].reshape(shaped)
    mixed_in = input_gate * value_part
    conv_out = (
        conv_weight[0] * delayed(mixed_in, 2)
        + conv_weight[1] * delayed(mixed_in, 1)
        + conv_weight[2] * mixed_in
    )
    gated_rows = (output_gate * conv_out).astype(jnp.bfloat16).reshape(rows, width)
    residual = inputs + lax.dot_general(
        gated_rows, out_full, (((1,), (1,)), ((), ())), preferred_element_type=jnp.float32
    )
    scale_ff = norm_scale(residual)
    normed_ff = (residual * scale_ff * gain_ff).astype(jnp.bfloat16)
    gate_up = jnp.einsum(
        "gd,jdf->jgf", normed_ff, gate_up_full, preferred_element_type=jnp.float32
    )
    gate_pre = gate_up[0]
    up_value = gate_up[1]
    sigmoid_gate = jax.nn.sigmoid(gate_pre)
    silu_gate = gate_pre * sigmoid_gate
    hidden = (silu_gate * up_value).astype(jnp.bfloat16)
    block_out = (
        residual
        + lax.dot_general(
            hidden, down_full, (((1,), (1,)), ((), ())), preferred_element_type=jnp.float32
        )
    ).astype(jnp.bfloat16)
    hidden_grad = jnp.dot(grad_out, down_full, preferred_element_type=jnp.float32)
    down_grad = lax.dot_general(
        grad_out, hidden, (((0,), (0,)), ((), ())), preferred_element_type=jnp.float32
    )
    down_sum = scatter_sum(down_grad, 1)
    silu_slope = sigmoid_gate * (1.0 + gate_pre * (1.0 - sigmoid_gate))
    gate_grad = (hidden_grad * up_value * silu_slope).astype(jnp.bfloat16)
    up_grad = (hidden_grad * silu_gate).astype(jnp.bfloat16)
    gate_up_grad = jnp.stack([gate_grad, up_grad])
    gate_up_weight_grad = jnp.einsum(
        "gd,jgf->jdf", normed_ff, gate_up_grad, preferred_element_type=jnp.float32
    )
    gate_up_sum = scatter_sum(gate_up_weight_grad, 2)
    ffn_in_grad = jnp.einsum(
        "jgf,jdf->gd", gate_up_grad, gate_up_full, preferred_element_type=jnp.float32
    )
    residual_back, gain_ff_grad = norm_back(residual, scale_ff, gain_ff, ffn_in_grad)
    residual_grad = grad_out.astype(jnp.float32) + residual_back
    mixer_grads = residual_grad.astype(jnp.bfloat16)
    gated_grad = jnp.dot(mixer_grads, out_full, preferred_element_type=jnp.float32).reshape(shaped)
    out_weight_grad = lax.dot_general(
        mixer_grads, gated_rows, (((0,), (0,)), ((), ())), preferred_element_type=jnp.float32
    )
    out_sum = scatter_sum(out_weight_grad, 1)
    output_gate_grad = gated_grad * conv_out
    conv_grad_in = gated_grad * output_gate
    mixed_grad = (
        conv_weight[2] * conv_grad_in
        + conv_weight[1] * advanced(conv_grad_in, 1)
        + conv_weight[0] * advanced(conv_grad_in, 2)
    )
    tap_grads = jnp.stack(
        [
            jnp.sum(conv_grad_in * delayed(mixed_in, 2), axis=(0, 1)),
            jnp.sum(conv_grad_in * delayed(mixed_in, 1), axis=(0, 1)),
            jnp.sum(conv_grad_in * mixed_in, axis=(0, 1)),
        ]
    )
    proj_grad = (
        jnp.stack([mixed_grad * value_part, output_gate_grad, mixed_grad * input_gate])
        .astype(jnp.bfloat16)
        .reshape(3, rows, width)
    )
    in_weight_grad = jnp.einsum(
        "gd,jgc->jdc", normed_mix, proj_grad, preferred_element_type=jnp.float32
    )
    in_sum = scatter_sum(in_weight_grad, 2)
    mixer_in_grad = jnp.einsum(
        "jgc,jdc->gd", proj_grad, in_full, preferred_element_type=jnp.float32
    )
    input_back, gain_mix_grad = norm_back(inputs, scale_mix, gain_mix, mixer_in_grad)
    input_grad = residual_grad + input_back
    gain_mix_sum, gain_ff_sum, conv_sum = lax.psum(
        (gain_mix_grad, gain_ff_grad, tap_grads), ("dp", "tensor")
    )
    return (
        block_out,
        input_grad,
        gain_mix_sum,
        in_sum,
        conv_sum,
        out_sum,
        gain_ff_sum,
        gate_up_sum,
        down_sum,
    )


def solution(mesh):
    in_specs = (
        P(("dp", "tensor"), None),
        P(),
        P(None, "dp", "tensor"),
        P(),
        P("dp", "tensor"),
        P(),
        P(None, "dp", "tensor"),
        P("dp", "tensor"),
        P(("dp", "tensor"), None),
    )
    out_specs = (
        P(("dp", "tensor"), None),
        P(("dp", "tensor"), None),
        P(),
        P(None, "dp", "tensor"),
        P(),
        P("dp", "tensor"),
        P(),
        P(None, "dp", "tensor"),
        P("dp", "tensor"),
    )
    return jax.shard_map(
        per_device, mesh=mesh, in_specs=in_specs, out_specs=out_specs, check_vma=False
    )
```

time: 1590 us -> 1170 us (0.74)
  waiting for transfers between devices: 1180 us -> 729 us
  local copies, waits for them, and re-layouts: 75.3 us -> 110 us
  other arithmetic: 59.3 us -> 30.2 us
  blocking collectives: 41.3 us -> 68.4 us
    reduce_scatter x5 -> x8, waiting for transfers between devices: 298 us -> 129 us  [the longest x7 66 us: scatter_sum(): lax.psum_scatter(part, 'tensor', scatter_dimension=col_axis, tiled=True)]
    all_gather x8 -> x5, waiting for transfers between devices: 383 us -> 222 us  [the longest x4 211 us: gather_cols(): return lax.all_gather(part, 'dp', axis=col_axis - 1, tiled=True)]
    unnamed x17 -> x25, waiting for transfers between devices: 501 us -> 378 us
    unnamed x66 -> x59, local copies, waits for them, and re-layouts: 21.9 us -> 90.1 us
    transpose x2 -> x0, local copies, waits for them, and re-layouts: 37.7 us -> none  [the longest x1 28.4 us: per_device(): jnp.einsum('gd,jgf->jdf', ff_rows, gate_up_grad, preferred_element_type=j...]
    all_gather x0 -> x3, blocking collectives: none -> 27.7 us  [gather_cols(): part = lax.all_gather(shard, 'tensor', axis=col_axis, tiled=True)]
    convert_element_type x0 -> x2, local copies, waits for them, and re-layouts: none -> 17.9 us  [scatter_sum(): partial.astype(jnp.bfloat16)]
    convert_element_type x4 -> x1, other arithmetic: 18.4 us -> 1.5 us  [scatter_sum(): lax.psum_scatter(part, 'tensor', scatter_dimension=col_axis, tiled=True)]
  transfers between devices with their start and end apart: 15 -> 19, of which waited for: 14 -> 14; matrix products, arithmetic and copies ran while one was open for 13% -> 21% of each run, Pallas kernels for 0% -> 0%
where the time goes in v1:
time: 1170 us; the launch traced here: 1160 us
  waiting for transfers between devices  729 us (62%)
  matrix products  211 us (18%)
  local copies, waits for them, and re-layouts  110 us (9%)
  blocking collectives  68.4 us (6%)
  other arithmetic  30.2 us (3%)
  between operations  14.7 us (1%)
    unnamed x25, waiting for transfers between devices  378 us
    all_gather x4, waiting for transfers between devices, gather_cols(): return lax.all_gather(part, 'dp', axis=col_axis - 1, tiled=True)  211 us
    unnamed x59, local copies, waits for them, and re-layouts  90.1 us
    reduce_scatter x7, waiting for transfers between devices, scatter_sum(): lax.psum_scatter(part, 'tensor', scatter_dimension=col_axis, tiled=True)  66 us
    reduce_scatter x1, waiting for transfers between devices, scatter_sum(): lax.psum_scatter(partial.astype(jnp.bfloat16), 'dp', scatter_dimension=co...  63.2 us
    psum x1, blocking collectives, per_device(): lax.psum((gain_mix_grad, gain_ff_grad, tap_grads), ('dp', 'tensor'))  40.8 us
    dot_general x1, matrix products, per_device(): jnp.einsum('jgf,jdf->gd', gate_up_grad, gate_up_full, preferred_element_t...  32.2 us
    dot_general x1, matrix products, per_device(): jnp.einsum('gd,jdf->jgf', normed_ff, gate_up_full, preferred_element_type...  30.1 us
  transfers between devices with their start and end apart: 19, of which 14 were waited for; matrix products, arithmetic and copies ran while one was open for 21% of the time, Pallas kernels for 0%

profile of v1, /device:TPU:0, one launch (start us, length us, event | category | flops | bytes accessed | tf_op | source)
XLA Modules:
  0.0 1164.1 jit_solution(8418909406327394682)
XLA Ops:
  8.0 10.5 all_gather.24
  18.5 6.5 all_gather.26
  25.0 10.7 all-gather.10.cloned.1.call-done
  35.8 10.7 all_gather.30
  46.6 2.9 copy.36
  49.5 4.6 copy.40
  55.3 44.8 %all-gather.6.cloned.1.call-done = bf16[3,1024,1024]{2,1,0:T(8,128)(2,1)} async-done(((bf16[3,64,1024]{2,1,0:T(8,128)(2,1)}), bf16[3,1024,1024]{2,1,0:T(8,128)(2,1)}) %all-gather.6.cloned.1.call-update) | async-done | bytes 6291472 | tf_op jit(solution)/shard_map/all_gather | solution.py:34
  100.1 11.0 convolution_bitcast_fusion.1
  111.1 1.4 slice_multiply_fusion
  112.5 3.6 copy-done.2
  116.9 4.5 fusion.18
  121.4 21.0 %all-gather.8.cloned.1.call-done = bf16[1024,1024]{1,0:T(8,128)(2,1)} async-done(((bf16[64,1024]{1,0:T(8,128)(2,1)}), bf16[1024,1024]{1,0:T(8,128)(2,1)}) %all-gather.8.cloned.1.call-update) | async-done | bytes 2097168 | tf_op jit(solution)/shard_map/all_gather | solution.py:34
  142.5 6.6 multiply_reduce_fusion.4
  149.1 92.4 %all-gather.12.cloned.1.call-done = bf16[2,1024,4608]{2,1,0:T(8,128)(2,1)} async-done(((bf16[2,64,4608]{2,1,0:T(8,128)(2,1)}), bf16[2,1024,4608]{2,1,0:T(8,128)(2,1)}) %all-gather.12.cloned.1.call-update) | async-done | bytes 18874384 | tf_op jit(solution)/shard_map/all_gather | solution.py:34
  241.5 30.1 %convolution_bitcast_fusion = f32[2,1024,4608]{2,1,0:T(8,128)} fusion(bf16[2,1024,4608]{2,1,0:T(8,128)(2,1)} %all-gather.12.cloned.1.call-done, f32[1024,1024]{0,1:T(8,128)} %get-tuple-element.59, f32[1024]{0:T(1024)S(1)} %copy-done.14, f32[1024]{0:T(1024)S(1)} %get-tuple-element.57), kind=kOutput, calls=%fused_computation.9 | convolution fusion | flops 19330498560 | bytes 60825600 | tf_op jit(solution)/shard_map/gd,jdf->jgf/dot_general | solution.py:85
  271.6 53.0 %all-gather.14.cloned.1.call-done = bf16[1024,4608]{1,0:T(8,128)(2,1)} async-done(((bf16[64,4608]{1,0:T(8,128)(2,1)}), bf16[1024,4608]{1,0:T(8,128)(2,1)}) %all-gather.14.cloned.1.call-update) | async-done | bytes 9437200 | tf_op jit(solution)/shard_map/all_gather | solution.py:34
  324.6 29.0 %fusion.3 = (bf16[1,1024,4608]{2,1,0:T(8,128)(2,1)}, bf16[1,1024,4608]{2,1,0:T(8,128)(2,1)}, bf16[1024,4608]{1,0:T(8,128)(2,1)}) fusion(f32[2,1024,4608]{2,1,0:T(8,128)} %convolution_bitcast_fusion, bf16[1024,1024]{1,0:T(8,128)(2,1)S(1)} %copy-done.8, bf16[1024,4608]{1,0:T(8,128)(2,1)} %all-gather.14.cloned.1.call-done), kind=kOutput, calls=%fused_computation.21 | convolution fusion | flops 9734455296 | bytes 77594624 | tf_op jit(solution)/shard_map/dot_general | solution.py:99
  353.6 32.2 %fusion.16 = (f32[1024]{0:T(1024)}, f32[1024]{0:T(1024)S(1)}, f32[1024,1024,1]{0,1,2:T(8,128)}) fusion(f32[1024,1024]{0,1:T(8,128)} %get-tuple-element.59, f32[1024]{0:T(1024)S(1)} %get-tuple-element.57, f32[1024]{0:T(1024)S(1)} %copy-done.14, bf16[2,1024,4608]{2,1,0:T(8,128)(2,1)} %all-gather.12.cloned.1.call-done, ...), kind=kOutput, calls=%fused_computation.42 | convolution fusion | flops 19343081472 | bytes 46153728 | tf_op jit(solution)/shard_map/jgf,jdf->gd/dot_general | solution.py:112
  385.8 6.7 subtract_add_fusion
  392.5 11.3 multiply_reduce_fusion.2
  403.7 0.9 slice.61
  404.7 0.9 slice.60
  405.6 3.8 multiply_convert_fusion.4
  409.4 2.0 multiply_convert_fusion.3
  411.4 0.9 copy-done.6
  413.0 8.8 convert_bitcast_fusion.1
  421.8 2.9 slice_bitcast_fusion.6
  424.7 4.0 copy.75
  428.8 3.9 copy.73
  432.8 4.0 copy.71
  436.8 6.7 convolution_convert_fusion.1
  443.6 28.2 %convert_bitcast_fusion = bf16[2,1024,4608]{1,2,0:T(8,128)(2,1)} fusion(bf16[1,1024,4608]{2,1,0:T(8,128)(2,1)} %get-tuple-element.43, bf16[1,1024,4608]{2,1,0:T(8,128)(2,1)} %get-tuple-element.42, f32[1024,1024]{0,1:T(8,128)} %get-tuple-element.59, f32[1024]{0:T(1024)S(1)} %copy-done.14, f32[1024]{0:T(1024)S(1)} %get-tuple-element.57), kind=kOutput, calls=%fused_computation.3 | convolution fusion | flops 19349372928 | bytes 41951232 | tf_op jit(solution)/shard_map/gd,jgf->jdf/dot_general | solution.py:108
  471.8 15.0 %slice_bitcast_fusion.3 = (bf16[1024,4608]{0,1:T(8,128)(2,1)}, bf16[1024,4608]{0,1:T(8,128)(2,1)}) fusion(bf16[2,1024,4608]{1,2,0:T(8,128)(2,1)} %convert_bitcast_fusion), kind=kLoop, calls=%fused_computation.14 | loop fusion | bytes 37748736 | tf_op jit(solution)/shard_map/convert_element_type | solution.py:41
  486.8 12.7 %copy.79 = bf16[1024,4608]{1,0:T(8,128)(2,1)} copy(bf16[1024,4608]{0,1:T(8,128)(2,1)} %get-tuple-element.46) | data formatting | bytes 18874368
  499.6 12.9 %copy.77 = bf16[1024,4608]{1,0:T(8,128)(2,1)} copy(bf16[1024,4608]{0,1:T(8,128)(2,1)} %get-tuple-element.45) | data formatting | bytes 18874368
  512.5 16.9 %fusion.4 = bf16[1024,4608]{0,1:T(8,128)(2,1)} fusion(bf16[1024,4608]{1,0:T(8,128)(2,1)} %get-tuple-element.44, bf16[1024,1024]{1,0:T(8,128)(2,1)} %param.17), kind=kOutput, calls=%fused_computation.22 | convolution fusion | flops 9668395008 | bytes 20971520 | tf_op jit(solution)/shard_map/dot_general | solution.py:100
  529.4 12.6 %copy.81 = bf16[1024,4608]{1,0:T(8,128)(2,1)} copy(bf16[1024,4608]{0,1:T(8,128)(2,1)} %fusion.4) | data formatting | bytes 18874368
  542.1 1.7 copy.76
  543.9 9.6 reduce-scatter.45.cloned.1.call-done
  553.5 1.7 copy.74
  555.4 62.7 %reduce-scatter.43.cloned.1.call-done = bf16[64,1024]{1,0:T(8,128)(2,1)} async-done(((bf16[1024,1024]{1,0:T(8,128)(2,1)}), bf16[64,1024]{1,0:T(8,128)(2,1)}) %reduce-scatter.43.cloned.1.call-update) | async-done | bytes 131088
  618.1 1.7 copy.72
  619.9 63.2 %reduce-scatter.33.cloned.1.call-done = bf16[64,1024]{1,0:T(8,128)(2,1)} async-done(((bf16[1024,1024]{1,0:T(8,128)(2,1)}), bf16[64,1024]{1,0:T(8,128)(2,1)}) %reduce-scatter.33.cloned.1.call-update) | async-done | bytes 131088 | tf_op jit(solution)/shard_map/reduce_scatter | solution.py:40
  683.2 114.1 %reduce-scatter.51.cloned.1.call-done = bf16[64,4608]{1,0:T(8,128)(2,1)} async-done(((bf16[1024,4608]{1,0:T(8,128)(2,1)}), bf16[64,4608]{1,0:T(8,128)(2,1)}) %reduce-scatter.51.cloned.1.call-update) | async-done | bytes 589840
  797.3 2.3 copy.80
  799.6 16.8 %add_convert_fusion = bf16[1024,1024]{0,1:T(8,128)(2,1)} fusion(f32[1024,1024]{0,1:T(8,128)} %get-tuple-element.59, bf16[1024,4608]{1,0:T(8,128)(2,1)} %get-tuple-element.44, bf16[1024,4608]{1,0:T(8,128)(2,1)} %all-gather.14.cloned.1.call-done), kind=kOutput, calls=%fused_computation.51 | convolution fusion | flops 9665773568 | bytes 25165824 | tf_op jit(solution)/shard_map/dot_general | solution.py:95
  816.4 4.2 copy.49
  820.6 91.6 %reduce-scatter.49.cloned.1.call-done = bf16[64,4608]{1,0:T(8,128)(2,1)} async-done(((bf16[1024,4608]{1,0:T(8,128)(2,1)}), bf16[64,4608]{1,0:T(8,128)(2,1)}) %reduce-scatter.49.cloned.1.call-update) | async-done | bytes 589840
  912.3 2.3 copy.78
  914.6 13.5 %fusion.13 = (f32[1024]{0:T(1024)S(1)}, f32[1024]{0:T(1024)S(1)}, f32[1024,1024,1]{0,1,2:T(8,128)}) fusion(bf16[1024,1024]{0,1:T(8,128)(2,1)S(1)} %copy-done.4, f32[1024]{0:T(1024)S(1)} %get-tuple-element.55, f32[1024]{0:T(1024)S(1)} %copy-done.15, bf16[3,1024,1024]{2,1,0:T(8,128)(2,1)} %all-gather.6.cloned.1.call-done, ...), kind=kOutput, calls=%fused_computation.34 | convolution fusion | flops 6456080384 | bytes 18890752 | tf_op jit(solution)/shard_map/jgc,jdc->gd/dot_general | solution.py:146
  928.1 99.0 %reduce-scatter.53.cloned.1.call-done = bf16[64,4608]{1,0:T(8,128)(2,1)} async-done(((bf16[1024,4608]{1,0:T(8,128)(2,1)}), bf16[64,4608]{1,0:T(8,128)(2,1)}) %reduce-scatter.53.cloned.1.call-update) | async-done | bytes 589840
  1027.1 2.3 copy.82
  1029.4 6.4 fusion.10
  1035.9 5.4 copy.50
  1041.3 40.8 %all-reduce.4 = (f32[1024]{0:T(1024)}, f32[3,1024]{1,0:T(4,128)}, f32[1024]{0:T(1024)}) all-reduce(f32[1024]{0:T(1024)S(1)} %get-tuple-element.29, f32[3,1024]{1,0:T(4,128)S(1)} %pad_maximum_fusion.6, f32[1024]{0:T(1024)S(1)} %copy-done.16), channel_id=1, replica_groups=mesh['dp'=16,'tensor'=2] {'dp','tensor'}, use_global_device_ids=true, to_apply=%region_5.6 | all-reduce | flops 5120 | bytes 40960 | tf_op jit(solution)/shard_map/psum | solution.py:151
  1082.0 1.2 maximum_convert_fusion.1
  1083.2 1.0 copy.51
  1084.2 1.5 convert_element_type.98
  1085.7 21.2 %reduce-scatter.39.cloned.1.call-done = bf16[64,2304]{0,1:T(8,128)(2,1)} async-done(((bf16[64,4608]{0,1:T(8,128)(2,1)}), bf16[64,2304]{0,1:T(8,128)(2,1)}) %reduce-scatter.39.cloned.1.call-update) | async-done | bytes 294928 | tf_op jit(solution)/shard_map/reduce_scatter | solution.py:43
  1106.9 23.9 %reduce-scatter.37.cloned.1.call-done = bf16[64,2304]{0,1:T(8,128)(2,1)} async-done(((bf16[64,4608]{0,1:T(8,128)(2,1)}), bf16[64,2304]{0,1:T(8,128)(2,1)}) %reduce-scatter.37.cloned.1.call-update) | async-done | bytes 294928 | tf_op jit(solution)/shard_map/reduce_scatter | solution.py:43
  1130.9 1.6 maximum_convert_fusion
  1132.5 1.7 copy.52
  1134.2 20.8 %reduce-scatter.41.cloned.1.call-done = bf16[64,2304]{0,1:T(8,128)(2,1)} async-done(((bf16[64,4608]{0,1:T(8,128)(2,1)}), bf16[64,2304]{0,1:T(8,128)(2,1)}) %reduce-scatter.41.cloned.1.call-update) | async-done | bytes 294928 | tf_op jit(solution)/shard_map/reduce_scatter | solution.py:43
  1155.0 2.1 copy.53
  (89 shorter events, 4.4 us)
Async XLA Ops:
  7.2 28.6 %all-gather.10.cloned.1.call-start = ((), (), s32[]{:S(2)}) async-start(), calls=%async_computation.16 | async-start | bytes 1769472 | tf_op jit(solution)/shard_map/all_gather | solution.py:33
  7.9 92.2 %all-gather.6.cloned.1.call-start = ((), (), s32[]{:S(2)}) async-start(), calls=%async_computation.14 | async-start | bytes 6684672 | tf_op jit(solution)/shard_map/all_gather | solution.py:34
  18.5 124.0 %all-gather.8.cloned.1.call-start = ((), (), s32[]{:S(2)}) async-start(), calls=%async_computation.15 | async-start | bytes 2228224 | tf_op jit(solution)/shard_map/all_gather | solution.py:34
  25.0 216.5 %all-gather.12.cloned.1.call-start = ((), (), s32[]{:S(2)}) async-start(), calls=%async_computation.17 | async-start | bytes 20054016 | tf_op jit(solution)/shard_map/all_gather | solution.py:34
  35.8 288.8 %all-gather.14.cloned.1.call-start = ((), (), s32[]{:S(2)}) async-start(), calls=%async_computation.18 | async-start | bytes 10027008 | tf_op jit(solution)/shard_map/all_gather | solution.py:34
  46.6 495.6 %reduce-scatter.47.cloned.1.call-start = ((), (), s32[]{:S(2)}) async-start(), calls=%async_computation.29 | async-start | bytes 2228224
  49.5 92.9 %copy-start.3 = (bf16[1024,1024]{0,1:T(8,128)(2,1)}, bf16[1024,1024]{0,1:T(8,128)(2,1)S(1)}, u32[]{:S(2)}) copy-start(bf16[1024,1024]{0,1:T(8,128)(2,1)S(1)} %copy.36) | copy-start | bytes 6291460
  49.5 5.8 copy-start.13
  49.5 50.6 %copy-start.15 = (f32[1024]{0:T(1024)S(1)}, f32[1024]{0:T(1024)}, u32[]{:S(2)}) copy-start(f32[1024]{0:T(1024)} %param.10) | copy-start | bytes 12292
  111.1 5.0 copy-start.2
  112.5 4.4 copy-start
  142.5 99.1 %copy-start.14 = (f32[1024]{0:T(1024)S(1)}, f32[1024]{0:T(1024)}, u32[]{:S(2)}) copy-start(f32[1024]{0:T(1024)} %param.14) | copy-start | bytes 12292
  241.5 83.0 %copy-start.8 = (bf16[1024,1024]{1,0:T(8,128)(2,1)S(1)}, bf16[1024,1024]{1,0:T(8,128)(2,1)}, u32[]{:S(2)}) copy-start(bf16[1024,1024]{1,0:T(8,128)(2,1)} %param.17) | copy-start | bytes 6291460
  353.6 32.2 %copy-start.5 = (bf16[1024,1024]{0,1:T(8,128)(2,1)S(1)}, bf16[1024,1024]{0,1:T(8,128)(2,1)}, u32[]{:S(2)}) copy-start(bf16[1024,1024]{0,1:T(8,128)(2,1)} %copy.40) | copy-start | bytes 6291460
  385.8 6.7 copy-start.1
  385.8 19.8 %slice-start = ((s8[12582912]{0:T(1024)(128)(4,1)}), s8[4194304]{0:T(1024)(128)(4,1)S(1)}, s32[]{:S(2)}) async-start(s8[12582912]{0:T(1024)(128)(4,1)} %bitcast.121), calls=%async_computation.33 | async-start | bytes 8388608
  392.5 13.1 %slice-start.1 = ((s8[12582912]{0:T(1024)(128)(4,1)}), s8[4194304]{0:T(1024)(128)(4,1)S(1)}, s32[]{:S(2)}) async-start(s8[12582912]{0:T(1024)(128)(4,1)} %bitcast.121), calls=%async_computation.34 | async-start | bytes 8388608
  392.5 13.1 %slice-start.2 = ((s8[12582912]{0:T(1024)(128)(4,1)}), s8[4194304]{0:T(1024)(128)(4,1)S(1)}, s32[]{:S(2)}) async-start(s8[12582912]{0:T(1024)(128)(4,1)} %bitcast.121), calls=%async_computation.35 | async-start | bytes 8388608
  409.4 2.1 copy-start.4
  409.4 3.0 copy-start.6
  409.4 3.6 copy-start.7
  428.7 124.8 %reduce-scatter.45.cloned.1.call-start = ((), (), s32[]{:S(2)}) async-start(), calls=%async_computation.28 | async-start | bytes 2228224
  432.7 185.3 %reduce-scatter.43.cloned.1.call-start = ((), (), s32[]{:S(2)}) async-start(), calls=%async_computation.27 | async-start | bytes 2228224
  436.8 246.3 %reduce-scatter.33.cloned.1.call-start = ((), (), s32[]{:S(2)}) async-start(), calls=%async_computation.22 | async-start | bytes 2228224 | tf_op jit(solution)/shard_map/reduce_scatter | solution.py:40
  443.5 353.7 %reduce-scatter.51.cloned.1.call-start = ((), (), s32[]{:S(2)}) async-start(), calls=%async_computation.31 | async-start | bytes 10027008
  499.5 412.7 %reduce-scatter.49.cloned.1.call-start = ((), (), s32[]{:S(2)}) async-start(), calls=%async_computation.30 | async-start | bytes 10027008
  512.5 514.6 %reduce-scatter.53.cloned.1.call-start = ((), (), s32[]{:S(2)}) async-start(), calls=%async_computation.32 | async-start | bytes 10027008
  542.1 540.0 %reduce-scatter.31.cloned.1.call-start = ((), (), s32[]{:S(2)}) async-start(), calls=%async_computation.21 | async-start | bytes 393216 | tf_op jit(solution)/shard_map/reduce_scatter | solution.py:43
  543.9 538.1 %reduce-scatter.29.cloned.1.call-start = ((), (), s32[]{:S(2)}) async-start(), calls=%async_computation.20 | async-start | bytes 393216 | tf_op jit(solution)/shard_map/reduce_scatter | solution.py:43
  555.3 526.7 %reduce-scatter.27.cloned.1.call-start = ((), (), s32[]{:S(2)}) async-start(), calls=%async_computation.19 | async-start | bytes 393216 | tf_op jit(solution)/shard_map/reduce_scatter | solution.py:43
  619.8 464.4 %reduce-scatter.35.cloned.1.call-start = ((), (), s32[]{:S(2)}) async-start(), calls=%async_computation.23 | async-start | bytes 196608 | tf_op jit(solution)/shard_map/reduce_scatter | solution.py:43
  683.1 423.8 %reduce-scatter.39.cloned.1.call-start = ((), (), s32[]{:S(2)}) async-start(), calls=%async_computation.25 | async-start | bytes 1769472 | tf_op jit(solution)/shard_map/reduce_scatter | solution.py:43
  799.6 331.3 %reduce-scatter.37.cloned.1.call-start = ((), (), s32[]{:S(2)}) async-start(), calls=%async_computation.24 | async-start | bytes 1769472 | tf_op jit(solution)/shard_map/reduce_scatter | solution.py:43
  914.6 114.8 %copy-start.9 = (f32[1024]{0:T(1024)S(1)}, f32[1024]{0:T(1024)}, u32[]{:S(2)}) copy-start(f32[1024]{0:T(1024)} %get-tuple-element.54) | copy-start | bytes 12292
  914.6 240.4 %reduce-scatter.41.cloned.1.call-start = ((), (), s32[]{:S(2)}) async-start(), calls=%async_computation.26 | async-start | bytes 1769472 | tf_op jit(solution)/shard_map/reduce_scatter | solution.py:43
  1035.8 5.4 copy-start.10
  1035.8 5.4 copy-start.11
  1035.8 5.4 copy-start.12
  1035.9 5.4 copy-start.16
Sparse Core Ops, SparseCore 0:
  9.5 26.1 all-gather.9
  37.9 62.1 all-gather.5
  102.3 40.1 all-gather.7
  143.9 97.6 all-gather.11
  243.6 80.8 all-gather.13
  428.8 60.1 reduce-scatter.46
  492.8 60.6 reduce-scatter.44
  557.3 60.7 reduce-scatter.42
  622.4 60.6 reduce-scatter.32
  687.1 110.1 reduce-scatter.50
  801.4 110.8 reduce-scatter.48
  916.2 110.8 reduce-scatter.52
  1029.9 11.3 reduce-scatter.30
  1044.0 11.7 reduce-scatter.28
  1057.8 11.8 reduce-scatter.26
  1071.8 10.7 reduce-scatter.34
  1085.3 21.6 reduce-scatter.38
  1109.0 21.8 reduce-scatter.36
  1133.1 21.8 reduce-scatter.40

commit v2 on v1

--- a/solution.py
+++ b/solution.py
@@ -1,6 +1,10 @@
+import functools
+
 import jax
 import jax.numpy as jnp
 from jax import lax
+from jax.experimental import pallas as pl
+from jax.experimental.pallas import tpu as pltpu
 from jax.sharding import PartitionSpec as P
 
 LEN = 1024
@@ -29,9 +33,196 @@
     return (grad_values, gain_grad)
 
 
-def gather_cols(shard, col_axis):
-    part = lax.all_gather(shard, "tensor", axis=col_axis, tiled=True)
-    return lax.all_gather(part, "dp", axis=col_axis - 1, tiled=True)
+MESH = pl.DeviceIdType.MESH
+ORDERS = ("xzy", "yzx", "zxy", "zyx")
+GROUPS = ((0, 0, 3), (1, 0, 1), (2, 0, 1), (2, 1, 1), (3, 0, 1))
+STAGES = {"x": 0, "y": 1, "z": 2, "c": 3}
+
+
+class Place:
+    def __init__(self, slabs):
+        dp = lax.axis_index("dp")
+        self.dp, self.x = dp, lax.axis_index("tensor")
+        self.slabs = slabs
+        self.a = dp // 4
+        self.y = (dp // 2) % 2
+        self.c = dp % 2
+        self.peer = {
+            "x": (dp, 1 - self.x),
+            "y": (dp + 2 - 4 * self.y, self.x),
+            "c": (dp + 1 - 2 * self.c, self.x),
+            "down": (dp - 4, self.x),
+            "up": (dp + 4, self.x),
+        }
+        self.has = {"down": self.a > 0, "up": self.a < slabs - 1}
+
+    def greet(self):
+        barrier = pltpu.get_barrier_semaphore()
+        for name in ("x", "y", "c"):
+            pl.semaphore_signal(barrier, 1, device_id=self.peer[name], device_id_type=MESH)
+        for name in ("down", "up"):
+
+            @pl.when(self.has[name])
+            def _(name=name):
+                pl.semaphore_signal(barrier, 1, device_id=self.peer[name], device_id_type=MESH)
+
+        ends = self.has["down"].astype(jnp.int32) + self.has["up"].astype(jnp.int32)
+        pl.semaphore_wait(barrier, 3 + ends)
+
+
+def pick(own, which):
+    if which == "all":
+        return slice(None)
+    return own if which == "own" else 1 - own
+
+
+def gather_ticks(place, full, planes, rows, cols, order, send_sem, recv_sem, base):
+    here = place
+    n = cols
+
+    def region(slab, y, c, x):
+        columns = slice(None) if x == "all" else pl.ds(pl.multiple_of(pick(here.x, x) * n, 128), n)
+        return full.at[planes, slab, pick(here.y, y), pick(here.c, c), rows, columns]
+
+    def span(stage, side):
+        i = order.index(stage) if stage != "c" else 3
+        done = order[:i]
+        sel = {d: ("all" if d in done else "own") for d in "xy"}
+        if stage in "xy":
+            sel[stage] = side
+        return sel["y"], (side if stage == "c" else "own"), sel["x"]
+
+    def copy(stage, slab, side, peer):
+        ref = region(slab, *span(stage, side))
+        k = STAGES[stage]
+        return pltpu.make_async_remote_copy(
+            ref, ref, send_sem.at[base, k, slab], recv_sem.at[base, k, slab], peer, MESH
+        )
+
+    zi = order.index("z")
+    pre, post = order[:zi], order[zi + 1 :] + "c"
+    total = len(pre) + here.slabs + len(post) + 1
+    ticks = [[] for _ in range(total)]
+    sends = []
+
+    def start(stage, slab, peer):
+        copy(stage, slab, "own", peer).start()
+
+    def finish(stage, slab):
+        copy(stage, slab, "own" if stage == "z" else "other", here.peer["x"]).wait_recv()
+
+    def chain(t, stages, slab, cond):
+        for i, stage in enumerate(stages):
+            ticks[t + i].append((cond, functools.partial(start, stage, slab, here.peer[stage])))
+            ticks[t + i + 1].append((cond, functools.partial(finish, stage, slab)))
+            sends.append((cond, stage, slab))
+
+    chain(0, pre, here.a, None)
+    t0 = len(pre)
+    for name in ("down", "up"):
+        ticks[t0].append((here.has[name], functools.partial(start, "z", here.a, here.peer[name])))
+        sends.append((here.has[name], "z", here.a))
+    chain(t0, post, here.a, None)
+    for s in range(1, here.slabs):
+        for slab, come, to in (
+            (here.a - s, here.a >= s, "up"),
+            (here.a + s, here.a + s < here.slabs, "down"),
+        ):
+            both = jnp.logical_and(come, here.has[to])
+            ticks[t0 + s].append((come, functools.partial(finish, "z", slab)))
+            ticks[t0 + s].append((both, functools.partial(start, "z", slab, here.peer[to])))
+            sends.append((both, "z", slab))
+            chain(t0 + s, post, slab, come)
+
+    def drain():
+        for cond, stage, slab in sends:
+            when(cond, copy(stage, slab, "own", here.peer["x"]).wait_send)
+
+    return ticks, drain
+
+
+def when(cond, action):
+    if cond is None:
+        action()
+    else:
+        pl.when(cond)(action)
+
+
+def merge(schedules, lag):
+    longest = max(lag * i + len(s) for i, s in enumerate(schedules))
+    for t in range(longest):
+        for i, s in enumerate(schedules):
+            k = t - lag * i
+            if 0 <= k < len(s):
+                for cond, action in s[k]:
+                    when(cond, action)
+
+
+def parts_of(rows):
+    return 4 if rows >= 64 else 1
+
+
+def gather_kernel(slabs, layout, lag, *refs):
+    count = len(layout["shapes"])
+    shards, fulls = refs[:count], refs[count : 2 * count]
+    send_sem, recv_sem, own_sem = refs[2 * count :]
+    place = Place(slabs)
+    local = []
+    for i, (shard, full) in enumerate(zip(shards, fulls)):
+        n = shard.shape[2]
+        columns = pl.ds(pl.multiple_of(place.x * n, 128), n)
+        own = pltpu.make_async_copy(
+            shard, full.at[:, place.a, place.y, place.c, :, columns], own_sem.at[i]
+        )
+        own.start()
+        local.append(own)
+    place.greet()
+    for own in local:
+        own.wait()
+    schedules, drains = [], []
+    base = 0
+    for i, plane0, planes in layout["groups"]:
+        rows, n = shards[i].shape[1:]
+        parts = parts_of(rows)
+        size = rows // parts
+        both = []
+        for p in range(parts):
+            ticks, drain = gather_ticks(
+                place, fulls[i], pl.ds(plane0, planes), pl.ds(p * size, size), n,
+                ORDERS[p], send_sem, recv_sem, base,
+            )
+            base += 1
+            both.append(ticks)
+            drains.append(drain)
+        length = max(len(t) for t in both)
+        schedules.append([sum((t[k] for t in both if k < len(t)), []) for k in range(length)])
+    merge(schedules, lag)
+    for drain in drains:
+        drain()
+
+
+def gather_all(shards, groups, dp, tensor, lag=2):
+    slabs = dp // 4
+    shapes = [s.shape for s in shards]
+    parts = parts_of(shapes[0][1])
+    bases = len(groups) * parts
+    out = [
+        jax.ShapeDtypeStruct((s[0], slabs, 2, 2, s[1], s[2] * tensor), jnp.bfloat16) for s in shapes
+    ]
+    full = pl.pallas_call(
+        functools.partial(gather_kernel, slabs, {"shapes": shapes, "groups": groups}, lag),
+        out_shape=out,
+        in_specs=[pl.BlockSpec(memory_space=pltpu.VMEM)] * len(shards),
+        out_specs=[pl.BlockSpec(memory_space=pl.ANY)] * len(shards),
+        scratch_shapes=[
+            pltpu.SemaphoreType.DMA((bases, 4, slabs)),
+            pltpu.SemaphoreType.DMA((bases, 4, slabs)),
+            pltpu.SemaphoreType.DMA((len(shards),)),
+        ],
+        compiler_params=pltpu.CompilerParams(collective_id=0, has_side_effects=True),
+        name="gather_weights",
+    )(*shards)
+    return [f.reshape(s[0], dp * s[1], s[2] * tensor) for f, s in zip(full, shapes)]
 
 
 def scatter_sum(partial, col_axis):
@@ -57,10 +248,13 @@
     grad_out,
 ):
     inputs = tokens.astype(jnp.float32)
-    in_full = gather_cols(in_weight, 2)
-    out_full = gather_cols(out_weight, 1)
-    gate_up_full = gather_cols(gate_up_weight, 2)
-    down_full = gather_cols(down_weight, 1)
+    in_full, out_full, gate_up_full, down_full = gather_all(
+        [in_weight, out_weight[None], gate_up_weight, down_weight[None]],
+        GROUPS,
+        lax.axis_size("dp"),
+        lax.axis_size("tensor"),
+    )
+    out_full, down_full = out_full[0], down_full[0]
     rows, width = tokens.shape
     seq_count = rows // LEN
     scale_mix = norm_scale(inputs)

time: 1170 us -> 1060 us (0.906)
  waiting for transfers between devices: 729 us -> 497 us
  Pallas kernels: 0 us -> 145 us
  blocking collectives: 68.4 us -> 40.7 us
    all_gather x5 -> x0, waiting for transfers between devices: 222 us -> none  [the longest x4 211 us: gather_cols(): return lax.all_gather(part, 'dp', axis=col_axis - 1, tiled=True)]
    pallas_call x0 -> x1, Pallas kernels: none -> 145 us  [gather_all(): pl.pallas_call(functools.partial(gather_kernel, slabs, {'shapes': shapes,...]
    all_gather x3 -> x0, blocking collectives: 27.7 us -> none  [gather_cols(): part = lax.all_gather(shard, 'tensor', axis=col_axis, tiled=True)]
    unnamed x25 -> x20, waiting for transfers between devices: 378 us -> 368 us
    unnamed x59 -> x93, local copies, waits for them, and re-layouts: 90.1 us -> 89.8 us
  transfers between devices with their start and end apart: 19 -> 14, of which waited for: 14 -> 9; matrix products, arithmetic and copies ran while one was open for 21% -> 18% of each run, Pallas kernels for 0% -> 0%
where the time goes in v2:
time: 1060 us; the launch traced here: 1050 us
  waiting for transfers between devices  497 us (47%)
  matrix products  217 us (20%)
  Pallas kernels  145 us (14%)
  local copies, waits for them, and re-layouts  109 us (10%)
  blocking collectives  40.7 us (4%)
  other arithmetic  26.3 us (2%)
  between operations  14.8 us (1%)
    unnamed x20, waiting for transfers between devices  368 us
    pallas_call x1, Pallas kernels, gather_all(): pl.pallas_call(functools.partial(gather_kernel, slabs, {'shapes': shapes,...  145 us
    unnamed x93, local copies, waits for them, and re-layouts  89.8 us
    reduce_scatter x7, waiting for transfers between devices, scatter_sum(): lax.psum_scatter(part, 'tensor', scatter_dimension=col_axis, tiled=True)  66.4 us
    reduce_scatter x1, waiting for transfers between devices, scatter_sum(): lax.psum_scatter(partial.astype(jnp.bfloat16), 'dp', scatter_dimension=co...  62.6 us
    psum x1, blocking collectives, per_device(): lax.psum((gain_mix_grad, gain_ff_grad, tap_grads), ('dp', 'tensor'))  40.7 us
    dot_general x1, matrix products, per_device(): jnp.einsum('jgf,jdf->gd', gate_up_grad, gate_up_full, preferred_element_t...  31.5 us
    dot_general x1, matrix products, per_device(): jnp.einsum('gd,jdf->jgf', normed_ff, gate_up_full, preferred_element_type...  30 us
  transfers between devices with their start and end apart: 14, of which 9 were waited for; matrix products, arithmetic and copies ran while one was open for 18% of the time, Pallas kernels for 0%

profile of v2, /device:TPU:0, one launch (start us, length us, event | category | flops | bytes accessed | tf_op | source)
XLA Modules:
  0.0 1050.5 jit_solution(3721393666112752212)
XLA Ops:
  7.2 2.9 copy.37
  10.1 0.5 fusion.18
  10.6 0.8 multiply_multiply_fusion
  11.5 145.1 %gather_weights.1 = (bf16[3,4,2,2,64,1024]{5,4,3,2,1,0:T(8,128)(2,1)}, bf16[1,4,2,2,64,1024]{5,4,3,2,1,0:T(8,128)(2,1)}, bf16[2,4,2,2,64,4608]{5,4,3,2,1,0:T(8,128)(2,1)}, bf16[1,4,2,2,64,4608]{5,4,3,2,1,0:T(8,128)(2,1)}) custom-call(bf16[3,64,512]{2,1,0:T(8,128)(2,1)} %refs_0_.1, bf16[1,64,512]{2,1,0:T(8,128)(2,1)} %bitcast.170, ...), custom_call_target="tpu_custom_call" | custom-call | tf_op jit(solution)/shard_map/gather_weights/pallas_call | solution.py:212
  156.5 10.6 %convolution_bitcast_fusion.1 = f32[3,1024,1024]{2,1,0:T(8,128)S(1)} fusion(bf16[3,1024,1024]{2,1,0:T(8,128)(2,1)} %bitcast.184, bf16[1024,1024]{0,1:T(8,128)(2,1)S(1)} %copy.37, f32[1024]{0:T(1024)S(1)} %copy-done.30, f32[1024]{0:T(1024)S(1)} %get-tuple-element.62), kind=kOutput, calls=%fused_computation.36 | convolution fusion | flops 6446645248 | bytes 20979712 | tf_op jit(solution)/shard_map/gd,jdc->jgc/dot_general | solution.py:262
  167.2 1.4 slice_multiply_fusion
  168.6 3.6 copy-done.2
  172.2 4.2 fusion.31
  176.4 4.4 multiply_reduce_fusion.4
  180.8 3.9 copy.42
  184.8 30.0 %convolution_bitcast_fusion = f32[2,1024,4608]{1,2,0:T(8,128)} fusion(bf16[2,1024,4608]{2,1,0:T(8,128)(2,1)} %bitcast.180, f32[1024,1024]{0,1:T(8,128)} %get-tuple-element.66, f32[1024]{0:T(1024)S(1)} %copy-done.29, f32[1024]{0:T(1024)S(1)} %get-tuple-element.64), kind=kOutput, calls=%fused_computation.18 | convolution fusion | flops 19330498560 | bytes 60825600 | tf_op jit(solution)/shard_map/gd,jdf->jgf/dot_general | solution.py:279
  214.8 27.4 %fusion.14 = (bf16[1,1024,4608]{1,2,0:T(8,128)(2,1)}, bf16[1,1024,4608]{1,2,0:T(8,128)(2,1)}) fusion(f32[2,1024,4608]{1,2,0:T(8,128)} %convolution_bitcast_fusion, bf16[1024,4608]{1,0:T(8,128)(2,1)} %bitcast.182, bf16[1024,1024]{1,0:T(8,128)(2,1)S(1)} %copy-done.12), kind=kOutput, calls=%fused_computation.32 | convolution fusion | flops 9725018112 | bytes 68157440 | tf_op jit(solution)/shard_map/dot_general | solution.py:293
  242.3 31.5 %fusion.29 = (f32[1024]{0:T(1024)}, f32[1024]{0:T(1024)S(1)}, f32[1024,1024,1]{0,1,2:T(8,128)}) fusion(f32[1024,1024]{0,1:T(8,128)} %get-tuple-element.66, f32[1024]{0:T(1024)S(1)} %get-tuple-element.64, f32[1024]{0:T(1024)S(1)} %copy-done.29, bf16[2,1024,4608]{2,1,0:T(8,128)(2,1)} %bitcast.181, bf16[1,1024,4608]{1,2,0:T(8,128)(2,1)} %get-tuple-element.51, ...), kind=kOutput, calls=%fused_computation.53 | convolution fusion | flops 19343081472 | bytes 46153728 | tf_op jit(solution)/shard_map/jgf,jdf->gd/dot_general | solution.py:306
  273.8 5.3 subtract_add_fusion
  279.1 11.4 %multiply_reduce_fusion.2 = (f32[1024]{0:T(1024)}, f32[1024]{0:T(1024)}, f32[1024]{0:T(1024)}, f32[1,1024,1024]{2,1,0:T(8,128)S(1)}, bf16[1,1024,1024]{2,1,0:T(8,128)(2,1)}) fusion(f32[1,1022,1024]{2,1,0:T(8,128)S(1)} %bitcast.159, f32[1,1024,1024]{2,1,0:T(8,128)S(1)} %copy-done.1, f32[1,1023,1024]{2,1,0:T(8,128)S(1)} %bitcast.158, ...), kind=kOutput, calls=%fused_computation.56 | convolution fusion | flops 2157966336 | bytes 33554432 | tf_op jit(solution)/shard_map/dot_general | solution.py:312
  290.5 0.5 slice.61
  291.0 0.5 slice.60
  291.5 0.1 copy-done.16
  291.7 2.2 multiply_convert_fusion.3
  294.0 1.1 multiply_convert_fusion.2
  295.1 0.2 copy-done.9
  295.2 1.6 copy-done.4
  296.9 0.8 copy-done.8
  297.7 7.5 convert_bitcast_fusion.1
  305.2 2.7 slice_bitcast_fusion.4
  308.0 3.9 copy.78
  312.0 3.9 copy.76
  316.0 2.6 copy.74
  318.6 6.7 convolution_convert_fusion.1
  325.4 28.1 %convert_bitcast_fusion = bf16[2,1024,4608]{1,2,0:T(8,128)(2,1)} fusion(bf16[1,1024,4608]{1,2,0:T(8,128)(2,1)} %get-tuple-element.51, bf16[1,1024,4608]{1,2,0:T(8,128)(2,1)} %get-tuple-element.50, f32[1024,1024]{0,1:T(8,128)} %get-tuple-element.66, f32[1024]{0:T(1024)S(1)} %copy-done.29, f32[1024]{0:T(1024)S(1)} %get-tuple-element.64), kind=kOutput, calls=%fused_computation.16 | convolution fusion | flops 19349372928 | bytes 41951232 | tf_op jit(solution)/shard_map/gd,jgf->jdf/dot_general | solution.py:302
  353.5 15.1 %slice_bitcast_fusion.1 = (bf16[1024,4608]{0,1:T(8,128)(2,1)}, bf16[1024,4608]{0,1:T(8,128)(2,1)}) fusion(bf16[2,1024,4608]{1,2,0:T(8,128)(2,1)} %convert_bitcast_fusion), kind=kLoop, calls=%fused_computation.23 | loop fusion | bytes 37748736 | tf_op jit(solution)/shard_map/convert_element_type | solution.py:232
  368.6 12.7 %copy.82 = bf16[1024,4608]{1,0:T(8,128)(2,1)} copy(bf16[1024,4608]{0,1:T(8,128)(2,1)} %get-tuple-element.53) | data formatting | bytes 18874368
  381.4 12.8 %copy.80 = bf16[1024,4608]{1,0:T(8,128)(2,1)} copy(bf16[1024,4608]{0,1:T(8,128)(2,1)} %get-tuple-element.52) | data formatting | bytes 18874368
  394.1 0.0 reduce-scatter.53.cloned.1.call-start
  394.2 1.6 copy-done.13
  395.8 20.5 %fusion.15 = bf16[1024,4608]{0,1:T(8,128)(2,1)} fusion(bf16[1024,1024]{1,0:T(8,128)(2,1)S(1)} %copy-done.13, f32[2,1024,4608]{1,2,0:T(8,128)} %convolution_bitcast_fusion), kind=kOutput, calls=%fused_computation.33 | convolution fusion | flops 9696706560 | bytes 49283072 | tf_op jit(solution)/shard_map/dot_general | solution.py:294
  416.3 12.7 %copy.84 = bf16[1024,4608]{1,0:T(8,128)(2,1)} copy(bf16[1024,4608]{0,1:T(8,128)(2,1)} %fusion.15) | data formatting | bytes 18874368
  429.1 1.7 copy.79
  430.9 8.8 reduce-scatter.45.cloned.1.call-done
  439.7 1.7 copy.77
  441.5 63.3 %reduce-scatter.43.cloned.1.call-done = bf16[64,1024]{1,0:T(8,128)(2,1)} async-done(((bf16[1024,1024]{1,0:T(8,128)(2,1)}), bf16[64,1024]{1,0:T(8,128)(2,1)}) %reduce-scatter.43.cloned.1.call-update) | async-done | bytes 131088
  504.8 1.7 copy.75
  506.6 62.6 %reduce-scatter.33.cloned.1.call-done = bf16[64,1024]{1,0:T(8,128)(2,1)} async-done(((bf16[1024,1024]{1,0:T(8,128)(2,1)}), bf16[64,1024]{1,0:T(8,128)(2,1)}) %reduce-scatter.33.cloned.1.call-update) | async-done | bytes 131088 | tf_op jit(solution)/shard_map/reduce_scatter | solution.py:231
  569.3 114.1 %reduce-scatter.51.cloned.1.call-done = bf16[64,4608]{1,0:T(8,128)(2,1)} async-done(((bf16[1024,4608]{1,0:T(8,128)(2,1)}), bf16[64,4608]{1,0:T(8,128)(2,1)}) %reduce-scatter.51.cloned.1.call-update) | async-done | bytes 589840
  683.4 2.3 copy.83
  685.7 26.1 %add_convert_fusion = bf16[1024,1024]{0,1:T(8,128)(2,1)} fusion(f32[1024,1024]{0,1:T(8,128)} %get-tuple-element.66, bf16[1024,4608]{1,0:T(8,128)(2,1)} %bitcast.183, f32[2,1024,4608]{1,2,0:T(8,128)} %convolution_bitcast_fusion), kind=kOutput, calls=%fused_computation.62 | convolution fusion | flops 9694085120 | bytes 53477376 | tf_op jit(solution)/shard_map/dot_general | solution.py:289
  711.8 4.1 copy.51
  715.9 82.3 %reduce-scatter.49.cloned.1.call-done = bf16[64,4608]{1,0:T(8,128)(2,1)} async-done(((bf16[1024,4608]{1,0:T(8,128)(2,1)}), bf16[64,4608]{1,0:T(8,128)(2,1)}) %reduce-scatter.49.cloned.1.call-update) | async-done | bytes 589840
  798.2 2.3 copy.81
  800.6 13.2 %fusion.26 = (f32[1024]{0:T(1024)S(1)}, f32[1024]{0:T(1024)S(1)}, f32[1024,1024,1]{0,1,2:T(8,128)}) fusion(bf16[1024,1024]{0,1:T(8,128)(2,1)S(1)} %copy-done.5, f32[1024]{0:T(1024)S(1)} %copy-done.24, f32[1024]{0:T(1024)S(1)} %copy-done.32, bf16[3,1024,1024]{2,1,0:T(8,128)(2,1)} %bitcast.185, bf16[1,1024,1024]{2,1,0:T(8,128)(2,1)} %copy-done.10, ...), kind=kOutput, calls=%fused_computation.45 | convolution fusion | flops 6456080384 | bytes 18890752 | tf_op jit(solution)/shard_map/jgc,jdc->gd/dot_general | solution.py:340
  813.8 99.3 %reduce-scatter.53.cloned.1.call-done = bf16[64,4608]{1,0:T(8,128)(2,1)} async-done(((bf16[1024,4608]{1,0:T(8,128)(2,1)}), bf16[64,4608]{1,0:T(8,128)(2,1)}) %reduce-scatter.53.cloned.1.call-update) | async-done | bytes 589840
  913.1 2.3 copy.85
  915.5 6.5 fusion.23
  921.9 5.4 copy.52
  927.4 40.7 %all-reduce.4 = (f32[1024]{0:T(1024)}, f32[3,1024]{1,0:T(4,128)}, f32[1024]{0:T(1024)}) all-reduce(f32[1024]{0:T(1024)S(1)} %get-tuple-element.37, f32[3,1024]{1,0:T(4,128)S(1)} %pad_maximum_fusion.6, f32[1024]{0:T(1024)S(1)} %copy-done.33), channel_id=1, replica_groups=mesh['dp'=16,'tensor'=2] {'dp','tensor'}, use_global_device_ids=true, to_apply=%region_5.6 | all-reduce | flops 5120 | bytes 40960 | tf_op jit(solution)/shard_map/psum | solution.py:345
  968.1 1.2 maximum_convert_fusion.1
  969.3 1.0 copy.53
  970.3 1.5 convert_element_type.104
  971.8 21.6 %reduce-scatter.39.cloned.1.call-done = bf16[64,2304]{0,1:T(8,128)(2,1)} async-done(((bf16[64,4608]{0,1:T(8,128)(2,1)}), bf16[64,2304]{0,1:T(8,128)(2,1)}) %reduce-scatter.39.cloned.1.call-update) | async-done | bytes 294928 | tf_op jit(solution)/shard_map/reduce_scatter | solution.py:234
  993.3 24.1 %reduce-scatter.37.cloned.1.call-done = bf16[64,2304]{0,1:T(8,128)(2,1)} async-done(((bf16[64,4608]{0,1:T(8,128)(2,1)}), bf16[64,2304]{0,1:T(8,128)(2,1)}) %reduce-scatter.37.cloned.1.call-update) | async-done | bytes 294928 | tf_op jit(solution)/shard_map/reduce_scatter | solution.py:234
  1017.5 1.6 maximum_convert_fusion
  1019.0 1.7 copy.54
  1020.8 20.7 %reduce-scatter.41.cloned.1.call-done = bf16[64,2304]{0,1:T(8,128)(2,1)} async-done(((bf16[64,4608]{0,1:T(8,128)(2,1)}), bf16[64,2304]{0,1:T(8,128)(2,1)}) %reduce-scatter.41.cloned.1.call-update) | async-done | bytes 294928 | tf_op jit(solution)/shard_map/reduce_scatter | solution.py:234
  1041.4 2.1 copy.55
  (106 shorter events, 1.0 us)
Async XLA Ops:
  7.2 4.2 copy-start.28
  7.2 149.4 %copy-start.30 = (f32[1024]{0:T(1024)S(1)}, f32[1024]{0:T(1024)}, u32[]{:S(2)}) copy-start(f32[1024]{0:T(1024)} %param.10) | copy-start | bytes 12292
  7.2 421.9 %reduce-scatter.47.cloned.1.call-start = ((), (), s32[]{:S(2)}) async-start(), calls=%async_computation.24 | async-start | bytes 2228224
  10.1 166.3 %copy-start.3 = (bf16[1024,1024]{0,1:T(8,128)(2,1)}, bf16[1024,1024]{0,1:T(8,128)(2,1)S(1)}, u32[]{:S(2)}) copy-start(bf16[1024,1024]{0,1:T(8,128)(2,1)S(1)} %copy.37) | copy-start | bytes 6291460
  11.4 155.8 %copy-start.22 = (f32[1024]{0:T(1024)}, f32[1024]{0:T(1024)S(1)}, u32[]{:S(2)}) copy-start(f32[1024]{0:T(1024)S(1)} %get-tuple-element.62) | copy-start | bytes 12292
  11.4 157.2 %copy-start.15 = (f32[1,1024]{1,0:T(1,128)}, f32[1,1024]{1,0:T(1,128)S(1)}, u32[]{:S(2)}) copy-start(f32[1,1024]{1,0:T(1,128)S(1)} %get-tuple-element.58) | copy-start | bytes 12292
  11.4 157.2 %copy-start.17 = (f32[1,1024]{1,0:T(1,128)}, f32[1,1024]{1,0:T(1,128)S(1)}, u32[]{:S(2)}) copy-start(f32[1,1024]{1,0:T(1,128)S(1)} %get-tuple-element.59) | copy-start | bytes 12292
  11.4 157.2 %copy-start.19 = (f32[1,1024]{1,0:T(1,128)}, f32[1,1024]{1,0:T(1,128)S(1)}, u32[]{:S(2)}) copy-start(f32[1,1024]{1,0:T(1,128)S(1)} %get-tuple-element.60) | copy-start | bytes 12292
  167.2 5.0 copy-start.2
  168.6 7.9 copy-start
  172.2 4.3 copy-start.11
  176.4 4.4 copy-start.14
  180.8 4.0 copy-start.29
  184.8 30.0 %copy-start.12 = (bf16[1024,1024]{1,0:T(8,128)(2,1)S(1)}, bf16[1024,1024]{1,0:T(8,128)(2,1)}, u32[]{:S(2)}) copy-start(bf16[1024,1024]{1,0:T(8,128)(2,1)} %param.17) | copy-start | bytes 6291460
  242.3 31.5 %copy-start.6 = (bf16[1024,1024]{0,1:T(8,128)(2,1)S(1)}, bf16[1024,1024]{0,1:T(8,128)(2,1)}, u32[]{:S(2)}) copy-start(bf16[1024,1024]{0,1:T(8,128)(2,1)} %copy.42) | copy-start | bytes 6291460
  242.3 31.5 %copy-start.7 = (f32[1024,1024]{0,1:T(8,128)S(1)}, f32[1024,1024]{0,1:T(8,128)}, u32[]{:S(2)}) copy-start(f32[1024,1024]{0,1:T(8,128)} %get-tuple-element.66) | copy-start | bytes 12582916
  273.7 5.3 copy-start.1
  273.7 17.7 %slice-start = ((s8[12582912]{0:T(1024)(128)(4,1)}), s8[4194304]{0:T(1024)(128)(4,1)S(1)}, s32[]{:S(2)}) async-start(s8[12582912]{0:T(1024)(128)(4,1)} %bitcast.160), calls=%async_computation.28 | async-start | bytes 8388608
  279.1 12.4 %slice-start.1 = ((s8[12582912]{0:T(1024)(128)(4,1)}), s8[4194304]{0:T(1024)(128)(4,1)S(1)}, s32[]{:S(2)}) async-start(s8[12582912]{0:T(1024)(128)(4,1)} %bitcast.160), calls=%async_computation.29 | async-start | bytes 8388608
  279.1 12.4 %slice-start.2 = ((s8[12582912]{0:T(1024)(128)(4,1)}), s8[4194304]{0:T(1024)(128)(4,1)S(1)}, s32[]{:S(2)}) async-start(s8[12582912]{0:T(1024)(128)(4,1)} %bitcast.160), calls=%async_computation.30 | async-start | bytes 8388608
  291.0 0.7 copy-start.16
  291.0 0.7 copy-start.18
  291.0 0.7 copy-start.20
  293.9 1.3 copy-start.9
  293.9 2.9 copy-start.4
  294.0 3.7 copy-start.8
  294.0 3.7 copy-start.23
  294.0 3.7 copy-start.31
  295.1 10.2 copy-start.10
  311.9 127.7 %reduce-scatter.45.cloned.1.call-start = ((), (), s32[]{:S(2)}) async-start(), calls=%async_computation.23 | async-start | bytes 2228224
  315.9 188.9 %reduce-scatter.43.cloned.1.call-start = ((), (), s32[]{:S(2)}) async-start(), calls=%async_computation.22 | async-start | bytes 2228224
  318.6 250.6 %reduce-scatter.33.cloned.1.call-start = ((), (), s32[]{:S(2)}) async-start(), calls=%async_computation.17 | async-start | bytes 2228224 | tf_op jit(solution)/shard_map/reduce_scatter | solution.py:231
  325.4 358.0 %reduce-scatter.51.cloned.1.call-start = ((), (), s32[]{:S(2)}) async-start(), calls=%async_computation.26 | async-start | bytes 10027008
  381.3 416.9 %reduce-scatter.49.cloned.1.call-start = ((), (), s32[]{:S(2)}) async-start(), calls=%async_computation.25 | async-start | bytes 10027008
  394.1 1.7 copy-start.13
  394.1 519.0 %reduce-scatter.53.cloned.1.call-start = ((), (), s32[]{:S(2)}) async-start(), calls=%async_computation.27 | async-start | bytes 10027008
  429.0 539.1 %reduce-scatter.31.cloned.1.call-start = ((), (), s32[]{:S(2)}) async-start(), calls=%async_computation.16 | async-start | bytes 393216 | tf_op jit(solution)/shard_map/reduce_scatter | solution.py:234
  430.8 537.3 %reduce-scatter.29.cloned.1.call-start = ((), (), s32[]{:S(2)}) async-start(), calls=%async_computation.15 | async-start | bytes 393216 | tf_op jit(solution)/shard_map/reduce_scatter | solution.py:234
  441.4 526.7 %reduce-scatter.27.cloned.1.call-start = ((), (), s32[]{:S(2)}) async-start(), calls=%async_computation.14 | async-start | bytes 393216 | tf_op jit(solution)/shard_map/reduce_scatter | solution.py:234
  506.6 463.7 %reduce-scatter.35.cloned.1.call-start = ((), (), s32[]{:S(2)}) async-start(), calls=%async_computation.18 | async-start | bytes 196608 | tf_op jit(solution)/shard_map/reduce_scatter | solution.py:234
  569.2 424.1 %reduce-scatter.39.cloned.1.call-start = ((), (), s32[]{:S(2)}) async-start(), calls=%async_computation.20 | async-start | bytes 1769472 | tf_op jit(solution)/shard_map/reduce_scatter | solution.py:234
  685.7 331.8 %reduce-scatter.37.cloned.1.call-start = ((), (), s32[]{:S(2)}) async-start(), calls=%async_computation.19 | async-start | bytes 1769472 | tf_op jit(solution)/shard_map/reduce_scatter | solution.py:234
  711.8 88.8 %copy-start.5 = (bf16[1024,1024]{0,1:T(8,128)(2,1)S(1)}, bf16[1024,1024]{0,1:T(8,128)(2,1)}, u32[]{:S(2)}) copy-start(bf16[1024,1024]{0,1:T(8,128)(2,1)} %copy-done.3) | copy-start | bytes 6291460
  711.8 88.8 %copy-start.24 = (f32[1024]{0:T(1024)S(1)}, f32[1024]{0:T(1024)}, u32[]{:S(2)}) copy-start(f32[1024]{0:T(1024)} %copy-done.22) | copy-start | bytes 12292
  711.8 88.8 %copy-start.32 = (f32[1024]{0:T(1024)S(1)}, f32[1024]{0:T(1024)}, u32[]{:S(2)}) copy-start(f32[1024]{0:T(1024)} %param.10) | copy-start | bytes 12292
  800.5 115.0 %copy-start.21 = (f32[1024]{0:T(1024)S(1)}, f32[1024]{0:T(1024)}, u32[]{:S(2)}) copy-start(f32[1024]{0:T(1024)} %get-tuple-element.61) | copy-start | bytes 12292
  800.5 240.9 %reduce-scatter.41.cloned.1.call-start = ((), (), s32[]{:S(2)}) async-start(), calls=%async_computation.21 | async-start | bytes 1769472 | tf_op jit(solution)/shard_map/reduce_scatter | solution.py:234
  921.9 5.4 copy-start.25
  921.9 5.4 copy-start.26
  921.9 5.4 copy-start.27
  921.9 5.4 copy-start.33
Sparse Core Ops, SparseCore 0:
  312.0 62.4 reduce-scatter.46
  378.9 60.7 reduce-scatter.44
  444.0 60.7 reduce-scatter.42
  508.4 60.7 reduce-scatter.32
  573.2 110.1 reduce-scatter.50
  687.3 110.8 reduce-scatter.48
  802.3 110.8 reduce-scatter.52
  915.9 11.3 reduce-scatter.30
  930.2 11.7 reduce-scatter.28
  944.0 11.8 reduce-scatter.26
  958.1 10.6 reduce-scatter.34
  971.6 21.7 reduce-scatter.38
  995.6 21.8 reduce-scatter.36
  1019.6 21.8 reduce-scatter.40

commit v3 on v2

--- a/solution.py
+++ b/solution.py
@@ -36,6 +36,7 @@
 MESH = pl.DeviceIdType.MESH
 ORDERS = ("xzy", "yzx", "zxy", "zyx")
 GROUPS = ((0, 0, 3), (1, 0, 1), (2, 0, 1), (2, 1, 1), (3, 0, 1))
+SUM_GROUPS = ((0, 0, 1), (1, 0, 1), (1, 1, 1), (2, 0, 3), (3, 0, 1))
 STAGES = {"x": 0, "y": 1, "z": 2, "c": 3}
 
 
@@ -56,10 +57,24 @@
         }
         self.has = {"down": self.a > 0, "up": self.a < slabs - 1}
 
-    def greet(self):
+    def greet(self, chain=False):
         barrier = pltpu.get_barrier_semaphore()
         for name in ("x", "y", "c"):
             pl.semaphore_signal(barrier, 1, device_id=self.peer[name], device_id_type=MESH)
+        if chain:
+            for slab in range(self.slabs):
+
+                @pl.when(slab != self.a)
+                def _(slab=slab):
+                    pl.semaphore_signal(
+                        barrier,
+                        1,
+                        device_id=(self.dp + 4 * (slab - self.a), self.x),
+                        device_id_type=MESH,
+                    )
+
+            pl.semaphore_wait(barrier, 2 + self.slabs)
+            return
         for name in ("down", "up"):
 
             @pl.when(self.has[name])
@@ -225,15 +240,299 @@
     return [f.reshape(s[0], dp * s[1], s[2] * tensor) for f, s in zip(full, shapes)]
 
 
-def scatter_sum(partial, col_axis):
-    if col_axis == 2:
-        return jnp.stack([scatter_sum(one, 1) for one in partial])
-    part = lax.psum_scatter(
-        partial.astype(jnp.bfloat16), "dp", scatter_dimension=col_axis - 1, tiled=True
-    )
-    return lax.psum_scatter(part, "tensor", scatter_dimension=col_axis, tiled=True).astype(
-        jnp.float32
-    )
+def add_into(target, extra):
+    rows, cols = target.shape[-2:]
+    step = next(w for w in (1152, 1024, 512, 256, 128) if cols % w == 0)
+    lead = target.shape[:-2]
+    count = 1
+    for d in lead:
+        count *= d
+
+    def body(i, carry):
+        at = []
+        k = i // (cols // step)
+        for d in reversed(lead):
+            at.insert(0, k % d)
+            k = k // d
+        where = (*at, slice(None), pl.ds(pl.multiple_of((i % (cols // step)) * step, 128), step))
+        total = target[where].astype(jnp.float32) + extra[where].astype(jnp.float32)
+        target[where] = total.astype(target.dtype)
+        return carry
+
+    lax.fori_loop(0, count * (cols // step), body, 0)
+
+
+class PartSum:
+    def __init__(self, place, src, out, planes, rows, n, order, bufs, sems, base):
+        self.place, self.src, self.out = place, src, out
+        self.planes, self.rows, self.n, self.order = planes, rows, n, order
+        self.acc, self.got = bufs["acc"], bufs
+        self.load_sem, self.send_sem, self.recv_sem = sems
+        self.base = base
+        self.sends = []
+
+    def cut(self, ref, slab, y, x):
+        place = self.place
+        y = slice(None) if y == "all" else pl.ds(pick(place.y, y), 1)
+        n = self.n
+        x = slice(None) if x == "all" else pl.ds(pl.multiple_of(pick(place.x, x) * n, 128), n)
+        return ref.at[:, slab, y, :, x]
+
+    def span(self, stage, side):
+        i = self.order.index(stage)
+        sel = {d: ("all" if d in self.order[:i] else "own") for d in "xy"}
+        if stage in "xy":
+            sel[stage] = side
+        return sel["y"], sel["x"]
+
+    def load(self, slab):
+        return pltpu.make_async_copy(
+            self.src.at[self.planes, slab, :, self.place.c, self.rows, :],
+            self.acc.at[:, slab],
+            self.load_sem.at[self.base, slab],
+        )
+
+    def copy(self, stage, slab, peer, slot=None):
+        k = STAGES[stage]
+        slot = slab if slot is None else slot
+        if stage == "c":
+            ref = self.src.at[self.planes, slab, :, 1 - self.place.c, self.rows, :]
+        else:
+            ref = self.cut(self.acc, slab, *self.span(stage, "other"))
+        into = self.got[stage]
+        into = into.at[:, 0] if (stage != "c" and "z" in self.order[self.order.index(stage) :][1:]) else into.at[:, slot]
+        return pltpu.make_async_remote_copy(
+            ref, into, self.send_sem.at[self.base, k, slot], self.recv_sem.at[self.base, k, slot],
+            peer, MESH,
+        )
+
+    def start(self, stage, slab):
+        self.copy(stage, slab, self.place.peer[stage]).start()
+
+    def begin(self, slab):
+        self.load(slab).start()
+        self.start("c", slab)
+
+    def take(self, stage, slab, slot=None):
+        copy = self.copy(stage, slab, self.place.peer["x"], slot)
+        copy.wait_recv()
+        slot = slab if slot is None else slot
+        if stage == "c":
+            self.load(slab).wait()
+            add_into(self.acc.at[:, slab], self.got["c"].at[:, slot])
+            return
+        first = "z" in self.order[self.order.index(stage) :][1:]
+        add_into(
+            self.cut(self.acc, slab, *self.span(stage, "own")),
+            self.got[stage].at[:, 0 if first else slot],
+        )
+
+    def take_z(self, slab, slot):
+        self.take("z", slab, slot)
+
+    def send_z(self, slab, to):
+        place = self.place
+        target = place.a + (1 if to == "up" else -1)
+        slot = slab if to == "up" else jnp.where(slab == target, place.slabs, slab)
+        self.copy("z", slab, place.peer[to], slot).start()
+
+    def finish(self):
+        place = self.place
+        y, x = "own", "own"
+        rows = self.rows
+        self.out[:, rows, :] = self.cut(self.acc, place.a, y, x)[:, 0].astype(jnp.float32)
+
+    def ticks(self):
+        place, order = self.place, self.order
+        zi = order.index("z")
+        after = "c" + "".join(reversed(order[zi + 1 :]))
+        before = "".join(reversed(order[:zi]))
+        slabs = place.slabs
+        ticks = [[] for _ in range(slabs + len(after) + len(before) + 2)]
+        bind = functools.partial
+
+        def early(t, slab, cond):
+            ticks[t].append((cond, bind(self.begin, slab)))
+            self.sends.append((cond, "c", slab, None))
+            for i, stage in enumerate(after):
+                ticks[t + i + 1].append((cond, bind(self.take, stage, slab)))
+                if i + 1 < len(after):
+                    ticks[t + i + 1].append((cond, bind(self.start, after[i + 1], slab)))
+                    self.sends.append((cond, after[i + 1], slab, None))
+
+        z0 = len(after)
+        for k, s in enumerate(range(slabs - 1, 0, -1)):
+            for slab, cond, to, more in (
+                (place.a + s, place.a + s < slabs, "up", place.has["down"]),
+                (place.a - s, place.a >= s, "down", place.has["up"]),
+            ):
+                early(k, slab, cond)
+                both = jnp.logical_and(cond, more)
+                ticks[z0 + k].append((both, bind(self.take_z, slab, slab)))
+                ticks[z0 + k].append((cond, bind(self.send_z, slab, to)))
+                self.sends.append((cond, "z", slab, to))
+        last = slabs - 1
+        early(last, place.a, None)
+        ticks[z0 + last].append((place.has["down"], bind(self.take_z, place.a, place.a)))
+        ticks[z0 + last].append((place.has["up"], bind(self.take_z, place.a, slabs)))
+        t = z0 + last
+        for stage in before:
+            ticks[t].append((None, bind(self.start, stage, place.a)))
+            self.sends.append((None, stage, place.a, None))
+            ticks[t + 1].append((None, bind(self.take, stage, place.a)))
+            t += 1
+        ticks[t].append((None, self.finish))
+        return ticks
+
+    def drain(self):
+        place = self.place
+        for cond, stage, slab, to in self.sends:
+            slot = None
+            if to == "down":
+                slot = jnp.where(slab == place.a - 1, place.slabs, slab)
+            when(cond, self.copy(stage, slab, place.peer["x"], slot).wait_send)
+
+
+def sum_buffers(planes, slabs, size, n, tensor, order):
+    cols = n * tensor
+    shapes = {"acc": (planes, slabs, 2, size, cols), "c": (planes, slabs, 2, size, cols)}
+    for i, d in enumerate(order):
+        ys = 2 if "y" in order[:i] else 1
+        xs = cols if "x" in order[:i] else n
+        count = slabs + 1 if d == "z" else (1 if "z" in order[i + 1 :] else slabs)
+        shapes[d] = (planes, count, ys, size, xs)
+    return shapes
+
+
+def small_sum(place, mine, total, got, sems):
+    send_sem, recv_sem = sems
+    steps = []
+
+    def exchange(k, name):
+        return pltpu.make_async_remote_copy(
+            total, got.at[k], send_sem.at[k], recv_sem.at[k], place.peer[name], MESH
+        )
+
+    def open_(k, name):
+        exchange(k, name).start()
+
+    def close(k, name):
+        copy = exchange(k, name)
+        copy.wait_send()
+        copy.wait_recv()
+        total[...] = total[...] + got[k]
+
+    def begin():
+        total[...] = mine[...]
+
+    def chain(slab):
+        return pltpu.make_async_remote_copy(
+            total, got.at[3 + place.a], send_sem.at[3 + slab], recv_sem.at[3 + place.a],
+            (place.dp + 4 * (slab - place.a), place.x), MESH,
+        )
+
+    def arrival(slab):
+        return pltpu.make_async_remote_copy(
+            total, got.at[3 + slab], send_sem.at[3 + slab], recv_sem.at[3 + slab],
+            (place.dp, place.x), MESH,
+        )
+
+    def spread():
+        for slab in range(place.slabs):
+            pl.when(slab != place.a)(lambda slab=slab: chain(slab).start())
+
+    def collect():
+        for slab in range(place.slabs):
+
+            def wait(slab=slab):
+                chain(slab).wait_send()
+                arrival(slab).wait_recv()
+
+            pl.when(slab != place.a)(wait)
+        got[3 + place.a] = total[...]
+        value = got[3]
+        for slab in range(1, place.slabs):
+            value = value + got[3 + slab]
+        total[...] = value
+
+    names = "cxy"
+    steps.append([begin, functools.partial(open_, 0, "c")])
+    for k, name in enumerate(names):
+        then = functools.partial(open_, k + 1, names[k + 1]) if k < 2 else spread
+        steps.append([functools.partial(close, k, name), then])
+    steps.append([collect])
+    return [[(None, action) for action in step] for step in steps]
+
+
+def sum_kernel(slabs, tensor, groups, lag, count, *refs):
+    parts_in, small = refs[:count], refs[count]
+    outs, small_out = refs[count + 1 : 2 * count + 1], refs[2 * count + 1]
+    scratch = list(refs[2 * count + 2 :])
+    load_sem, send_sem, recv_sem, small_got, small_send, small_recv = scratch[:6]
+    scratch = scratch[6:]
+    place = Place(slabs)
+    place.greet(chain=True)
+    schedules, jobs, base = [], [], 0
+    for i, plane0, planes in groups:
+        rows, n = outs[i].shape[1:]
+        parts = parts_of(rows)
+        size = rows // parts
+        both = []
+        for p in range(parts):
+            names = sum_buffers(planes, slabs, size, n, tensor, ORDERS[p])
+            bufs = {name: scratch.pop(0) for name in names}
+            job = PartSum(
+                place, parts_in[i], outs[i].at[pl.ds(plane0, planes)],
+                pl.ds(plane0, planes), pl.ds(p * size, size), n, ORDERS[p], bufs,
+                (load_sem, send_sem, recv_sem), base,
+            )
+            base += 1
+            both.append(job.ticks())
+            jobs.append(job)
+        length = max(len(t) for t in both)
+        schedules.append([sum((t[k] for t in both if k < len(t)), []) for k in range(length)])
+    schedules.append(small_sum(place, small, small_out, small_got, (small_send, small_recv)))
+    merge(schedules, lag)
+    for job in jobs:
+        job.drain()
+
+
+def sum_all(partials, small, groups, dp, tensor, lag=2):
+    slabs = dp // 4
+    wide, outs = [], []
+    for part in partials:
+        planes, rows, cols = part.shape
+        wide.append(part.reshape(planes, slabs, 2, 2, rows // dp, cols))
+        outs.append(jax.ShapeDtypeStruct((planes, rows // dp, cols // tensor), jnp.float32))
+    scratch, bases = [], 0
+    for i, _, planes in groups:
+        rows, n = outs[i].shape[1:]
+        parts = parts_of(rows)
+        for p in range(parts):
+            shapes = sum_buffers(planes, slabs, rows // parts, n, tensor, ORDERS[p])
+            scratch += [pltpu.VMEM(shape, jnp.bfloat16) for shape in shapes.values()]
+            bases += 1
+    dma = pltpu.SemaphoreType.DMA
+    vmem = pl.BlockSpec(memory_space=pltpu.VMEM)
+    return pl.pallas_call(
+        functools.partial(sum_kernel, slabs, tensor, groups, lag, len(partials)),
+        out_shape=[*outs, jax.ShapeDtypeStruct(small.shape, jnp.float32)],
+        in_specs=[pl.BlockSpec(memory_space=pl.ANY)] * len(partials) + [vmem],
+        out_specs=[vmem] * (len(partials) + 1),
+        scratch_shapes=[
+            dma((bases, slabs)),
+            dma((bases, 4, slabs + 1)),
+            dma((bases, 4, slabs + 1)),
+            pltpu.VMEM((3 + slabs, *small.shape), jnp.float32),
+            dma((3 + slabs,)),
+            dma((3 + slabs,)),
+            *scratch,
+        ],
+        compiler_params=pltpu.CompilerParams(
+            collective_id=1, has_side_effects=True, vmem_limit_bytes=67043328
+        ),
+        name="sum_gradients",
+    )(*wide, small)
 
 
 def per_device(
@@ -248,11 +547,9 @@
     grad_out,
 ):
     inputs = tokens.astype(jnp.float32)
+    dp, tensor = lax.axis_size("dp"), lax.axis_size("tensor")
     in_full, out_full, gate_up_full, down_full = gather_all(
-        [in_weight, out_weight[None], gate_up_weight, down_weight[None]],
-        GROUPS,
-        lax.axis_size("dp"),
-        lax.axis_size("tensor"),
+        [in_weight, out_weight[None], gate_up_weight, down_weight[None]], GROUPS, dp, tensor
     )
     out_full, down_full = out_full[0], down_full[0]
     rows, width = tokens.shape
@@ -294,7 +591,6 @@
     down_grad = lax.dot_general(
         grad_out, hidden, (((0,), (0,)), ((), ())), preferred_element_type=jnp.float32
     )
-    down_sum = scatter_sum(down_grad, 1)
     silu_slope = sigmoid_gate * (1.0 + gate_pre * (1.0 - sigmoid_gate))
     gate_grad = (hidden_grad * up_value * silu_slope).astype(jnp.bfloat16)
     up_grad = (hidden_grad * silu_gate).astype(jnp.bfloat16)
@@ -302,7 +598,6 @@
     gate_up_weight_grad = jnp.einsum(
         "gd,jgf->jdf", normed_ff, gate_up_grad, preferred_element_type=jnp.float32
     )
-    gate_up_sum = scatter_sum(gate_up_weight_grad, 2)
     ffn_in_grad = jnp.einsum(
         "jgf,jdf->gd", gate_up_grad, gate_up_full, preferred_element_type=jnp.float32
     )
@@ -313,7 +608,6 @@
     out_weight_grad = lax.dot_general(
         mixer_grads, gated_rows, (((0,), (0,)), ((), ())), preferred_element_type=jnp.float32
     )
-    out_sum = scatter_sum(out_weight_grad, 1)
     output_gate_grad = gated_grad * conv_out
     conv_grad_in = gated_grad * output_gate
     mixed_grad = (
@@ -336,25 +630,36 @@
     in_weight_grad = jnp.einsum(
         "gd,jgc->jdc", normed_mix, proj_grad, preferred_element_type=jnp.float32
     )
-    in_sum = scatter_sum(in_weight_grad, 2)
     mixer_in_grad = jnp.einsum(
         "jgc,jdc->gd", proj_grad, in_full, preferred_element_type=jnp.float32
     )
     input_back, gain_mix_grad = norm_back(inputs, scale_mix, gain_mix, mixer_in_grad)
     input_grad = residual_grad + input_back
-    gain_mix_sum, gain_ff_sum, conv_sum = lax.psum(
-        (gain_mix_grad, gain_ff_grad, tap_grads), ("dp", "tensor")
+    small = jnp.concatenate(
+        [gain_mix_grad[None], gain_ff_grad[None], tap_grads, jnp.zeros((3, width), jnp.float32)]
+    )
+    down_sum, gate_up_sum, in_sum, out_sum, small_sums = sum_all(
+        [
+            down_grad.astype(jnp.bfloat16)[None],
+            gate_up_weight_grad.astype(jnp.bfloat16),
+            in_weight_grad.astype(jnp.bfloat16),
+            out_weight_grad.astype(jnp.bfloat16)[None],
+        ],
+        small,
+        SUM_GROUPS,
+        dp,
+        tensor,
     )
     return (
         block_out,
         input_grad,
-        gain_mix_sum,
+        small_sums[0],
         in_sum,
-        conv_sum,
-        out_sum,
-        gain_ff_sum,
+        small_sums[2:5],
+        out_sum[0],
+        small_sums[1],
         gate_up_sum,
-        down_sum,
+        down_sum[0],
     )
 
 

time: 1060 us -> 575 us (0.54)
  waiting for transfers between devices: 497 us -> 0 us
  Pallas kernels: 145 us -> 302 us
  local copies, waits for them, and re-layouts: 109 us -> 34.5 us
  blocking collectives: 40.7 us -> 0 us
  between operations: 14.8 us -> 1.49 us
    unnamed x20 -> x0, waiting for transfers between devices: 368 us -> none
    pallas_call x0 -> x1, Pallas kernels: none -> 157 us  [sum_all(): pl.pallas_call(functools.partial(sum_kernel, slabs, tensor, groups, lag,...]
    reduce_scatter x8 -> x0, waiting for transfers between devices: 129 us -> none  [the longest x7 66.4 us: scatter_sum(): lax.psum_scatter(part, 'tensor', scatter_dimension=col_axis, tiled=True)]
    unnamed x93 -> x74, local copies, waits for them, and re-layouts: 89.8 us -> 29.3 us
    psum x1 -> x0, blocking collectives: 40.7 us -> none  [per_device(): lax.psum((gain_mix_grad, gain_ff_grad, tap_grads), ('dp', 'tensor'))]
    convert_element_type x2 -> x0, local copies, waits for them, and re-layouts: 17.8 us -> none  [scatter_sum(): partial.astype(jnp.bfloat16)]
  transfers between devices with their start and end apart: 14 -> 0, of which waited for: 9 -> 0; matrix products, arithmetic and copies ran while one was open for 18% -> 0% of each run, Pallas kernels for 0% -> 0%
where the time goes in v3:
time: 575 us; the launch traced here: 568 us
  Pallas kernels  302 us (53%)
  matrix products  207 us (36%)
  local copies, waits for them, and re-layouts  34.5 us (6%)
  other arithmetic  22.1 us (4%)
    pallas_call x1, Pallas kernels, sum_all(): pl.pallas_call(functools.partial(sum_kernel, slabs, tensor, groups, lag,...  157 us
    pallas_call x1, Pallas kernels, gather_all(): pl.pallas_call(functools.partial(gather_kernel, slabs, {'shapes': shapes,...  145 us
    dot_general x1, matrix products, per_device(): jnp.einsum('jgf,jdf->gd', gate_up_grad, gate_up_full, preferred_element_t...  30.5 us
    unnamed x74, local copies, waits for them, and re-layouts  29.3 us
    dot_general x1, matrix products, per_device(): jnp.einsum('gd,jdf->jgf', normed_ff, gate_up_full, preferred_element_type...  29 us
    dot_general x1, matrix products, per_device(): jnp.dot(grad_out, down_full, preferred_element_type=jnp.float32)  27.5 us
    dot_general x1, matrix products, per_device(): jnp.einsum('gd,jgf->jdf', normed_ff, gate_up_grad, preferred_element_type...  27 us
    dot_general x1, matrix products, per_device(): lax.dot_general(hidden, down_full, (((1,), (1,)), ((), ())), preferred_el...  23.7 us

profile of v3, /device:TPU:0, one launch (start us, length us, event | category | flops | bytes accessed | tf_op | source)
XLA Modules:
  0.0 567.6 jit_solution(2090376982338465916)
XLA Ops:
  0.6 0.0 copy-start.28
  0.7 145.1 %gather_weights.1 = (bf16[3,4,2,2,64,1024]{5,4,3,2,1,0:T(8,128)(2,1)}, bf16[1,4,2,2,64,1024]{5,4,3,2,1,0:T(8,128)(2,1)}, bf16[2,4,2,2,64,4608]{5,4,3,2,1,0:T(8,128)(2,1)}, bf16[1,4,2,2,64,4608]{5,4,3,2,1,0:T(8,128)(2,1)}) custom-call(bf16[3,64,512]{2,1,0:T(8,128)(2,1)} %refs_0_.1, bf16[1,64,512]{2,1,0:T(8,128)(2,1)} %bitcast.158, ...), custom_call_target="tpu_custom_call" | custom-call | tf_op jit(solution)/shard_map/gather_weights/pallas_call | solution.py:227
  145.7 3.1 copy.18
  148.8 0.0 copy-start.5
  148.8 0.5 fusion.15
  149.3 0.8 multiply_multiply_fusion
  150.1 0.0 copy-done.28
  150.1 10.5 %convolution_bitcast_fusion.1 = f32[3,1024,1024]{2,1,0:T(8,128)S(1)} fusion(bf16[3,1024,1024]{2,1,0:T(8,128)(2,1)} %bitcast.176, bf16[1024,1024]{0,1:T(8,128)(2,1)S(1)} %copy.18, f32[1024]{0:T(1024)S(1)} %copy-done.28, f32[1024]{0:T(1024)S(1)} %get-tuple-element.57), kind=kOutput, calls=%fused_computation.32 | convolution fusion | flops 6446645248 | bytes 20979712 | tf_op jit(solution)/shard_map/gd,jdc->jgc/dot_general | solution.py:559
  160.6 0.0 copy-start.16
  160.6 0.0 copy-start.18
  160.6 0.0 copy-start.20
  160.7 1.4 slice_multiply_fusion
  162.0 0.0 copy-start
  162.0 3.6 copy-done.2
  165.6 0.0 copy-done.16
  165.6 4.3 fusion.28
  169.9 0.0 copy-done
  169.9 0.0 copy-done.5
  169.9 0.0 copy-start.27
  169.9 2.5 multiply_reduce_fusion.4
  172.4 0.7 multiply_multiply_fusion.1
  173.0 1.3 copy-done.8
  174.3 29.0 %convolution_bitcast_fusion = f32[2,1024,4608]{1,2,0:T(8,128)} fusion(bf16[2,1024,4608]{2,1,0:T(8,128)(2,1)} %bitcast.172, f32[1024,1024]{0,1:T(8,128)S(1)} %get-tuple-element.61, f32[1024]{0:T(1024)S(1)} %copy-done.27, f32[1024]{0:T(1024)S(1)} %get-tuple-element.59), kind=kOutput, calls=%fused_computation.17 | convolution fusion | flops 19330498560 | bytes 60825600 | tf_op jit(solution)/shard_map/gd,jdf->jgf/dot_general | solution.py:576
  203.4 23.7 %add_convert_fusion = bf16[1024,1024]{0,1:T(8,128)(2,1)} fusion(f32[1024,1024]{0,1:T(8,128)} %copy-done.8, bf16[1024,4608]{1,0:T(8,128)(2,1)} %bitcast.174, f32[2,1024,4608]{1,2,0:T(8,128)} %convolution_bitcast_fusion), kind=kOutput, calls=%fused_computation.58 | convolution fusion | flops 9694085120 | bytes 53477376 | tf_op jit(solution)/shard_map/dot_general | solution.py:586
  227.0 4.2 copy.30
  231.2 2.5 copy.23
  233.8 27.5 %fusion.14 = (bf16[1,1024,4608]{1,2,0:T(8,128)(2,1)}, bf16[1,1024,4608]{1,2,0:T(8,128)(2,1)}) fusion(f32[2,1024,4608]{1,2,0:T(8,128)} %convolution_bitcast_fusion, bf16[1024,4608]{1,0:T(8,128)(2,1)} %bitcast.175, bf16[1024,1024]{1,0:T(8,128)(2,1)S(1)} %copy-done.13), kind=kOutput, calls=%fused_computation.30 | convolution fusion | flops 9725018112 | bytes 68157440 | tf_op jit(solution)/shard_map/dot_general | solution.py:590
  261.2 0.0 copy-start.25
  261.2 30.5 %fusion.26 = (f32[1024]{0:T(1024)S(1)}, f32[1024]{0:T(1024)S(1)}, f32[1024,1024,1]{0,1,2:T(8,128)}) fusion(f32[1024,1024]{0,1:T(8,128)} %copy-done.8, f32[1024]{0:T(1024)S(1)} %get-tuple-element.59, f32[1024]{0:T(1024)S(1)} %copy-done.27, bf16[2,1024,4608]{2,1,0:T(8,128)(2,1)} %bitcast.173, bf16[1,1024,4608]{1,2,0:T(8,128)(2,1)} %get-tuple-element.49, ...), kind=kOutput, calls=%fused_computation.49 | convolution fusion | flops 19343081472 | bytes 46153728 | tf_op jit(solution)/shard_map/jgf,jdf->gd/dot_general | solution.py:601
  291.7 0.0 copy-done.9
  291.7 0.0 copy-done.25
  291.7 0.0 copy-start.1
  291.7 0.0 slice-start
  291.7 5.3 subtract_add_fusion
  297.0 10.9 %multiply_reduce_fusion = (f32[1024]{0:T(1024)S(1)}, f32[1024]{0:T(1024)S(1)}, f32[1024]{0:T(1024)S(1)}, f32[1,1024,1024]{2,1,0:T(8,128)S(1)}, bf16[1,1024,1024]{2,1,0:T(8,128)(2,1)}) fusion(f32[1,1024,1024]{2,1,0:T(8,128)S(1)} %copy-done.1, f32[1,1023,1024]{2,1,0:T(8,128)S(1)} %bitcast.145, f32[1,1022,1024]{2,1,0:T(8,128)S(1)} %bitcast.146, ...), kind=kOutput, calls=%fused_computation.50 | convolution fusion | flops 2157966336 | bytes 33554432 | tf_op jit(solution)/shard_map/dot_general | solution.py:607
  307.9 0.9 slice.73
  308.8 0.0 copy-start.17
  308.8 0.0 copy-start.19
  308.8 0.0 copy-start.21
  308.9 0.9 slice.72
  309.8 4.1 multiply_convert_fusion.3
  314.0 0.0 copy-start.23
  314.0 0.0 copy-start.29
  314.0 2.1 multiply_convert_fusion.2
  316.1 0.0 copy-done.6
  316.1 0.9 copy-done.11
  317.0 0.6 copy-done.12
  317.6 0.0 copy-done.29
  317.6 10.6 %fusion.23 = (f32[1024]{0:T(1024)S(1)}, f32[1024]{0:T(1024)S(1)}, f32[1024,1024,1]{0,1,2:T(8,128)S(1)}) fusion(bf16[1024,1024]{0,1:T(8,128)(2,1)S(1)} %copy-done.6, f32[1024]{0:T(1024)S(1)} %copy-done.23, f32[1024]{0:T(1024)S(1)} %copy-done.29, bf16[3,1024,1024]{2,1,0:T(8,128)(2,1)} %bitcast.177, bf16[1,1024,1024]{2,1,0:T(8,128)(2,1)} %multiply_convert_fusion.2, ...), kind=kOutput, calls=%fused_computation.41 | convolution fusion | flops 6456080384 | bytes 18890752 | tf_op jit(solution)/shard_map/jgc,jdc->gd/dot_general | solution.py:633
  328.3 3.0 fusion.20
  331.3 5.3 copy.31
  336.6 20.9 %convolution_convert_fusion.1 = bf16[4608,1024]{0,1:T(8,128)(2,1)} fusion(bf16[1024,1024]{1,0:T(8,128)(2,1)} %param.17, f32[2,1024,4608]{1,2,0:T(8,128)} %convolution_bitcast_fusion), kind=kOutput, calls=%fused_computation.20 | convolution fusion | flops 9696706560 | bytes 49283072 | tf_op jit(solution)/shard_map/dot_general | solution.py:591
  357.6 27.0 %convolution_convert_fusion = bf16[2,4608,1024]{1,2,0:T(8,128)(2,1)} fusion(bf16[1,1024,4608]{1,2,0:T(8,128)(2,1)} %get-tuple-element.49, bf16[1,1024,4608]{1,2,0:T(8,128)(2,1)} %get-tuple-element.48, f32[1024,1024]{0,1:T(8,128)} %copy-done.8, f32[1024]{0:T(1024)S(1)} %copy-done.27, f32[1024]{0:T(1024)S(1)} %get-tuple-element.59), kind=kOutput, calls=%fused_computation.18 | convolution fusion | flops 19349372928 | bytes 41951232 | tf_op jit(solution)/shard_map/gd,jgf->jdf/dot_general | solution.py:598
  384.6 10.7 %convolution_convert_fusion.2 = bf16[3,1024,1024]{1,2,0:T(8,128)(2,1)} fusion(bf16[1,1024,1024]{2,1,0:T(8,128)(2,1)} %multiply_convert_fusion.2, bf16[1,1024,1024]{2,1,0:T(8,128)(2,1)} %get-tuple-element.50, bf16[1,1024,1024]{2,1,0:T(8,128)(2,1)} %get-tuple-element.44, bf16[1024,1024]{0,1:T(8,128)(2,1)S(1)} %copy-done.6, f32[1024]{0:T(1024)S(1)} %copy-done.29, ...), kind=kOutput, calls=%fused_computation.64 | convolution fusion | flops 6468665344 | bytes 14688256 | tf_op jit(solution)/shard_map/gd,jgc->jdc/dot_general | solution.py:630
  395.2 0.0 copy-done.15
  395.2 3.7 convolution_convert_fusion.3
  399.0 0.7 concatenate.7.refs_4_
  399.6 157.1 %sum_gradients.1 = (f32[1,64,2304]{2,1,0:T(8,128)}, f32[2,64,2304]{2,1,0:T(8,128)}, f32[3,64,512]{2,1,0:T(8,128)}, f32[1,64,512]{2,1,0:T(8,128)}, f32[8,1024]{1,0:T(8,128)}) custom-call(bf16[1,4,2,2,64,4608]{5,4,3,2,1,0:T(8,128)(2,1)} %bitcast.150, bf16[2,4,2,2,64,4608]{5,4,3,2,1,0:T(8,128)(2,1)} %bitcast.149, bf16[3,4,2,2,64,1024]{5,4,3,2,1,0:T(8,128)(2,1)} %bitcast.151, ...), custom_call_target="tpu_custom_call" | custom-call | tf_op jit(solution)/shard_map/sum_gradients/pallas_call | solution.py:517
  556.8 1.4 fusion.46
  558.2 1.4 slice.63
  559.6 1.8 copy.50
  561.3 1.6 copy.51
  562.9 2.4 copy.52
  565.3 1.9 copy.53
  (43 shorter events, 0.1 us)
Async XLA Ops:
  0.6 149.5 %copy-start.28 = (f32[1024]{0:T(1024)S(1)}, f32[1024]{0:T(1024)}, u32[]{:S(2)}) copy-start(f32[1024]{0:T(1024)} %param.10) | copy-start | bytes 12292
  148.8 21.1 %copy-start.5 = (bf16[1024,1024]{0,1:T(8,128)(2,1)}, bf16[1024,1024]{0,1:T(8,128)(2,1)S(1)}, u32[]{:S(2)}) copy-start(bf16[1024,1024]{0,1:T(8,128)(2,1)S(1)} %copy.18) | copy-start | bytes 6291460
  150.1 10.5 %copy-start.22 = (f32[1024]{0:T(1024)}, f32[1024]{0:T(1024)S(1)}, u32[]{:S(2)}) copy-start(f32[1024]{0:T(1024)S(1)} %get-tuple-element.57) | copy-start | bytes 12292
  150.1 10.5 %copy-start.26 = (f32[3,1024]{1,0:T(4,128)S(1)}, f32[3,1024]{1,0:T(4,128)}, u32[]{:S(2)}) copy-start(f32[3,1024]{1,0:T(4,128)} %param.12) | copy-start | bytes 36868
  160.6 5.0 copy-start.2
  160.6 5.0 copy-start.16
  160.6 5.0 copy-start.18
  160.6 5.0 copy-start.20
  162.0 7.8 %copy-start = (f32[1,1024,1024]{2,1,0:T(8,128)}, f32[1,1024,1024]{2,1,0:T(8,128)S(1)}, u32[]{:S(2)}) copy-start(f32[1,1024,1024]{2,1,0:T(8,128)S(1)} %slice_multiply_fusion) | copy-start | bytes 12582916
  165.6 4.3 copy-start.10
  169.9 2.5 copy-start.14
  169.9 4.4 copy-start.27
  172.4 2.0 copy-start.8
  227.0 4.2 copy-start.13
  261.2 30.5 %copy-start.7 = (bf16[1024,1024]{0,1:T(8,128)(2,1)S(1)}, bf16[1024,1024]{0,1:T(8,128)(2,1)}, u32[]{:S(2)}) copy-start(bf16[1024,1024]{0,1:T(8,128)(2,1)} %copy.23) | copy-start | bytes 6291460
  261.2 30.5 %copy-start.9 = (f32[1024,1024]{0,1:T(8,128)S(1)}, f32[1024,1024]{0,1:T(8,128)}, u32[]{:S(2)}) copy-start(f32[1024,1024]{0,1:T(8,128)} %copy-done.8) | copy-start | bytes 12582916
  261.2 30.5 %copy-start.25 = (f32[1024]{0:T(1024)S(1)}, f32[1024]{0:T(1024)}, u32[]{:S(2)}) copy-start(f32[1024]{0:T(1024)} %get-tuple-element.58) | copy-start | bytes 12292
  291.7 5.3 copy-start.1
  291.7 18.0 %slice-start = ((s8[12582912]{0:T(1024)(128)(4,1)}), s8[4194304]{0:T(1024)(128)(4,1)S(1)}, s32[]{:S(2)}) async-start(s8[12582912]{0:T(1024)(128)(4,1)} %bitcast.147), calls=%async_computation | async-start | bytes 8388608
  297.0 12.7 %slice-start.1 = ((s8[12582912]{0:T(1024)(128)(4,1)}), s8[4194304]{0:T(1024)(128)(4,1)S(1)}, s32[]{:S(2)}) async-start(s8[12582912]{0:T(1024)(128)(4,1)} %bitcast.147), calls=%async_computation.1 | async-start | bytes 8388608
  297.0 12.7 %slice-start.2 = ((s8[12582912]{0:T(1024)(128)(4,1)}), s8[4194304]{0:T(1024)(128)(4,1)S(1)}, s32[]{:S(2)}) async-start(s8[12582912]{0:T(1024)(128)(4,1)} %bitcast.147), calls=%async_computation.2 | async-start | bytes 8388608
  308.8 1.0 copy-start.17
  308.8 1.0 copy-start.19
  308.8 1.0 copy-start.21
  314.0 2.1 copy-start.6
  314.0 3.0 copy-start.11
  314.0 3.6 copy-start.12
  314.0 3.6 copy-start.23
  314.0 3.6 copy-start.29
  317.6 10.7 %copy-start.3 = (f32[1024,1024]{0,1:T(8,128)S(1)}, f32[1024,1024]{0,1:T(8,128)}, u32[]{:S(2)}) copy-start(f32[1024,1024]{0,1:T(8,128)} %subtract_add_fusion) | copy-start | bytes 12582916
  317.6 10.7 %copy-start.24 = (f32[1024]{0:T(1024)S(1)}, f32[1024]{0:T(1024)}, u32[]{:S(2)}) copy-start(f32[1024]{0:T(1024)} %get-tuple-element.56) | copy-start | bytes 12292
  384.6 10.7 %copy-start.4 = (f32[1024,1024]{0,1:T(8,128)S(1)}, f32[1024,1024]{0,1:T(8,128)}, u32[]{:S(2)}) copy-start(f32[1024,1024]{0,1:T(8,128)} %subtract_add_fusion) | copy-start | bytes 12582916
  384.6 10.7 %copy-start.15 = (bf16[1024,1024]{1,0:T(8,128)(2,1)S(1)}, bf16[1024,1024]{1,0:T(8,128)(2,1)}, u32[]{:S(2)}) copy-start(bf16[1024,1024]{1,0:T(8,128)(2,1)} %copy-done.14) | copy-start | bytes 6291460

commit v4 on v3

--- a/solution.py
+++ b/solution.py
@@ -37,6 +37,7 @@
 ORDERS = ("xzy", "yzx", "zxy", "zyx")
 GROUPS = ((0, 0, 3), (1, 0, 1), (2, 0, 1), (2, 1, 1), (3, 0, 1))
 SUM_GROUPS = ((0, 0, 1), (1, 0, 1), (1, 1, 1), (2, 0, 3), (3, 0, 1))
+PRODUCTS = ((0, 0, 0, 0), (1, 1, 1, 0), (1, 2, 1, 1), (2, 3, 2, 0), (3, 4, 3, 0))
 STAGES = {"x": 0, "y": 1, "z": 2, "c": 3}
 
 
@@ -241,25 +242,16 @@
 
 
 def add_into(target, extra):
-    rows, cols = target.shape[-2:]
-    step = next(w for w in (1152, 1024, 512, 256, 128) if cols % w == 0)
     lead = target.shape[:-2]
     count = 1
     for d in lead:
         count *= d
-
-    def body(i, carry):
+    for k in range(count):
         at = []
-        k = i // (cols // step)
         for d in reversed(lead):
             at.insert(0, k % d)
             k = k // d
-        where = (*at, slice(None), pl.ds(pl.multiple_of((i % (cols // step)) * step, 128), step))
-        total = target[where].astype(jnp.float32) + extra[where].astype(jnp.float32)
-        target[where] = total.astype(target.dtype)
-        return carry
-
-    lax.fori_loop(0, count * (cols // step), body, 0)
+        target[tuple(at)] = target[tuple(at)] + extra[tuple(at)]
 
 
 class PartSum:
@@ -535,6 +527,251 @@
     )(*wide, small)
 
 
+TILE = 512
+AHEAD = 3
+
+
+def far_first(place):
+    slabs = place.slabs
+    tables = []
+    for a in range(slabs):
+        tables.append(sorted(range(slabs), key=lambda k: (-abs(k - a), -k)))
+    return [
+        sum(jnp.where(place.a == a, tables[a][i], 0) for a in range(slabs)) for i in range(slabs)
+    ]
+
+
+class TilePart(PartSum):
+    def ticks(self, order_of_slabs):
+        place, order = self.place, self.order
+        zi = order.index("z")
+        after = "".join(reversed(order[zi + 1 :]))
+        before = "".join(reversed(order[:zi]))
+        slabs = place.slabs
+        ticks = {}
+        bind = functools.partial
+
+        def put(t, unit, cond, action):
+            ticks.setdefault(t, []).append((unit, cond, action))
+
+        def begin(stage, slab):
+            self.sends.append((None, stage, slab, None))
+            return bind(self.start, stage, slab)
+
+        for i, slab in enumerate(order_of_slabs):
+            t = i + 1
+            for stage in after:
+                put(t, i, None, begin(stage, slab))
+                put(t + 1, i, None, bind(self.take, stage, slab))
+                t += 1
+            if i < slabs - 1:
+                up, down = slab > place.a, slab < place.a
+                from_both = jnp.logical_or(
+                    jnp.logical_and(up, place.has["down"]), jnp.logical_and(down, place.has["up"])
+                )
+                put(t, i, from_both, bind(self.take_z, slab, slab))
+                for cond, to in ((up, "up"), (down, "down")):
+                    put(t, i, cond, bind(self.send_z, slab, to))
+                    self.sends.append((cond, "z", slab, to))
+                continue
+            put(t, i, place.has["down"], bind(self.take_z, slab, slab))
+            put(t, i, place.has["up"], bind(self.take_z, slab, slabs))
+            for stage in before:
+                put(t, i, None, begin(stage, slab))
+                put(t + 1, i, None, bind(self.take, stage, slab))
+                t += 1
+            put(t, i, None, self.finish)
+        return ticks
+
+
+def tile_sum_kernel(slabs, tensor, groups, a_count, b_count, out_count, *refs):
+    lefts, refs = refs[:a_count], refs[a_count:]
+    rights, refs = refs[:b_count], refs[b_count:]
+    small, refs = refs[0], refs[1:]
+    outs, small_out, refs = refs[:out_count], refs[out_count], refs[out_count + 1 :]
+    send_sem, recv_sem, core_send, core_recv, small_got, small_send, small_recv = refs[:7]
+    left_buf, left_sem, turned, right_buf, right_sem = refs[7:12]
+    scratch = list(refs[12:])
+    place = Place(slabs)
+    place.greet(chain=True)
+    sigma = far_first(place)
+    units = [(g, i) for g in range(len(groups)) for i in range(slabs)]
+    block = 4 * outs[0].shape[1]
+
+    def left_copy(u):
+        g, i = units[u]
+        at = pl.ds(pl.multiple_of(sigma[i] * block, 128), block)
+        return pltpu.make_async_copy(
+            lefts[groups[g][0]].at[:, at], left_buf.at[u % 2], left_sem.at[u % 2]
+        )
+
+    def right_copy(g, k):
+        right = rights[groups[g][1]]
+        wide = right.shape[2] // TILE
+        at = pl.ds(pl.multiple_of((k % wide) * TILE, TILE), TILE)
+        slot = k % (AHEAD + 1)
+        return pltpu.make_async_copy(
+            right.at[k // wide, :, at], right_buf.at[slot], right_sem.at[slot]
+        )
+
+    def multiply(u, tile):
+        g = units[u][0]
+        right = rights[groups[g][1]]
+        wide = right.shape[2] // TILE
+        steps = right.shape[0] * wide
+        left_copy(u).wait()
+        if u + 1 < len(units):
+            left_copy(u + 1).start()
+        turned[...] = left_buf[u % 2].T
+
+        def body(k, carry):
+            right_copy(g, k).wait()
+
+            @pl.when(k + AHEAD < steps)
+            def _():
+                right_copy(g, k + AHEAD).start()
+
+            product = jnp.dot(
+                turned[...], right_buf[k % (AHEAD + 1)], preferred_element_type=jnp.float32
+            )
+            at = pl.ds(pl.multiple_of((k % wide) * TILE, TILE), TILE)
+            tile[k // wide, :, :, :, at] = product.reshape(2, 2, block // 4, TILE).astype(
+                tile.dtype
+            )
+            return carry
+
+        lax.fori_loop(0, steps, body, 0)
+        if u + 1 < len(units):
+            preload(u + 1)
+
+    def preload(u):
+        g = units[u][0]
+        right = rights[groups[g][1]]
+        for k in range(min(AHEAD, right.shape[0] * (right.shape[2] // TILE))):
+            right_copy(g, k).start()
+
+    schedule, jobs, base = {}, [], 0
+    tiles = {}
+
+    def put(t, rank, cond, action):
+        schedule.setdefault(t, []).append((rank, cond, action))
+
+    for g, (_, ri, oi, plane0) in enumerate(groups):
+        rows, n = outs[oi].shape[1:]
+        planes = rights[ri].shape[0]
+        key = (planes, n)
+        if key not in tiles:
+            tiles[key] = scratch.pop(0)
+        acc = scratch.pop(0)
+        tile_pair = tiles[key]
+        parts = parts_of(rows)
+        size = rows // parts
+
+        def core_copy(u, g=g, acc=acc, tile_pair=tile_pair):
+            slab = sigma[units[u][1]]
+            return pltpu.make_async_remote_copy(
+                tile_pair.at[u % 2, :, :, 1 - place.c],
+                acc.at[:, slab],
+                core_send.at[g, slab],
+                core_recv.at[g, slab],
+                place.peer["c"],
+                MESH,
+            )
+
+        def make(u, tile_pair=tile_pair, core_copy=core_copy):
+            multiply(u, tile_pair.at[u % 2])
+            core_copy(u).start()
+
+        def join(u, acc=acc, tile_pair=tile_pair, core_copy=core_copy):
+            copy = core_copy(u)
+            copy.wait_send()
+            copy.wait_recv()
+            add_into(
+                acc.at[:, sigma[units[u][1]]], tile_pair.at[u % 2, :, :, place.c]
+            )
+
+        for i in range(slabs):
+            u = g * slabs + i
+            put(u, (1, 0), None, functools.partial(make, u))
+            put(u + 1, (0, 0), None, functools.partial(join, u))
+        for p in range(parts):
+            shapes = sum_buffers(planes, slabs, size, n, tensor, ORDERS[p])
+            bufs = {name: scratch.pop(0) for name in "xyz"}
+            bufs["acc"] = acc.at[:, :, :, pl.ds(p * size, size)]
+            job = TilePart(
+                place, None, outs[oi].at[pl.ds(plane0, planes)], None, pl.ds(p * size, size), n,
+                ORDERS[p], bufs, (None, send_sem, recv_sem), base,
+            )
+            base += 1
+            jobs.append(job)
+            for t, actions in job.ticks(sigma).items():
+                for k, (i, cond, action) in enumerate(actions):
+                    u = g * slabs + i
+                    first = t == i + 1 and getattr(action, "func", None) == job.start
+                    rank = (0, 1 + p) if first else (2, -u)
+                    put(g * slabs + t, rank, cond, action)
+    for t, actions in enumerate(small_sum(place, small, small_out, small_got, (small_send, small_recv))):
+        for cond, action in actions:
+            put(t + 1, (3, 0), cond, action)
+    left_copy(0).start()
+    preload(0)
+    for t in sorted(schedule):
+        for _, cond, action in sorted(schedule[t], key=lambda item: item[0]):
+            when(cond, action)
+    for job in jobs:
+        job.drain()
+
+
+def tile_sum_all(lefts, rights, outs, groups, small, dp, tensor):
+    slabs = dp // 4
+    bf = jnp.bfloat16
+    seen, scratch, bases = set(), [], 0
+    for _, ri, oi, _ in groups:
+        planes = rights[ri].shape[0]
+        rows, n = outs[oi].shape[1:]
+        cols = n * tensor
+        if (planes, n) not in seen:
+            seen.add((planes, n))
+            scratch.append(pltpu.VMEM((2, planes, 2, 2, rows, cols), bf))
+        scratch.append(pltpu.VMEM((planes, slabs, 2, rows, cols), bf))
+        parts = parts_of(rows)
+        for p in range(parts):
+            shapes = sum_buffers(planes, slabs, rows // parts, n, tensor, ORDERS[p])
+            scratch += [pltpu.VMEM(shapes[name], bf) for name in "xyz"]
+            bases += 1
+    dma = pltpu.SemaphoreType.DMA
+    vmem = pl.BlockSpec(memory_space=pltpu.VMEM)
+    depth = lefts[0].shape[0]
+    block = 4 * outs[0].shape[1]
+    return pl.pallas_call(
+        functools.partial(
+            tile_sum_kernel, slabs, tensor, groups, len(lefts), len(rights), len(outs)
+        ),
+        out_shape=[*outs, jax.ShapeDtypeStruct(small.shape, jnp.float32)],
+        in_specs=[pl.BlockSpec(memory_space=pl.ANY)] * (len(lefts) + len(rights)) + [vmem],
+        out_specs=[vmem] * (len(outs) + 1),
+        scratch_shapes=[
+            dma((bases, 4, slabs + 1)),
+            dma((bases, 4, slabs + 1)),
+            dma((len(groups), slabs)),
+            dma((len(groups), slabs)),
+            pltpu.VMEM((3 + slabs, *small.shape), jnp.float32),
+            dma((3 + slabs,)),
+            dma((3 + slabs,)),
+            pltpu.VMEM((2, depth, block), bf),
+            dma((2,)),
+            pltpu.VMEM((block, depth), bf),
+            pltpu.VMEM((AHEAD + 1, depth, TILE), bf),
+            dma((AHEAD + 1,)),
+            *scratch,
+        ],
+        compiler_params=pltpu.CompilerParams(
+            collective_id=2, has_side_effects=True, vmem_limit_bytes=67043328
+        ),
+        name="sum_products",
+    )(*lefts, *rights, small)
+
+
 def per_device(
     tokens,
     gain_mix,
@@ -588,16 +825,10 @@
         )
     ).astype(jnp.bfloat16)
     hidden_grad = jnp.dot(grad_out, down_full, preferred_element_type=jnp.float32)
-    down_grad = lax.dot_general(
-        grad_out, hidden, (((0,), (0,)), ((), ())), preferred_element_type=jnp.float32
-    )
     silu_slope = sigmoid_gate * (1.0 + gate_pre * (1.0 - sigmoid_gate))
     gate_grad = (hidden_grad * up_value * silu_slope).astype(jnp.bfloat16)
     up_grad = (hidden_grad * silu_gate).astype(jnp.bfloat16)
     gate_up_grad = jnp.stack([gate_grad, up_grad])
-    gate_up_weight_grad = jnp.einsum(
-        "gd,jgf->jdf", normed_ff, gate_up_grad, preferred_element_type=jnp.float32
-    )
     ffn_in_grad = jnp.einsum(
         "jgf,jdf->gd", gate_up_grad, gate_up_full, preferred_element_type=jnp.float32
     )
@@ -605,9 +836,6 @@
     residual_grad = grad_out.astype(jnp.float32) + residual_back
     mixer_grads = residual_grad.astype(jnp.bfloat16)
     gated_grad = jnp.dot(mixer_grads, out_full, preferred_element_type=jnp.float32).reshape(shaped)
-    out_weight_grad = lax.dot_general(
-        mixer_grads, gated_rows, (((0,), (0,)), ((), ())), preferred_element_type=jnp.float32
-    )
     output_gate_grad = gated_grad * conv_out
     conv_grad_in = gated_grad * output_gate
     mixed_grad = (
@@ -627,9 +855,6 @@
         .astype(jnp.bfloat16)
         .reshape(3, rows, width)
     )
-    in_weight_grad = jnp.einsum(
-        "gd,jgc->jdc", normed_mix, proj_grad, preferred_element_type=jnp.float32
-    )
     mixer_in_grad = jnp.einsum(
         "jgc,jdc->gd", proj_grad, in_full, preferred_element_type=jnp.float32
     )
@@ -638,18 +863,42 @@
     small = jnp.concatenate(
         [gain_mix_grad[None], gain_ff_grad[None], tap_grads, jnp.zeros((3, width), jnp.float32)]
     )
-    down_sum, gate_up_sum, in_sum, out_sum, small_sums = sum_all(
-        [
-            down_grad.astype(jnp.bfloat16)[None],
-            gate_up_weight_grad.astype(jnp.bfloat16),
-            in_weight_grad.astype(jnp.bfloat16),
-            out_weight_grad.astype(jnp.bfloat16)[None],
-        ],
-        small,
-        SUM_GROUPS,
-        dp,
-        tensor,
-    )
+    if in_weight.shape[1] >= 64:
+        shards = (down_weight[None], gate_up_weight, in_weight, out_weight[None])
+        down_sum, gate_up_sum, in_sum, out_sum, small_sums = tile_sum_all(
+            [grad_out, normed_ff, normed_mix, mixer_grads],
+            [hidden[None], gate_grad[None], up_grad[None], proj_grad, gated_rows[None]],
+            [jax.ShapeDtypeStruct(shard.shape, jnp.float32) for shard in shards],
+            PRODUCTS,
+            small,
+            dp,
+            tensor,
+        )
+    else:
+        down_grad = lax.dot_general(
+            grad_out, hidden, (((0,), (0,)), ((), ())), preferred_element_type=jnp.float32
+        )
+        gate_up_weight_grad = jnp.einsum(
+            "gd,jgf->jdf", normed_ff, gate_up_grad, preferred_element_type=jnp.float32
+        )
+        out_weight_grad = lax.dot_general(
+            mixer_grads, gated_rows, (((0,), (0,)), ((), ())), preferred_element_type=jnp.float32
+        )
+        in_weight_grad = jnp.einsum(
+            "gd,jgc->jdc", normed_mix, proj_grad, preferred_element_type=jnp.float32
+        )
+        down_sum, gate_up_sum, in_sum, out_sum, small_sums = sum_all(
+            [
+                down_grad.astype(jnp.bfloat16)[None],
+                gate_up_weight_grad.astype(jnp.bfloat16),
+                in_weight_grad.astype(jnp.bfloat16),
+                out_weight_grad.astype(jnp.bfloat16)[None],
+            ],
+            small,
+            SUM_GROUPS,
+            dp,
+            tensor,
+        )
     return (
         block_out,
         input_grad,

time: 575 us -> 540 us (0.939)
  matrix products: 207 us -> 136 us
  other arithmetic: 22.1 us -> 53.3 us
  Pallas kernels: 302 us -> 323 us
  local copies, waits for them, and re-layouts: 34.5 us -> 18.7 us
    dot_general x4 -> x0, matrix products: 62.3 us -> none  [the longest x1 27 us: per_device(): jnp.einsum('gd,jgf->jdf', normed_ff, gate_up_grad, preferred_element_type...]
    convert_element_type x0 -> x5, other arithmetic: none -> 29.8 us  [the longest x1 17.3 us: per_device(): hidden = (silu_gate * up_value).astype(jnp.bfloat16)]
    pallas_call x1, Pallas kernels: 157 us -> 178 us  [tile_sum_all(): pl.pallas_call(functools.partial(tile_sum_kernel, slabs, tensor, groups,...]
    unnamed x74 -> x56, local copies, waits for them, and re-layouts: 29.3 us -> 12.1 us
    dot_general x1, matrix products: 23.7 us -> 14.3 us  [per_device(): lax.dot_general(hidden, down_full, (((1,), (1,)), ((), ())), preferred_el...]
    another operation x2 -> x3, other arithmetic: 6.2 us -> 12.7 us  [the longest x1 6.5 us: per_device(): jnp.stack([mixed_grad * value_part, output_gate_grad, mixed_grad * input_...]
where the time goes in v4:
time: 540 us; the launch traced here: 532 us
  Pallas kernels  323 us (60%)
  matrix products  136 us (25%)
  other arithmetic  53.3 us (10%)
  local copies, waits for them, and re-layouts  18.7 us (3%)
    pallas_call x1, Pallas kernels, tile_sum_all(): pl.pallas_call(functools.partial(tile_sum_kernel, slabs, tensor, groups,...  178 us
    pallas_call x1, Pallas kernels, gather_all(): pl.pallas_call(functools.partial(gather_kernel, slabs, {'shapes': shapes,...  145 us
    dot_general x1, matrix products, per_device(): jnp.dot(grad_out, down_full, preferred_element_type=jnp.float32)  31.9 us
    dot_general x1, matrix products, per_device(): jnp.einsum('gd,jdf->jgf', normed_ff, gate_up_full, preferred_element_type...  28.8 us
    dot_general x1, matrix products, per_device(): jnp.einsum('jgf,jdf->gd', gate_up_grad, gate_up_full, preferred_element_t...  26.7 us
    convert_element_type x1, other arithmetic, per_device(): hidden = (silu_gate * up_value).astype(jnp.bfloat16)  17.3 us
    dot_general x1, matrix products, per_device(): lax.dot_general(hidden, down_full, (((1,), (1,)), ((), ())), preferred_el...  14.3 us
    dot_general x1, matrix products, per_device(): jnp.einsum('jgc,jdc->gd', proj_grad, in_full, preferred_element_type=jnp....  12.2 us

profile of v4, /device:TPU:0, one launch (start us, length us, event | category | flops | bytes accessed | tf_op | source)
XLA Modules:
  0.0 532.4 jit_solution(4693009269305347626)
XLA Ops:
  0.6 0.0 copy-start.5
  0.7 145.2 %gather_weights.1 = (bf16[3,4,2,2,64,1024]{5,4,3,2,1,0:T(8,128)(2,1)}, bf16[1,4,2,2,64,1024]{5,4,3,2,1,0:T(8,128)(2,1)}, bf16[2,4,2,2,64,4608]{5,4,3,2,1,0:T(8,128)(2,1)}, bf16[1,4,2,2,64,4608]{5,4,3,2,1,0:T(8,128)(2,1)}) custom-call(bf16[3,64,512]{2,1,0:T(8,128)(2,1)} %refs_0_.2, bf16[1,64,512]{2,1,0:T(8,128)(2,1)} %bitcast.135, ...), custom_call_target="tpu_custom_call" | custom-call | tf_op jit(solution)/shard_map/gather_weights/pallas_call | solution.py:228
  145.9 2.1 fusion.17
  147.9 0.6 multiply_multiply_fusion
  148.6 0.6 copy-done.18
  149.1 0.0 copy-done.5
  149.1 1.2 fusion.19.refs_2_
  150.4 0.0 copy-start.7
  150.4 1.3 copy-done.7
  151.7 8.9 %convolution_bitcast_fusion.1 = f32[3,1024,1024]{2,1,0:T(8,128)S(1)} fusion(bf16[3,1024,1024]{2,1,0:T(8,128)(2,1)} %bitcast.153, bf16[1024,1024]{1,0:T(8,128)(2,1)S(1)} %fusion.19.refs_2_), kind=kOutput, calls=%fused_computation.30 | convolution fusion | flops 6442450944 | bytes 20971520 | tf_op jit(solution)/shard_map/gd,jdc->jgc/dot_general | solution.py:796
  160.6 0.0 copy-start.2
  160.6 0.0 copy-start.22
  160.6 1.4 slice_multiply_fusion
  162.0 0.0 copy-start
  162.0 0.0 copy-done.22
  162.0 3.6 copy-done.2
  165.6 4.2 multiply_convert_fusion.4
  169.8 0.0 copy-done
  169.8 0.0 copy-done.13
  169.9 4.4 multiply_reduce_fusion.4
  174.3 0.0 copy-done.12
  174.3 0.0 copy-done.20
  174.3 2.6 multiply_convert_fusion.3.refs_1_
  176.9 0.0 copy-start.8
  176.9 28.8 %convolution_bitcast_fusion = f32[2,1024,4608]{2,1,0:T(8,128)} fusion(bf16[2,1024,4608]{2,1,0:T(8,128)(2,1)} %bitcast.149, bf16[1024,1024]{1,0:T(8,128)(2,1)S(1)} %multiply_convert_fusion.3.refs_1_), kind=kOutput, calls=%fused_computation.18 | convolution fusion | flops 19327352832 | bytes 58720256 | tf_op jit(solution)/shard_map/gd,jdf->jgf/dot_general | solution.py:813
  205.7 0.0 copy-done.8
  205.7 31.9 %fusion.16 = (bf16[1,1024,4608]{2,1,0:T(8,128)(2,1)}, bf16[1,1024,4608]{2,1,0:T(8,128)(2,1)}) fusion(f32[2,1024,4608]{2,1,0:T(8,128)} %convolution_bitcast_fusion, bf16[1024,1024]{1,0:T(8,128)(2,1)} %refs_0_.3, bf16[1024,4608]{1,0:T(8,128)(2,1)} %bitcast.151), kind=kOutput, calls=%fused_computation.28 | convolution fusion | flops 9725018112 | bytes 68157440 | tf_op jit(solution)/shard_map/dot_general | solution.py:827
  237.6 26.7 %fusion.28 = (f32[1024]{0:T(1024)S(1)}, f32[1024]{0:T(1024)S(1)}, f32[1024,1024,1]{1,0,2:T(8,128)S(1)}) fusion(f32[1024,1024]{1,0:T(8,128)} %get-tuple-element.54, f32[1024]{0:T(1024)S(1)} %get-tuple-element.52, f32[1024]{0:T(1024)S(1)} %copy-done.20, bf16[2,1024,4608]{2,1,0:T(8,128)(2,1)} %bitcast.150, ...), kind=kOutput, calls=%fused_computation.47 | convolution fusion | flops 19343081472 | bytes 46153728 | tf_op jit(solution)/shard_map/jgf,jdf->gd/dot_general | solution.py:832
  264.3 0.0 copy-done.6
  264.3 0.0 copy-start.1
  264.3 4.3 fusion.39
  268.6 0.0 copy-done.1
  268.6 0.0 slice-start.1
  268.7 8.9 %multiply_reduce_fusion = (f32[1024]{0:T(1024)S(1)}, f32[1024]{0:T(1024)S(1)}, f32[1024]{0:T(1024)S(1)}, f32[1,1024,1024]{2,1,0:T(8,128)S(1)}, bf16[1,1024,1024]{2,1,0:T(8,128)(2,1)}) fusion(f32[1,1024,1024]{2,1,0:T(8,128)S(1)} %copy-done.1, f32[1,1023,1024]{2,1,0:T(8,128)S(1)} %bitcast.126, f32[1,1022,1024]{2,1,0:T(8,128)S(1)} %bitcast.127, ...), kind=kOutput, calls=%fused_computation.48 | convolution fusion | flops 2156917760 | bytes 31457280 | tf_op jit(solution)/shard_map/dot_general | solution.py:838
  277.5 0.0 copy-done.4
  277.5 0.5 slice.72
  278.0 2.6 slice.73
  280.6 0.0 slice-done
  280.6 0.0 slice-done.1
  280.6 0.0 slice-done.2
  280.6 5.0 multiply_convert_fusion.2
  285.7 1.2 multiply_convert_fusion.1
  286.8 0.0 copy-start.11
  286.8 0.4 copy-done.9
  287.3 0.8 copy-done.10
  288.1 0.0 copy-done.19
  288.1 0.0 copy-done.21
  288.1 12.2 %fusion.25 = (f32[1024]{0:T(1024)S(1)}, f32[1024]{0:T(1024)}, f32[1024,1024,1]{1,0,2:T(8,128)}) fusion(bf16[1024,1024]{1,0:T(8,128)(2,1)S(1)} %copy-done.5, f32[1024]{0:T(1024)S(1)} %copy-done.19, f32[1024]{0:T(1024)S(1)} %copy-done.21, bf16[3,1024,1024]{2,1,0:T(8,128)(2,1)} %bitcast.154, bf16[1,1024,1024]{2,1,0:T(8,128)(2,1)S(1)} %multiply_convert_fusion.1, ...), kind=kOutput, calls=%fused_computation.39 | convolution fusion | flops 6456080384 | bytes 18890752 | tf_op jit(solution)/shard_map/jgc,jdc->gd/dot_general | solution.py:858
  300.2 0.7 concatenate.7.refs_9_
  300.9 6.5 %pad_maximum_fusion.refs_7_ = bf16[3,1024,1024]{2,1,0:T(8,128)(2,1)} fusion(bf16[1,1024,1024]{2,1,0:T(8,128)(2,1)} %copy-done.11, bf16[1,1024,1024]{2,1,0:T(8,128)(2,1)} %get-tuple-element.43, bf16[1,1024,1024]{2,1,0:T(8,128)(2,1)} %get-tuple-element.35), kind=kLoop, calls=%fused_computation.29 | loop fusion | flops 6291456 | bytes 12582912 | tf_op jit(solution)/shard_map/stack | solution.py:854
  307.4 17.3 %multiply_convert_fusion.refs_4_ = bf16[1,1024,4608]{2,1,0:T(8,128)(2,1)} fusion(f32[2,1024,4608]{2,1,0:T(8,128)} %convolution_bitcast_fusion), kind=kLoop, calls=%fused_computation.17 | loop fusion | flops 28311552 | bytes 47185920 | tf_op jit(solution)/shard_map/convert_element_type | solution.py:820
  324.7 177.9 %sum_products.1 = (f32[1,64,2304]{2,1,0:T(8,128)}, f32[2,64,2304]{2,1,0:T(8,128)}, f32[3,64,512]{2,1,0:T(8,128)}, f32[1,64,512]{2,1,0:T(8,128)}, f32[8,1024]{1,0:T(8,128)}) custom-call(bf16[1024,1024]{1,0:T(8,128)(2,1)} %refs_0_.3, bf16[1024,1024]{1,0:T(8,128)(2,1)} %copy-done.8, bf16[1024,1024]{1,0:T(8,128)(2,1)} %copy-done.7, ...), custom_call_target="tpu_custom_call" | custom-call | tf_op jit(solution)/shard_map/sum_products/pallas_call | solution.py:746
  502.6 1.4 slice.63
  504.0 1.4 fusion.40
  505.4 0.7 broadcast_multiply_fusion
  506.1 6.2 %fusion.22 = f32[1024,1024]{1,0:T(8,128)} fusion(f32[1024,1024]{1,0:T(8,128)} %get-tuple-element.38, bf16[1024,1024]{1,0:T(8,128)(2,1)} %param.9, f32[1024,1024,1]{1,0,2:T(8,128)} %get-tuple-element.56, f32[1024]{0:T(1024)S(1)} %broadcast_multiply_fusion, f32[1024]{0:T(1024)} %get-tuple-element.49, f32[1024]{0:T(1024)} %param.10, f32[1024]{0:T(1024)} %copy-done.18), kind=kLoop, calls=%fused_computation.36 | loop fusion | flops 7340032 | bytes 14696448 | tf_op jit(solution)/shard_map/add | solution.py:862
  512.3 2.1 copy-done.3
  514.4 14.3 %add_convert_fusion = bf16[1024,1024]{1,0:T(8,128)(2,1)} fusion(f32[1024,1024]{1,0:T(8,128)} %get-tuple-element.54, bf16[1024,4608]{1,0:T(8,128)(2,1)} %bitcast.152, bf16[1,1024,4608]{2,1,0:T(8,128)(2,1)S(1)} %copy-done.3), kind=kOutput, calls=%fused_computation.56 | convolution fusion | flops 9665773568 | bytes 25165824 | tf_op jit(solution)/shard_map/dot_general | solution.py:823
  528.7 0.7 copy.30
  529.5 0.0 copy-done.17
  529.5 0.7 copy.31
  530.1 0.0 copy-done.14
  530.1 1.0 copy.32
  531.1 0.8 copy.33
  (25 shorter events, 0.1 us)
Async XLA Ops:
  0.6 148.5 %copy-start.5 = (bf16[1024,1024]{1,0:T(8,128)(2,1)S(1)}, bf16[1024,1024]{1,0:T(8,128)(2,1)}, u32[]{:S(2)}) copy-start(bf16[1024,1024]{1,0:T(8,128)(2,1)} %param.9) | copy-start | bytes 6291460
  148.5 0.6 copy-start.18
  150.4 1.3 copy-start.7
  160.6 5.0 copy-start.2
  160.6 1.4 copy-start.22
  162.0 7.8 %copy-start = (f32[1,1024,1024]{2,1,0:T(8,128)}, f32[1,1024,1024]{2,1,0:T(8,128)S(1)}, u32[]{:S(2)}) copy-start(f32[1,1024,1024]{2,1,0:T(8,128)S(1)} %slice_multiply_fusion) | copy-start | bytes 12582916
  165.6 4.2 copy-start.13
  169.8 4.4 copy-start.12
  169.8 4.4 copy-start.20
  176.9 28.8 %copy-start.8 = (bf16[1024,1024]{1,0:T(8,128)(2,1)}, bf16[1024,1024]{1,0:T(8,128)(2,1)S(1)}, u32[]{:S(2)}) copy-start(bf16[1024,1024]{1,0:T(8,128)(2,1)S(1)} %multiply_convert_fusion.3.refs_1_) | copy-start | bytes 6291460
  237.6 26.7 %copy-start.6 = (bf16[1024,1024]{1,0:T(8,128)(2,1)S(1)}, bf16[1024,1024]{1,0:T(8,128)(2,1)}, u32[]{:S(2)}) copy-start(bf16[1024,1024]{1,0:T(8,128)(2,1)} %refs_0_.3) | copy-start | bytes 6291460
  264.3 4.4 copy-start.1
  268.6 8.9 %copy-start.4 = (bf16[1024,1024]{1,0:T(8,128)(2,1)}, bf16[1024,1024]{1,0:T(8,128)(2,1)S(1)}, u32[]{:S(2)}) copy-start(bf16[1024,1024]{1,0:T(8,128)(2,1)S(1)} %get-tuple-element.37.refs_3_) | copy-start | bytes 6291460
  268.6 12.0 %slice-start = ((s8[12582912]{0:T(1024)(128)(4,1)}), s8[4194304]{0:T(1024)(128)(4,1)S(1)}, s32[]{:S(2)}) async-start(s8[12582912]{0:T(1024)(128)(4,1)} %bitcast.128), calls=%async_computation | async-start | bytes 8388608
  268.6 12.0 %slice-start.1 = ((s8[12582912]{0:T(1024)(128)(4,1)}), s8[4194304]{0:T(1024)(128)(4,1)S(1)}, s32[]{:S(2)}) async-start(s8[12582912]{0:T(1024)(128)(4,1)} %bitcast.128), calls=%async_computation.1 | async-start | bytes 8388608
  277.5 3.1 slice-start.2
  285.7 1.6 copy-start.9
  285.7 2.4 copy-start.10
  285.7 2.4 copy-start.19
  285.7 2.4 copy-start.21
  286.8 13.4 %copy-start.11 = (bf16[1,1024,1024]{2,1,0:T(8,128)(2,1)}, bf16[1,1024,1024]{2,1,0:T(8,128)(2,1)S(1)}, u32[]{:S(2)}) copy-start(bf16[1,1024,1024]{2,1,0:T(8,128)(2,1)S(1)} %multiply_convert_fusion.1) | copy-start | bytes 6291460
  506.1 8.3 %copy-start.3 = (bf16[1,1024,4608]{2,1,0:T(8,128)(2,1)S(1)}, bf16[1,1024,4608]{2,1,0:T(8,128)(2,1)}, u32[]{:S(2)}) copy-start(bf16[1,1024,4608]{2,1,0:T(8,128)(2,1)} %multiply_convert_fusion.refs_4_) | copy-start | bytes 28311556
  514.4 14.3 %copy-start.16 = (f32[3,64,512]{2,1,0:T(8,128)S(1)}, f32[3,64,512]{2,1,0:T(8,128)}, u32[]{:S(2)}) copy-start(f32[3,64,512]{2,1,0:T(8,128)} %get-tuple-element.69) | copy-start | bytes 1179652
  514.4 15.0 %copy-start.17 = (f32[1,64,512]{2,1,0:T(8,128)S(1)}, f32[1,64,512]{2,1,0:T(8,128)}, u32[]{:S(2)}) copy-start(f32[1,64,512]{2,1,0:T(8,128)} %get-tuple-element.24) | copy-start | bytes 393220
  514.4 15.7 %copy-start.14 = (f32[2,64,2304]{2,1,0:T(8,128)S(1)}, f32[2,64,2304]{2,1,0:T(8,128)}, u32[]{:S(2)}) copy-start(f32[2,64,2304]{2,1,0:T(8,128)} %get-tuple-element.73) | copy-start | bytes 3538948
  514.4 16.7 %copy-start.15 = (f32[1,64,2304]{2,1,0:T(8,128)S(1)}, f32[1,64,2304]{2,1,0:T(8,128)}, u32[]{:S(2)}) copy-start(f32[1,64,2304]{2,1,0:T(8,128)} %get-tuple-element.26) | copy-start | bytes 1769476

commit v5 on v4

--- a/solution.py
+++ b/solution.py
@@ -38,6 +38,7 @@
 GROUPS = ((0, 0, 3), (1, 0, 1), (2, 0, 1), (2, 1, 1), (3, 0, 1))
 SUM_GROUPS = ((0, 0, 1), (1, 0, 1), (1, 1, 1), (2, 0, 3), (3, 0, 1))
 PRODUCTS = ((0, 0, 0, 0), (1, 1, 1, 0), (1, 2, 1, 1), (2, 3, 2, 0), (3, 4, 3, 0))
+STARTS = (0, 1, 3, 5, 7)
 STAGES = {"x": 0, "y": 1, "z": 2, "c": 3}
 
 
@@ -176,69 +177,6 @@
 
 def parts_of(rows):
     return 4 if rows >= 64 else 1
-
-
-def gather_kernel(slabs, layout, lag, *refs):
-    count = len(layout["shapes"])
-    shards, fulls = refs[:count], refs[count : 2 * count]
-    send_sem, recv_sem, own_sem = refs[2 * count :]
-    place = Place(slabs)
-    local = []
-    for i, (shard, full) in enumerate(zip(shards, fulls)):
-        n = shard.shape[2]
-        columns = pl.ds(pl.multiple_of(place.x * n, 128), n)
-        own = pltpu.make_async_copy(
-            shard, full.at[:, place.a, place.y, place.c, :, columns], own_sem.at[i]
-        )
-        own.start()
-        local.append(own)
-    place.greet()
-    for own in local:
-        own.wait()
-    schedules, drains = [], []
-    base = 0
-    for i, plane0, planes in layout["groups"]:
-        rows, n = shards[i].shape[1:]
-        parts = parts_of(rows)
-        size = rows // parts
-        both = []
-        for p in range(parts):
-            ticks, drain = gather_ticks(
-                place, fulls[i], pl.ds(plane0, planes), pl.ds(p * size, size), n,
-                ORDERS[p], send_sem, recv_sem, base,
-            )
-            base += 1
-            both.append(ticks)
-            drains.append(drain)
-        length = max(len(t) for t in both)
-        schedules.append([sum((t[k] for t in both if k < len(t)), []) for k in range(length)])
-    merge(schedules, lag)
-    for drain in drains:
-        drain()
-
-
-def gather_all(shards, groups, dp, tensor, lag=2):
-    slabs = dp // 4
-    shapes = [s.shape for s in shards]
-    parts = parts_of(shapes[0][1])
-    bases = len(groups) * parts
-    out = [
-        jax.ShapeDtypeStruct((s[0], slabs, 2, 2, s[1], s[2] * tensor), jnp.bfloat16) for s in shapes
-    ]
-    full = pl.pallas_call(
-        functools.partial(gather_kernel, slabs, {"shapes": shapes, "groups": groups}, lag),
-        out_shape=out,
-        in_specs=[pl.BlockSpec(memory_space=pltpu.VMEM)] * len(shards),
-        out_specs=[pl.BlockSpec(memory_space=pl.ANY)] * len(shards),
-        scratch_shapes=[
-            pltpu.SemaphoreType.DMA((bases, 4, slabs)),
-            pltpu.SemaphoreType.DMA((bases, 4, slabs)),
-            pltpu.SemaphoreType.DMA((len(shards),)),
-        ],
-        compiler_params=pltpu.CompilerParams(collective_id=0, has_side_effects=True),
-        name="gather_weights",
-    )(*shards)
-    return [f.reshape(s[0], dp * s[1], s[2] * tensor) for f, s in zip(full, shapes)]
 
 
 def add_into(target, extra):
@@ -772,6 +710,306 @@
     )(*lefts, *rights, small)
 
 
+BLOCK = 256
+
+
+class Forward:
+    def __init__(self, refs, fulls):
+        (self.tokens, self.gain_mix, self.taps, self.gain_ff, outs, scratch) = refs
+        self.in_full, self.out_full, self.gate_up_full = fulls[:3]
+        (self.normed_o, self.proj_o, self.gated_o, self.residual_o, self.ff_o, self.gate_o,
+         self.up_o, self.hidden_o) = outs
+        (self.normed, self.proj, self.mixed, self.proj_low, self.gated, self.residual, self.ff,
+         self.gate, self.weight, self.first, self.second, self.load_sem, self.save_sem,
+         self.first_sem, self.second_sem) = scratch
+        self.rows, self.width = self.tokens.shape
+        self.blocks = self.rows // BLOCK
+        self.late = []
+
+    def rows_of(self, k):
+        return pl.ds(pl.multiple_of(k * BLOCK, BLOCK), BLOCK)
+
+    def wide(self, tile):
+        return pl.ds(pl.multiple_of(tile * TILE, TILE), TILE)
+
+    def save(self, k, ref, out):
+        copy = pltpu.make_async_copy(ref, out, self.save_sem.at[k])
+        copy.start()
+        self.late.append(copy)
+
+    def weight_copy(self, full, plane, tile, slot):
+        wide = full.shape[-1]
+        matrix = full.at[plane].reshape(self.width, wide)
+        return pltpu.make_async_copy(
+            matrix.at[:, self.wide(tile)], self.weight.at[slot], self.load_sem.at[slot]
+        )
+
+    def norm_rows(self, source, gain, target):
+        def body(k, carry):
+            at = self.rows_of(k)
+            values = source[at, :].astype(jnp.float32)
+            scale = lax.rsqrt(jnp.mean(values * values, axis=-1, keepdims=True) + EPS)
+            target[at, :] = (values * scale * gain[...]).astype(jnp.bfloat16)
+            return carry
+
+        lax.fori_loop(0, self.blocks, body, 0)
+
+    def begin(self):
+        self.norm_rows(self.tokens, self.gain_mix, self.normed)
+        self.save(0, self.normed, self.normed_o)
+
+    def channels(self, tile):
+        for j in range(3):
+            self.weight_copy(self.in_full, j, tile, j).start()
+        if tile:
+            self.late.pop().wait()
+        for j in range(3):
+            self.weight_copy(self.in_full, j, tile, j).wait()
+
+            def project(k, carry, j=j):
+                at = self.rows_of(k)
+                product = jnp.dot(
+                    self.normed[at, :], self.weight[j], preferred_element_type=jnp.float32
+                )
+                self.proj[j, at, :] = product
+                self.proj_low[j, at, :] = product.astype(jnp.bfloat16)
+                return carry
+
+            lax.fori_loop(0, self.blocks, project, 0)
+        cols = slice(tile * TILE, (tile + 1) * TILE)
+        pad = 8
+        for s in range(self.rows // LEN):
+            self.mixed[:pad, :] = jnp.zeros((pad, TILE), jnp.float32)
+            for k in range(LEN // BLOCK):
+                at = slice(s * LEN + k * BLOCK, s * LEN + (k + 1) * BLOCK)
+                self.mixed[pad + k * BLOCK : pad + (k + 1) * BLOCK, :] = (
+                    self.proj[0, at, :] * self.proj[2, at, :]
+                )
+            for k in range(LEN // BLOCK):
+                at = slice(s * LEN + k * BLOCK, s * LEN + (k + 1) * BLOCK)
+                base = pad + k * BLOCK
+                conv = (
+                    self.taps[0:1, cols] * self.mixed[base - 2 : base - 2 + BLOCK, :]
+                    + self.taps[1:2, cols] * self.mixed[base - 1 : base - 1 + BLOCK, :]
+                    + self.taps[2:3, cols] * self.mixed[base : base + BLOCK, :]
+                )
+                self.gated[at, cols] = (self.proj[1, at, :] * conv).astype(jnp.bfloat16)
+        self.save(1, self.proj_low, self.proj_o.at[:, :, cols])
+
+    def mixer(self):
+        tiles = self.width // TILE
+        for c in range(tiles):
+            self.weight_copy(self.out_full, 0, c, c).start()
+        for c in range(tiles):
+            self.weight_copy(self.out_full, 0, c, c).wait()
+
+        def body(k, carry):
+            at = self.rows_of(k)
+            total = self.tokens[at, :].astype(jnp.float32)
+            for c in range(tiles):
+                total = total + lax.dot_general(
+                    self.gated[at, c * TILE : (c + 1) * TILE], self.weight[c],
+                    (((1,), (1,)), ((), ())), preferred_element_type=jnp.float32,
+                )
+            self.residual[at, :] = total
+            return carry
+
+        lax.fori_loop(0, self.blocks, body, 0)
+        self.norm_rows(self.residual, self.gain_ff, self.ff)
+        self.save(2, self.gated, self.gated_o)
+        self.save(3, self.residual, self.residual_o)
+        self.save(4, self.ff, self.ff_o)
+
+    def hidden_tiles(self, plane, first, count):
+        total = self.gate_o.shape[1] // TILE
+        ahead = min(3, count)
+        for k in range(ahead):
+            self.weight_copy(self.gate_up_full, plane, first + k, k).start()
+
+        def out_copies(t):
+            slot = t % 2
+            at = self.wide(t)
+            if plane == 0:
+                return [
+                    pltpu.make_async_copy(
+                        self.first.at[slot], self.gate_o.at[:, at], self.first_sem.at[slot]
+                    )
+                ]
+            return [
+                pltpu.make_async_copy(
+                    self.first.at[slot], self.up_o.at[:, at], self.first_sem.at[slot]
+                ),
+                pltpu.make_async_copy(
+                    self.second.at[slot], self.hidden_o.at[:, at], self.second_sem.at[slot]
+                ),
+            ]
+
+        def tile_step(i, carry):
+            t = first + i
+            slot = t % 2
+
+            @pl.when(i >= 2)
+            def _():
+                for copy in out_copies(t - 2):
+                    copy.wait()
+
+            self.weight_copy(self.gate_up_full, plane, t, i % 4).wait()
+
+            @pl.when(i + ahead < count)
+            def _():
+                self.weight_copy(
+                    self.gate_up_full, plane, t + ahead, (i + ahead) % 4
+                ).start()
+
+            def rows_step(k, inner):
+                at = self.rows_of(k)
+                product = jnp.dot(
+                    self.ff[at, :], self.weight[i % 4], preferred_element_type=jnp.float32
+                )
+                self.first[slot, at, :] = product.astype(jnp.bfloat16)
+                if plane == 0:
+                    self.gate[at, self.wide(t)] = product
+                else:
+                    gate = self.gate[at, self.wide(t)]
+                    hidden = gate * jax.nn.sigmoid(gate) * product
+                    self.second[slot, at, :] = hidden.astype(jnp.bfloat16)
+                return inner
+
+            lax.fori_loop(0, self.blocks, rows_step, 0)
+            for copy in out_copies(t):
+                copy.start()
+            return carry
+
+        lax.fori_loop(0, count, tile_step, 0)
+        for t in range(max(first, first + count - 2), first + count):
+            for copy in out_copies(t):
+                copy.wait()
+
+    def pieces(self, ends):
+        tiles = self.gate_o.shape[1] // TILE
+        some = 3
+        plan = [(0, self.begin)]
+        plan += [(ends[0] + c, functools.partial(self.channels, c)) for c in range(self.width // TILE)]
+        plan.append((max(ends[1], ends[0] + 2), self.mixer))
+        for plane in range(2):
+            for k, at in enumerate(range(0, tiles, some)):
+                plan.append(
+                    (ends[2 + plane] + k,
+                     functools.partial(self.hidden_tiles, plane, at, min(some, tiles - at)))
+                )
+        return plan
+
+    def close(self):
+        for copy in self.late:
+            copy.wait()
+
+
+def forward_kernel(slabs, groups, starts, count, *refs):
+    shards, refs = refs[:count], refs[count:]
+    (tokens, gain_mix, taps, gain_ff), refs = refs[:4], refs[4:]
+    fulls, refs = refs[:count], refs[count:]
+    outs, refs = refs[:8], refs[8:]
+    send_sem, recv_sem, own_sem = refs[:3]
+    place = Place(slabs)
+    local = []
+    for i, (shard, full) in enumerate(zip(shards, fulls)):
+        n = shard.shape[2]
+        columns = pl.ds(pl.multiple_of(place.x * n, 128), n)
+        own = pltpu.make_async_copy(
+            shard, full.at[:, place.a, place.y, place.c, :, columns], own_sem.at[i]
+        )
+        own.start()
+        local.append(own)
+    place.greet()
+    for own in local:
+        own.wait()
+    work = Forward((tokens, gain_mix, taps, gain_ff, outs, refs[3:]), fulls)
+    ticks, drains, ends, base = {}, [], [], 0
+    for g, (i, plane0, planes) in enumerate(groups):
+        rows, n = shards[i].shape[1:]
+        parts = parts_of(rows)
+        size = rows // parts
+        length = 0
+        for p in range(parts):
+            steps, drain = gather_ticks(
+                place, fulls[i], pl.ds(plane0, planes), pl.ds(p * size, size), n,
+                ORDERS[p], send_sem, recv_sem, base,
+            )
+            base += 1
+            drains.append(drain)
+            length = max(length, len(steps))
+            for k, actions in enumerate(steps):
+                ticks.setdefault(starts[g] + k, []).extend(actions)
+        ends.append(starts[g] + length - 1)
+    plan = work.pieces(ends)
+    for t in range(max(ends) + 1):
+        for cond, action in ticks[t]:
+            when(cond, action)
+        if plan and plan[0][0] <= t:
+            plan.pop(0)[1]()
+    for _, action in plan:
+        action()
+    for drain in drains:
+        drain()
+    work.close()
+
+
+def gather_forward(shards, tokens, gain_mix, taps, gain_ff, groups, starts, dp, tensor):
+    slabs = dp // 4
+    shapes = [s.shape for s in shards]
+    bases = len(groups) * parts_of(shapes[0][1])
+    rows, width = tokens.shape
+    units = shapes[2][2] * tensor
+    bf, f32 = jnp.bfloat16, jnp.float32
+    fulls = [
+        jax.ShapeDtypeStruct((s[0], slabs, 2, 2, s[1], s[2] * tensor), bf) for s in shapes
+    ]
+    kept = [
+        jax.ShapeDtypeStruct(shape, kind)
+        for shape, kind in (
+            ((rows, width), bf), ((3, rows, width), bf), ((rows, width), bf),
+            ((rows, width), f32), ((rows, width), bf), ((rows, units), bf),
+            ((rows, units), bf), ((rows, units), bf),
+        )
+    ]
+    dma = pltpu.SemaphoreType.DMA
+    vmem = pl.BlockSpec(memory_space=pltpu.VMEM)
+    anywhere = pl.BlockSpec(memory_space=pl.ANY)
+    out = pl.pallas_call(
+        functools.partial(forward_kernel, slabs, groups, starts, len(shards)),
+        out_shape=fulls + kept,
+        in_specs=[vmem] * (len(shards) + 4),
+        out_specs=[anywhere] * (len(fulls) + len(kept)),
+        scratch_shapes=[
+            dma((bases, 4, slabs)),
+            dma((bases, 4, slabs)),
+            dma((len(shards),)),
+            pltpu.VMEM((rows, width), bf),
+            pltpu.VMEM((3, rows, TILE), f32),
+            pltpu.VMEM((8 + LEN, TILE), f32),
+            pltpu.VMEM((3, rows, TILE), bf),
+            pltpu.VMEM((rows, width), bf),
+            pltpu.VMEM((rows, width), f32),
+            pltpu.VMEM((rows, width), bf),
+            pltpu.VMEM((rows, units), f32),
+            pltpu.VMEM((4, width, TILE), bf),
+            pltpu.VMEM((2, rows, TILE), bf),
+            pltpu.VMEM((2, rows, TILE), bf),
+            dma((4,)),
+            dma((5,)),
+            dma((2,)),
+            dma((2,)),
+        ],
+        compiler_params=pltpu.CompilerParams(
+            collective_id=0, has_side_effects=True, vmem_limit_bytes=67043328
+        ),
+        name="gather_forward",
+    )(*shards, tokens, gain_mix[None], taps, gain_ff[None])
+    count = len(shards)
+    weights = [f.reshape(s[0], dp * s[1], s[2] * tensor) for f, s in zip(out[:count], shapes)]
+    return weights, out[count:]
+
+
 def per_device(
     tokens,
     gain_mix,
@@ -785,15 +1023,24 @@
 ):
     inputs = tokens.astype(jnp.float32)
     dp, tensor = lax.axis_size("dp"), lax.axis_size("tensor")
-    in_full, out_full, gate_up_full, down_full = gather_all(
-        [in_weight, out_weight[None], gate_up_weight, down_weight[None]], GROUPS, dp, tensor
+    weights, kept = gather_forward(
+        [in_weight, out_weight[None], gate_up_weight, down_weight[None]],
+        tokens,
+        gain_mix,
+        conv_weight,
+        gain_ff,
+        GROUPS,
+        STARTS,
+        dp,
+        tensor,
     )
+    in_full, out_full, gate_up_full, down_full = weights
+    normed_mix, projected, gated_rows, residual, normed_ff, gate_low, up_low, hidden = kept
+    projected = projected.astype(jnp.float32)
     out_full, down_full = out_full[0], down_full[0]
     rows, width = tokens.shape
     seq_count = rows // LEN
     scale_mix = norm_scale(inputs)
-    normed_mix = (inputs * scale_mix * gain_mix).astype(jnp.bfloat16)
-    projected = jnp.einsum("gd,jdc->jgc", normed_mix, in_full, preferred_element_type=jnp.float32)
     shaped = (seq_count, LEN, width)
     input_gate = projected[0].reshape(shaped)
     output_gate = projected[1].reshape(shaped)
@@ -804,20 +1051,11 @@
         + conv_weight[1] * delayed(mixed_in, 1)
         + conv_weight[2] * mixed_in
     )
-    gated_rows = (output_gate * conv_out).astype(jnp.bfloat16).reshape(rows, width)
-    residual = inputs + lax.dot_general(
-        gated_rows, out_full, (((1,), (1,)), ((), ())), preferred_element_type=jnp.float32
-    )
     scale_ff = norm_scale(residual)
-    normed_ff = (residual * scale_ff * gain_ff).astype(jnp.bfloat16)
-    gate_up = jnp.einsum(
-        "gd,jdf->jgf", normed_ff, gate_up_full, preferred_element_type=jnp.float32
-    )
-    gate_pre = gate_up[0]
-    up_value = gate_up[1]
+    gate_pre = gate_low.astype(jnp.float32)
+    up_value = up_low.astype(jnp.float32)
     sigmoid_gate = jax.nn.sigmoid(gate_pre)
     silu_gate = gate_pre * sigmoid_gate
-    hidden = (silu_gate * up_value).astype(jnp.bfloat16)
     block_out = (
         residual
         + lax.dot_general(

time: 540 us -> 500 us (0.926)
  matrix products: 136 us -> 85.6 us
  Pallas kernels: 323 us -> 364 us
  other arithmetic: 53.3 us -> 30.2 us
  local copies, waits for them, and re-layouts: 18.7 us -> 9.54 us
    dot_general x3 -> x0, matrix products: 42.1 us -> none  [the longest x1 28.8 us: per_device(): jnp.einsum('gd,jdf->jgf', normed_ff, gate_up_full, preferred_element_type...]
    pallas_call x1, Pallas kernels: 145 us -> 179 us  [gather_forward(): pl.pallas_call(functools.partial(forward_kernel, slabs, groups, starts, l...]
    convert_element_type x4 -> x1, other arithmetic: 25.4 us -> 5.07 us  [per_device(): projected = projected.astype(jnp.float32)]
    unnamed x56 -> x34, local copies, waits for them, and re-layouts: 12.1 us -> 5.1 us
    pallas_call x1, Pallas kernels: 178 us -> 184 us  [tile_sum_all(): pl.pallas_call(functools.partial(tile_sum_kernel, slabs, tensor, groups,...]
    dot_general x1, matrix products: 31.9 us -> 25.9 us  [per_device(): jnp.dot(grad_out, down_full, preferred_element_type=jnp.float32)]
where the time goes in v5:
time: 500 us; the launch traced here: 490 us
  Pallas kernels  364 us (73%)
  matrix products  85.6 us (17%)
  other arithmetic  30.2 us (6%)
  local copies, waits for them, and re-layouts  9.54 us (2%)
    pallas_call x1, Pallas kernels, tile_sum_all(): pl.pallas_call(functools.partial(tile_sum_kernel, slabs, tensor, groups,...  184 us
    pallas_call x1, Pallas kernels, gather_forward(): pl.pallas_call(functools.partial(forward_kernel, slabs, groups, starts, l...  179 us
    dot_general x1, matrix products, per_device(): jnp.dot(grad_out, down_full, preferred_element_type=jnp.float32)  25.9 us
    dot_general x1, matrix products, per_device(): jnp.einsum('jgf,jdf->gd', gate_up_grad, gate_up_full, preferred_element_t...  25.1 us
    dot_general x1, matrix products, per_device(): lax.dot_general(hidden, down_full, (((1,), (1,)), ((), ())), preferred_el...  16.1 us
    dot_general x1, matrix products, per_device(): jnp.einsum('jgc,jdc->gd', proj_grad, in_full, preferred_element_type=jnp....  13 us

profile of v5, /device:TPU:0, one launch (start us, length us, event | category | flops | bytes accessed | tf_op | source)
XLA Modules:
  0.0 490.2 jit_solution(12380413571015731308)
XLA Ops:
  0.6 179.2 %gather_forward.1 = (bf16[3,4,2,2,64,1024]{5,4,3,2,1,0:T(8,128)(2,1)}, bf16[1,4,2,2,64,1024]{5,4,3,2,1,0:T(8,128)(2,1)}, bf16[2,4,2,2,64,4608]{5,4,3,2,1,0:T(8,1...) custom-call(bf16[3,64,512]{2,1,0:T(8,128)(2,1)} %refs_0_.2, ...), custom_call_target="tpu_custom_call" | custom-call | tf_op jit(solution)/shard_map/gather_forward/pallas_call | solution.py:978
  179.9 25.9 %fusion.14 = (bf16[1,1024,4608]{2,1,0:T(8,128)(2,1)}, bf16[1,1024,4608]{2,1,0:T(8,128)(2,1)}) fusion(bf16[1024,4608]{1,0:T(8,128)(2,1)} %get-tuple-element.30, bf16[1024,4608]{1,0:T(8,128)(2,1)} %get-tuple-element.29, bf16[1024,1024]{1,0:T(8,128)(2,1)} %refs_0_.3, bf16[1024,4608]{1,0:T(8,128)(2,1)} %bitcast.95), kind=kOutput, calls=%fused_computation.18 | convolution fusion | flops 9734455296 | bytes 49283072 | tf_op jit(solution)/shard_map/dot_general | solution.py:1065
  205.7 0.0 copy-start.2
  205.7 0.0 copy-start.12
  205.8 2.7 multiply_reduce_fusion.4
  208.5 0.7 copy-done.2
  209.2 0.0 copy-done.12
  209.2 0.0 copy-start.4
  209.2 25.1 %fusion.24 = (f32[1024]{0:T(1024)S(1)}, f32[1024]{0:T(1024)S(1)}, f32[1024,1024,1]{1,0,2:T(8,128)S(1)}) fusion(f32[1024,1024]{1,0:T(8,128)S(1)} %copy-done.2, f32[1024]{0:T(1024)S(1)} %get-tuple-element.66, f32[1024]{0:T(1024)S(1)} %copy-done.12, bf16[2,1024,4608]{2,1,0:T(8,128)(2,1)} %bitcast.94, bf16[1,1024,4608]{2,1,0:T(8,128)(2,1)} %get-tuple-element.56.refs_6_, ...), kind=kOutput, calls=%fused_computation.38 | convolution fusion | flops 19343081472 | bytes 46153728 | tf_op jit(solution)/shard_map/jgf,jdf->gd/dot_general | solution.py:1070
  234.3 0.0 copy-done.4
  234.3 2.7 fusion.27
  237.0 0.0 copy-start.1
  237.0 5.1 %convert_element_type.49 = f32[3,1024,1024]{2,1,0:T(8,128)S(1)} convert(bf16[3,1024,1024]{2,1,0:T(8,128)(2,1)} %get-tuple-element.33) | non-fusion elementwise | flops 3145728 | bytes 18874368 | tf_op jit(solution)/shard_map/convert_element_type | solution.py:1039
  242.1 0.0 copy-start.11
  242.1 0.0 copy-start.6
  242.1 1.0 slice_multiply_fusion.1
  243.1 0.0 copy-done.11
  243.1 0.0 copy-done.1
  243.1 0.6 copy-done.6
  243.7 5.5 %multiply_reduce_fusion = (f32[1024]{0:T(1024)S(1)}, f32[1024]{0:T(1024)S(1)}, f32[1024]{0:T(1024)S(1)}, f32[1,1024,1024]{2,1,0:T(8,128)S(1)}, bf16[1,1024,1024]{2,1,0:T(8,128)(2,1)}) fusion(f32[1,1024,1024]{2,1,0:T(8,128)S(1)} %slice_multiply_fusion.1, f32[1,1023,1024]{2,1,0:T(8,128)S(1)} %bitcast.70, f32[1,1022,1024]{2,1,0:T(8,128)S(1)} %bitcast.71, ...), kind=kOutput, calls=%fused_computation.39 | convolution fusion | flops 2162160640 | bytes 27275264 | tf_op jit(solution)/shard_map/dot_general | solution.py:1076
  249.2 0.5 slice.58
  249.7 0.5 slice.59
  250.2 3.3 multiply_convert_fusion.1
  253.4 0.0 copy-start
  253.4 0.0 copy-start.5
  253.4 0.0 copy-start.13
  253.4 2.0 multiply_convert_fusion
  255.5 0.0 copy-done
  255.5 0.5 fusion.15
  255.9 0.6 multiply_multiply_fusion
  256.6 0.0 copy-start.14
  256.6 0.0 copy-done.5
  256.6 0.0 copy-done.13
  256.6 13.0 %fusion.21 = (f32[1024]{0:T(1024)S(1)}, f32[1024]{0:T(1024)}, f32[1024,1024,1]{1,0,2:T(8,128)}) fusion(bf16[1024,1024]{1,0:T(8,128)(2,1)S(1)} %copy-done, f32[1024]{0:T(1024)S(1)} %get-tuple-element.64, f32[1024]{0:T(1024)S(1)} %copy-done.13, bf16[3,1024,1024]{2,1,0:T(8,128)(2,1)} %bitcast.97, bf16[1,1024,1024]{2,1,0:T(8,128)(2,1)} %multiply_convert_fusion, ...), kind=kOutput, calls=%fused_computation.30 | convolution fusion | flops 6456080384 | bytes 18890752 | tf_op jit(solution)/shard_map/jgc,jdc->gd/dot_general | solution.py:1096
  269.6 0.0 copy-done.14
  269.6 0.7 concatenate.7.refs_9_
  270.3 5.5 %pad_maximum_fusion.refs_7_ = bf16[3,1024,1024]{2,1,0:T(8,128)(2,1)} fusion(bf16[1,1024,1024]{2,1,0:T(8,128)(2,1)} %multiply_convert_fusion, bf16[1,1024,1024]{2,1,0:T(8,128)(2,1)} %get-tuple-element.57, bf16[1,1024,1024]{2,1,0:T(8,128)(2,1)S(1)} %copy-done.5), kind=kLoop, calls=%fused_computation.23 | loop fusion | flops 6291456 | bytes 12582912 | tf_op jit(solution)/shard_map/stack | solution.py:1092
  275.8 184.5 %sum_products.1 = (f32[1,64,2304]{2,1,0:T(8,128)}, f32[2,64,2304]{2,1,0:T(8,128)}, f32[3,64,512]{2,1,0:T(8,128)}, f32[1,64,512]{2,1,0:T(8,128)}, f32[8,1024]{1,0:T(8,128)}) custom-call(bf16[1024,1024]{1,0:T(8,128)(2,1)} %refs_0_.3, bf16[1024,1024]{1,0:T(8,128)(2,1)} %get-tuple-element.35.refs_1_, bf16[1024,1024]{1,0:T(8,128)(2,1)} %get-tuple-element.36.refs_2_, ...), custom_call_target="tpu_custom_call" | custom-call | tf_op jit(solution)/shard_map/sum_products/pallas_call | solution.py:684
  460.2 1.4 slice.55
  461.6 1.4 fusion.28
  463.0 0.7 broadcast_multiply_fusion
  463.7 0.0 copy-start.3
  463.7 6.2 %fusion.18 = f32[1024,1024]{1,0:T(8,128)} fusion(f32[1024,1024]{1,0:T(8,128)} %get-tuple-element.54, bf16[1024,1024]{1,0:T(8,128)(2,1)} %refs_4_.1, f32[1024,1024,1]{1,0,2:T(8,128)} %get-tuple-element.68, f32[1024]{0:T(1024)S(1)} %broadcast_multiply_fusion, f32[1024]{0:T(1024)} %get-tuple-element.63, f32[1024]{0:T(1024)} %param.10, f32[1024]{0:T(1024)} %copy-done.14), kind=kLoop, calls=%fused_computation.27 | loop fusion | flops 7340032 | bytes 14696448 | tf_op jit(solution)/shard_map/add | solution.py:1100
  469.9 0.5 copy-done.3
  470.4 0.0 copy-start.9
  470.4 0.0 copy-start.10
  470.4 0.0 copy-start.7
  470.4 0.0 copy-start.8
  470.4 16.1 %add_convert_fusion = bf16[1024,1024]{1,0:T(8,128)(2,1)} fusion(f32[1024,1024]{1,0:T(8,128)S(1)} %copy-done.3, bf16[1024,4608]{1,0:T(8,128)(2,1)} %get-tuple-element.27, bf16[1024,4608]{1,0:T(8,128)(2,1)} %bitcast.96), kind=kOutput, calls=%fused_computation.48 | convolution fusion | flops 9665773568 | bytes 25165824 | tf_op jit(solution)/shard_map/dot_general | solution.py:1061
  486.6 0.0 copy-done.9
  486.6 0.7 copy.24
  487.3 0.0 copy-done.10
  487.3 0.7 copy.25
  488.0 0.0 copy-done.7
  488.0 1.0 copy.26
  489.0 0.0 copy-done.8
  489.0 0.8 copy.27
  (4 shorter events, 0.0 us)
Async XLA Ops:
  205.7 3.4 copy-start.2
  205.7 3.5 copy-start.12
  209.2 25.1 %copy-start.4 = (bf16[1024,1024]{1,0:T(8,128)(2,1)S(1)}, bf16[1024,1024]{1,0:T(8,128)(2,1)}, u32[]{:S(2)}) copy-start(bf16[1024,1024]{1,0:T(8,128)(2,1)} %refs_0_.3) | copy-start | bytes 6291460
  237.0 6.1 %copy-start.1 = (bf16[1024,1024]{1,0:T(8,128)(2,1)}, bf16[1024,1024]{1,0:T(8,128)(2,1)S(1)}, u32[]{:S(2)}) copy-start(bf16[1024,1024]{1,0:T(8,128)(2,1)S(1)} %get-tuple-element.53.refs_3_) | copy-start | bytes 6291460
  242.1 1.0 copy-start.11
  242.1 1.6 copy-start.6
  253.4 2.0 copy-start
  253.4 3.1 copy-start.5
  253.4 3.1 copy-start.13
  256.6 13.1 %copy-start.14 = (f32[1024]{0:T(1024)}, f32[1024]{0:T(1024)S(1)}, u32[]{:S(2)}) copy-start(f32[1024]{0:T(1024)S(1)} %get-tuple-element.64) | copy-start | bytes 12292
  463.7 6.7 %copy-start.3 = (f32[1024,1024]{1,0:T(8,128)S(1)}, f32[1024,1024]{1,0:T(8,128)}, u32[]{:S(2)}) copy-start(f32[1024,1024]{1,0:T(8,128)} %get-tuple-element.26) | copy-start | bytes 12582916
  470.4 16.2 %copy-start.9 = (f32[3,64,512]{2,1,0:T(8,128)S(1)}, f32[3,64,512]{2,1,0:T(8,128)}, u32[]{:S(2)}) copy-start(f32[3,64,512]{2,1,0:T(8,128)} %get-tuple-element.81) | copy-start | bytes 1179652
  470.4 16.9 %copy-start.10 = (f32[1,64,512]{2,1,0:T(8,128)S(1)}, f32[1,64,512]{2,1,0:T(8,128)}, u32[]{:S(2)}) copy-start(f32[1,64,512]{2,1,0:T(8,128)} %get-tuple-element.40) | copy-start | bytes 393220
  470.4 17.6 %copy-start.7 = (f32[2,64,2304]{2,1,0:T(8,128)S(1)}, f32[2,64,2304]{2,1,0:T(8,128)}, u32[]{:S(2)}) copy-start(f32[2,64,2304]{2,1,0:T(8,128)} %get-tuple-element.85) | copy-start | bytes 3538948
  470.4 18.6 %copy-start.8 = (f32[1,64,2304]{2,1,0:T(8,128)S(1)}, f32[1,64,2304]{2,1,0:T(8,128)}, u32[]{:S(2)}) copy-start(f32[1,64,2304]{2,1,0:T(8,128)} %get-tuple-element.42) | copy-start | bytes 1769476
